TPU v7x, 256 devices: a whole 4x4x8 slice. The times are simulated.
256 devices in a mesh: dp: 8 (over x, core), expert: 32 (over y, z).
Axes of the slice: x: 4, y: 4, z: 8, core: 2. Of those that a mesh axis runs over, the one named last changes fastest.
Arguments:
- tokens: bfloat16 [8192, 3584], P(('dp', 'expert')), may hold values from -6 to 6
- expert_ids: int32 [8192, 2], P(('dp', 'expert')), may hold values from 0 to 31, all different within a row; in each aligned block of 32 rows (0 to 31, 32 to 63, ...) at most 3 rows name the same one
- mix_weights: float32 [8192, 2], P(('dp', 'expert')), may hold values from 0.25 to 1
- w_up: bfloat16 [32, 3584, 3072], P('expert', None, 'dp'), may hold values from -0.09375 to 0.09375
- w_down: bfloat16 [32, 3072, 3584], P('expert', 'dp'), may hold values from -0.109375 to 0.109375
- out_grad: bfloat16 [8192, 3584], P(('dp', 'expert')), may hold values from -3 to 3
Outputs:
- layer_out: bfloat16 [8192, 3584], P(('dp', 'expert'))
- token_grad: bfloat16 [8192, 3584], P(('dp', 'expert'))
- up_grad: bfloat16 [32, 3584, 3072], P('expert', None, 'dp')
- down_grad: bfloat16 [32, 3072, 3584], P('expert', 'dp')
Inputs may be any that keep to these rules, and one draw needn't show every extreme that they name: `expert_ids`: the two experts of a token differ. The 32 tokens of one device name one expert at most 3 times, and in every draw some device names some expert exactly 3 times.
All inputs are finite; a program needn't handle non-finite values.
Results may differ from a plain program's by a relative error of at most 0.015.
Values may be sent and summed in bfloat16 or wider, within the bound.
No kernel may reach another device: no remote copies, remote signals or barrier semaphores. Data moves between devices by JAX's collectives and lax.ppermute only.
A program may use at most 128 MiB of HBM per device.

v0:
```python
import functools

import jax
import jax.numpy as jnp
from jax import lax
from jax.experimental import pallas as pl
from jax.experimental.pallas import tpu as pltpu
from jax.sharding import PartitionSpec as P


BF16, F32, I32 = jnp.bfloat16, jnp.float32, jnp.int32
STEPS = 2
CAP = 3
GROUP = 8


def dot(a, b, dims=((1,), (0,))):
    return lax.dot_general(a, b, (dims, ((), ())), preferred_element_type=F32)


def full(shape):
    return pl.BlockSpec(shape, lambda k: (0, 0))


def cost(flops, bytes_accessed):
    return pl.CostEstimate(flops=flops, transcendentals=0, bytes_accessed=bytes_accessed)


def gather_body(back, *refs):
    pieces, (w_own, w_other) = refs[:4], refs[4:6]
    if back:
        pre, (rows_out, first, second), (acc,) = refs[6], refs[7:10], refs[10:]
    else:
        rows_out, pre_out, first, second, acc = refs[6:]
    k = pl.program_id(0)
    size = pieces[0].shape[0]
    for b, piece in enumerate(pieces):
        rows_out[b * size : (b + 1) * size, :] = piece[...]
    if back:
        weight = jnp.concatenate([w_own[...], w_other[...]], axis=0)
        part = dot(rows_out[...], weight, ((1,), (1,)))
    else:
        weight = jnp.concatenate([w_own[...], w_other[...]], axis=1)
        part = dot(rows_out[...], weight)

    @pl.when(k == 0)
    def _():
        acc[...] = part

    @pl.when(k > 0)
    def _():
        acc[...] += part

    @pl.when(k == pl.num_programs(0) - 1)
    def _():
        units = first.shape[1]
        if back:
            pre_act = pre[...]
            squash = jax.nn.sigmoid(pre_act)
            value = (acc[...] * (squash * (1.0 + pre_act * (1.0 - squash)))).astype(BF16)
        else:
            pre_act = acc[...]
            pre_out[...] = pre_act
            value = (pre_act * jax.nn.sigmoid(pre_act)).astype(BF16)
        first[...] = value[:, :units]
        second[...] = value[:, units:]


def rows_matmul(pieces, w_own, w_other, pre, steps):
    back = pre is not None
    size, width = pieces[0].shape
    rows, cols = 4 * size, width // steps
    units = w_own.shape[0] if back else w_own.shape[1]
    piece = pl.BlockSpec((size, cols), lambda k: (0, k))
    weight = pl.BlockSpec((units, cols), lambda k: (0, k)) if back else pl.BlockSpec((cols, units), lambda k: (k, 0))
    wide, narrow = full((rows, 2 * units)), full((rows, units))
    narrow_shape = jax.ShapeDtypeStruct((rows, units), BF16)
    return pl.pallas_call(
        functools.partial(gather_body, back),
        grid=(steps,),
        in_specs=[piece] * 4 + [weight, weight] + [wide] * back,
        out_specs=[pl.BlockSpec((rows, cols), lambda k: (0, k))] + [wide] * (not back) + [narrow, narrow],
        out_shape=[jax.ShapeDtypeStruct((rows, width), BF16)]
        + [jax.ShapeDtypeStruct((rows, 2 * units), F32)] * (not back) + [narrow_shape, narrow_shape],
        scratch_shapes=[pltpu.VMEM((rows, 2 * units), F32)],
        cost_estimate=cost(4 * rows * width * units, 4 * (rows * width + width * units)),
    )(*pieces, w_own, w_other, *([pre] * back))


def project_body(by_rows, h_own, h_other, w_own, w_other, *outs):
    hidden = jnp.concatenate([h_own[...], h_other[...]], axis=1)
    if by_rows:
        weight = jnp.concatenate([w_own[...], w_other[...]], axis=1)
        value = dot(hidden, weight, ((1,), (1,))).astype(BF16)
    else:
        weight = jnp.concatenate([w_own[...], w_other[...]], axis=0)
        value = dot(hidden, weight).astype(BF16)
    size = outs[0].shape[0]
    for b, out in enumerate(outs):
        out[...] = value[b * size : (b + 1) * size, :]


def project(h_own, h_other, w_own, w_other, by_rows, steps):
    rows, units = h_own.shape
    width = w_own.shape[0] if by_rows else w_own.shape[1]
    cols, size = width // steps, rows // 4
    if by_rows:
        weight = pl.BlockSpec((cols, units), lambda k: (k, 0))
    else:
        weight = pl.BlockSpec((units, cols), lambda k: (0, k))
    return pl.pallas_call(
        functools.partial(project_body, by_rows),
        grid=(steps,),
        in_specs=[full((rows, units))] * 2 + [weight, weight],
        out_specs=[pl.BlockSpec((size, cols), lambda k: (0, k))] * 4,
        out_shape=[jax.ShapeDtypeStruct((size, width), BF16)] * 4,
        cost_estimate=cost(4 * rows * width * units, 2 * (rows * width + 2 * width * units)),
    )(h_own, h_other, w_own, w_other)


def down_grad_body(h_a, h_b, g_a, g_b, out):
    hidden = jnp.concatenate([h_a[...], h_b[...]], axis=0)
    rows = jnp.concatenate([g_a[...], g_b[...]], axis=0)
    out[...] = dot(hidden, rows, ((0,), (0,))).astype(BF16)


def down_grad(h_a, h_b, g_a, g_b, steps):
    rows, units = h_a.shape
    width = g_a.shape[1]
    cols = width // steps
    g_spec = pl.BlockSpec((rows, cols), lambda k: (0, k))
    return pl.pallas_call(
        down_grad_body,
        grid=(steps,),
        in_specs=[full((rows, units))] * 2 + [g_spec, g_spec],
        out_specs=pl.BlockSpec((units, cols), lambda k: (0, k)),
        out_shape=jax.ShapeDtypeStruct((units, width), BF16),
        cost_estimate=cost(4 * rows * width * units, 2 * (2 * rows * width + width * units)),
        name="wgrad_down",
    )(h_a, h_b, g_a, g_b)


def up_grad_body(t_a, t_b, p_a, p_b, out):
    rows = jnp.concatenate([t_a[...], t_b[...]], axis=0)
    pre = jnp.concatenate([p_a[...], p_b[...]], axis=0)
    out[...] = dot(rows, pre, ((0,), (0,))).astype(BF16)


def up_grad(t_a, t_b, p_a, p_b, steps):
    rows, units = p_a.shape
    width = t_a.shape[1]
    cols = width // steps
    t_spec = pl.BlockSpec((rows, cols), lambda k: (0, k))
    return pl.pallas_call(
        up_grad_body,
        grid=(steps,),
        in_specs=[t_spec, t_spec] + [full((rows, units))] * 2,
        out_specs=pl.BlockSpec((cols, units), lambda k: (k, 0)),
        out_shape=jax.ShapeDtypeStruct((width, units), BF16),
        cost_estimate=cost(4 * rows * width * units, 2 * (2 * rows * width + width * units)),
        name="wgrad_up",
    )(t_a, t_b, p_a, p_b)


def sizes(width):
    rest = 6 * (width // 28)
    return (width - rest) // 2, rest


def block_width(width):
    return sizes(width)[0]


def placements(row, base, slot):
    main = [row == base + 2 * slot, row == base + 2 * slot + 1]
    rest = ((slot == 0) & (row == base + 6)) | ((slot == 1) & (row == base + 7))
    last = [(slot == 2) & (row == base + 6), (slot == 2) & (row == base + 7)]
    return [hit.astype(BF16) for hit in (main[0], main[1], rest, last[0], last[1])]


def write_blocks(out, place, rows):
    wide, rest = sizes(rows.shape[1])
    half, start = rest // 2, 2 * wide
    lead = jnp.concatenate(place[:3], axis=1)
    second = jnp.concatenate(place[:2] + place[3:], axis=1)
    third = jnp.concatenate(place[:2], axis=1)
    out[:, :rest] = dot(lead, jnp.concatenate(
        [rows[:, :rest], rows[:, wide : wide + rest], rows[:, start:]], axis=0)).astype(BF16)
    end = rest + half
    out[:, rest:end] = dot(second, jnp.concatenate(
        [rows[:, rest:end], rows[:, wide + rest : wide + end],
         rows[:, start : start + half], rows[:, start + half :]], axis=0)).astype(BF16)
    out[:, end:] = dot(third, jnp.concatenate(
        [rows[:, end:wide], rows[:, wide + end : start]], axis=0)).astype(BF16)


def read_blocks(out, place, block, precision=None):
    wide, rest = sizes(out.shape[1])
    half, start = rest // 2, 2 * wide

    def pick(a, b):
        return lax.dot_general(
            a, b, (((1,), (0,)), ((), ())), precision=precision, preferred_element_type=F32)

    out[:, :wide] = pick(place[0], block).astype(BF16)
    out[:, wide:start] = pick(place[1], block).astype(BF16)
    both = jnp.concatenate([place[2], place[3]], axis=1)
    other = jnp.concatenate([place[2], place[4]], axis=1)
    side = block[:, rest : rest + half]
    out[:, start : start + half] = pick(
        both, jnp.concatenate([block[:, :half], side], axis=0)).astype(BF16)
    out[:, start + half :] = pick(
        other, jnp.concatenate([block[:, half:rest], side], axis=0)).astype(BF16)


def pair_slots(by_lane, by_row):
    count = by_lane.shape[1]
    same = by_lane == by_row
    first = lax.broadcasted_iota(I32, (count, count), 0)
    second = lax.broadcasted_iota(I32, (count, count), 1)
    along_lane = jnp.sum((same & (first < second)).astype(F32), axis=0, keepdims=True)
    along_row = jnp.sum((same & (second < first)).astype(F32), axis=1, keepdims=True)
    return along_lane.astype(I32), along_row.astype(I32)


def dispatch_body(scaled, ids_lane, ids_row, *refs):
    by_lane = ids_lane[...]
    slot, _ = pair_slots(by_lane, ids_row[...])
    out = refs[-1]
    row = lax.broadcasted_iota(I32, (out.shape[0], by_lane.shape[1]), 0)
    place = placements(row, by_lane * GROUP, slot)
    source = refs[-2][...]
    if scaled:
        source = source.astype(F32)
        mix = refs[0][...]
        pairs = [(mix[:, k : k + 1] * source).astype(BF16) for k in range(2)]
    else:
        pairs = [source, source]
    write_blocks(out, place, jnp.concatenate(pairs, axis=0))


def static_slots(axis, shape):
    index = lax.broadcasted_iota(I32, shape, axis)
    owner = (index * 43) >> 7
    return owner * GROUP, index - owner * CAP


def collect_body(left, middle, right, out):
    total = left[...].astype(F32) + middle[...].astype(F32) + right[...].astype(F32)
    rows = total.astype(BF16)
    shape = (out.shape[0], rows.shape[0])
    base, slot = static_slots(1, shape)
    write_blocks(out, placements(lax.broadcasted_iota(I32, shape, 0), base, slot), rows)


def unpack_body(block, out):
    shape = (out.shape[0], block.shape[0])
    base, slot = static_slots(0, shape)
    place = placements(lax.broadcasted_iota(I32, shape, 1), base, slot)
    read_blocks(out, place, block[...])


def combine_body(weighted, ids_lane, ids_row, *refs):
    block, out = refs[-2], refs[-1]
    by_row = ids_row[...]
    _, slot = pair_slots(ids_lane[...], by_row)
    shape = (by_row.shape[0], block.shape[0])
    place = placements(lax.broadcasted_iota(I32, shape, 1), by_row * GROUP, slot)
    count = out.shape[0]
    if weighted:
        mix = refs[0][...]
        place = [
            p[:count].astype(F32) * mix[:, 0:1] + p[count:].astype(F32) * mix[:, 1:2]
            for p in place
        ]
        read_blocks(out, place, block[...].astype(F32), lax.Precision.HIGHEST)
    else:
        read_blocks(out, [p[:count] + p[count:] for p in place], block[...])


def single(body, shape, flops, *args):
    moved = sum(a.size * a.dtype.itemsize for a in args) + 2 * shape[0] * shape[1]
    return pl.pallas_call(
        body, out_shape=jax.ShapeDtypeStruct(shape, BF16), cost_estimate=cost(flops, moved)
    )(*args)


def per_device(tokens, expert_ids, mix_weights, w_up, w_down, out_grad):
    tok_count, width = tokens.shape
    dp_count = lax.axis_size("dp")
    ring = dp_count // 2
    experts = lax.axis_size("expert") * w_up.shape[0]
    block_shape = (experts * GROUP, block_width(width))
    rows_shape = (experts * CAP, width)
    small = 2 * block_shape[0] * block_shape[1] * 256
    core_perm = [(i, i ^ 1) for i in range(dp_count)]

    def shift(value, step):
        perm = [(2 * x + c, 2 * ((x + step) % ring) + c) for x in range(ring) for c in range(2)]
        return lax.ppermute(value, "dp", perm)

    def swap(value):
        return lax.ppermute(value, "dp", core_perm)

    def exchange(packed):
        blocks = packed.reshape(experts, GROUP, block_shape[1])
        moved = lax.all_to_all(blocks, "expert", split_axis=0, concat_axis=0, tiled=True)
        return moved.reshape(block_shape)

    def small_call(body, shape, *args):
        return single(body, shape, small, *args)

    def gather_x(own, forward):
        left, right = shift(own, -1), shift(own, 1)
        relayed = right if forward == 1 else left
        return own, left, right, shift(relayed, forward)

    def scatter_x(parts, forward):
        own, left, right, far = parts
        via = shift(far, forward)
        if forward == 1:
            left = (left.astype(F32) + via.astype(F32)).astype(BF16)
        else:
            right = (right.astype(F32) + via.astype(F32)).astype(BF16)
        return own, shift(left, 1), shift(right, -1)

    up_own, down_own = w_up[0], w_down[0]
    by_choice = expert_ids.T
    ids_lane, ids_row = by_choice.reshape(1, -1), by_choice.reshape(-1, 1)

    token_send = small_call(
        functools.partial(dispatch_body, False), block_shape, ids_lane, ids_row, tokens)
    token_moved = exchange(token_send)
    grad_send = small_call(
        functools.partial(dispatch_body, True), block_shape,
        ids_lane, ids_row, mix_weights, out_grad)
    grad_moved = exchange(grad_send)

    up_other, down_other = swap(up_own), swap(down_own)
    token_own = small_call(unpack_body, rows_shape, token_moved)
    grad_own = small_call(unpack_body, rows_shape, grad_moved)
    token_parts = gather_x(token_own, 1)
    grad_parts = gather_x(grad_own, -1)

    token_rows, pre_act, h_own, h_other = rows_matmul(
        token_parts, up_own, up_other, None, STEPS)
    out_parts = project(h_own, h_other, down_own, down_other, False, STEPS)
    grad_rows, p_own, p_other = rows_matmul(
        grad_parts, down_own, down_other, pre_act, STEPS)
    in_parts = project(p_own, p_other, up_own, up_other, True, STEPS)

    out_send = small_call(collect_body, block_shape, *scatter_x(out_parts, 1))
    in_send = small_call(collect_body, block_shape, *scatter_x(in_parts, -1))
    out_back = exchange(out_send)
    in_back = exchange(in_send)

    h_in, g_in = swap(h_other), swap(grad_rows)
    p_in, t_in = swap(p_other), swap(token_rows)
    grad_down = down_grad(h_own, h_in, grad_rows, g_in, STEPS)
    grad_up = up_grad(token_rows, t_in, p_own, p_in, STEPS)

    layer_out = small_call(
        functools.partial(combine_body, True), (tok_count, width),
        ids_lane, ids_row, mix_weights, out_back)
    token_grad = small_call(
        functools.partial(combine_body, False), (tok_count, width),
        ids_lane, ids_row, in_back)
    return layer_out, token_grad, grad_up[None], grad_down[None]


def solution(mesh):
    rows = P(("dp", "expert"), None)
    up, down = P("expert", None, "dp"), P("expert", "dp", None)

    return jax.shard_map(
        per_device,
        mesh=mesh,
        in_specs=(rows, rows, rows, up, down, rows),
        out_specs=(rows, rows, up, down),
        check_vma=False,
    )
```

profile of v0, /device:TPU:7, one launch (start us, length us, event | category | flops | bytes accessed | tf_op | source)
XLA Modules:
  0.0 194.3 jit_solution(15525184909775756538)
XLA Ops:
  1.9 1.4 reshape.48.ids_row
  3.3 2.3 %shard_map.93 = bf16[256,1408]{1,0:T(8,128)(2,1)} custom-call(s32[1,64]{1,0:T(1,128)} %reshape.38.ids_lane, s32[64,1]{1,0:T(8,128)} %reshape.48.ids_row, bf16[32,3584]{1,0:T(8,128)(2,1)} %refs_0_.3), custom_call_target="tpu_custom_call" | custom-call | flops 184549376 | bytes 950784 | tf_op jit(solution)/shard_map/pallas_call | solution.py:283
  5.6 11.2 %all-to-all-start = ((bf16[32,8,1408]{2,1,0:T(8,128)(2,1)}), bf16[32,8,1408]{2,1,0:T(8,128)(2,1)S(1)}, u32[]{:S(2)}, u32[]{:S(2)}) async-start(bf16[32,8,1408]{2,1,0:T(8,128)(2,1)} %bitcast.18), calls=%async_computation | async-start | bytes 1441792 | tf_op jit(solution)/shard_map/all_to_all | solution.py:307
  18.0 1.4 copy.12.refs_0_
  19.4 2.4 %shard_map.99 = bf16[256,1408]{1,0:T(8,128)(2,1)} custom-call(s32[1,64]{1,0:T(1,128)} %reshape.38.ids_lane, s32[64,1]{1,0:T(8,128)} %reshape.48.ids_row, f32[32,2]{1,0:T(8,128)} %copy.12.refs_0_, bf16[32,3584]{1,0:T(8,128)(2,1)} %refs_1_.1), custom_call_target="tpu_custom_call" | custom-call | flops 184549376 | bytes 951040 | tf_op jit(solution)/shard_map/pallas_call | solution.py:283
  21.7 13.4 %all-to-all-done = bf16[32,8,1408]{2,1,0:T(8,128)(2,1)S(1)} async-done(((bf16[32,8,1408]{2,1,0:T(8,128)(2,1)}), bf16[32,8,1408]{2,1,0:T(8,128)(2,1)S(1)}, u32[]{:S(2)}, u32[]{:S(2)}) %all-to-all-start) | async-done | bytes 720928 | tf_op jit(solution)/shard_map/all_to_all | solution.py:307
  35.1 7.9 %all-to-all-start.2 = ((bf16[32,8,1408]{2,1,0:T(8,128)(2,1)}), bf16[32,8,1408]{2,1,0:T(8,128)(2,1)S(1)}, u32[]{:S(2)}, u32[]{:S(2)}) async-start(bf16[32,8,1408]{2,1,0:T(8,128)(2,1)} %bitcast.16), calls=%async_computation.2 | async-start | bytes 1441792 | tf_op jit(solution)/shard_map/all_to_all | solution.py:307
  43.1 2.5 %shard_map.94.refs_0_ = bf16[96,3584]{1,0:T(8,128)(2,1)} custom-call(bf16[256,1408]{1,0:T(8,128)(2,1)} %bitcast.15), custom_call_target="tpu_custom_call" | custom-call | flops 184549376 | bytes 1409024 | tf_op jit(solution)/shard_map/pallas_call | solution.py:283
  47.1 14.6 %all-to-all-done.2 = bf16[32,8,1408]{2,1,0:T(8,128)(2,1)S(1)} async-done(((bf16[32,8,1408]{2,1,0:T(8,128)(2,1)}), bf16[32,8,1408]{2,1,0:T(8,128)(2,1)S(1)}, u32[]{:S(2)}, u32[]{:S(2)}) %all-to-all-start.2) | async-done | bytes 720928 | tf_op jit(solution)/shard_map/all_to_all | solution.py:307
  62.6 2.5 %shard_map.100.refs_0_ = bf16[96,3584]{1,0:T(8,128)(2,1)} custom-call(bf16[256,1408]{1,0:T(8,128)(2,1)} %bitcast.17), custom_call_target="tpu_custom_call" | custom-call | flops 184549376 | bytes 1409024 | tf_op jit(solution)/shard_map/pallas_call | solution.py:283
  65.6 2.1 %collective-permute-start.2 = (bf16[96,3584]{1,0:T(8,128)(2,1)S(1)}, bf16[96,3584]{1,0:T(8,128)(2,1)S(1)}, u32[]{:S(2)}, u32[]{:S(2)}) collective-permute-start(bf16[96,3584]{1,0:T(8,128)(2,1)S(1)} %collective-permute-done.1.refs_2_), channel_id=1, source_target_pairs={{0,64},{32,96},{64,128},{96,160},{128,192},{160,224},{192,0},{224,... | collective-permute-start | bytes 2064392 | tf_op jit(solution)/shard_map/ppermute | solution.py:300
  67.8 11.3 %collective-permute-done.8.refs_1_ = bf16[96,3584]{1,0:T(8,128)(2,1)S(1)} collective-permute-done((bf16[96,3584]{1,0:T(8,128)(2,1)}, bf16[96,3584]{1,0:T(8,128)(2,1)S(1)}, u32[]{:S(2)}, u32[]{:S(2)}) %collective-permute-start.8) | collective-permute-done | bytes 688160 | tf_op jit(solution)/shard_map/ppermute | solution.py:300
  80.1 6.8 %shard_map.95 = (bf16[384,3584]{1,0:T(8,128)(2,1)}, f32[384,768]{1,0:T(8,128)}, bf16[384,384]{1,0:T(8,128)(2,1)}, bf16[384,384]{1,0:T(8,128)(2,1)}) custom-call(bf16[96,3584]{1,0:T(8,128)(2,1)} %shard_map.94.refs_0_, bf16[96,3584]{1,0:T(8,128)(2,1)} %collective-permute-done.refs_1_, bf16[96,3584]{1,0:T(8,128)(2,1)} %copy-done.12, ...), custom_call_target="tpu_custom_call" | custom-call | flops 2113929216 | bytes 11010048 | tf_op jit(solution)/shard_map/pallas_call | solution.py:78
  86.9 5.5 %shard_map.96 = (bf16[96,3584]{1,0:T(8,128)(2,1)}, bf16[96,3584]{1,0:T(8,128)(2,1)}, bf16[96,3584]{1,0:T(8,128)(2,1)}, bf16[96,3584]{1,0:T(8,128)(2,1)}) custom-call(bf16[384,384]{1,0:T(8,128)(2,1)} %get-tuple-element.19.h_own.h_a, bf16[384,384]{1,0:T(8,128)(2,1)} %get-tuple-element.20.h_other, bf16[384,3584]{1,0:T(8,128)(2,1)} %bitcast.22, ...), custom_call_target="tpu_custom_call" | custom-call | flops 2113929216 | bytes 8257536 | tf_op jit(solution)/shard_map/pallas_call | solution.py:111
  92.4 2.6 %collective-permute-start.5 = (bf16[96,3584]{1,0:T(8,128)(2,1)}, bf16[96,3584]{1,0:T(8,128)(2,1)S(1)}, u32[]{:S(2)}, u32[]{:S(2)}) collective-permute-start(bf16[96,3584]{1,0:T(8,128)(2,1)} %get-tuple-element.23), channel_id=1, source_target_pairs={{0,64},{32,96},{64,128},{96,160},{128,192},{160,224},{192,0},{224,... | collective-permute-start | bytes 2064392 | tf_op jit(solution)/shard_map/ppermute | solution.py:300
  96.1 7.3 %shard_map.101 = (bf16[384,3584]{1,0:T(8,128)(2,1)}, bf16[384,384]{1,0:T(8,128)(2,1)}, bf16[384,384]{1,0:T(8,128)(2,1)}) custom-call(bf16[96,3584]{1,0:T(8,128)(2,1)} %shard_map.100.refs_0_, bf16[96,3584]{1,0:T(8,128)(2,1)} %copy-done.10, bf16[96,3584]{1,0:T(8,128)(2,1)} %copy-done.11, bf16[96,3584]{1,0:T(8,128)(2,1)} %copy-done.13, ...), custom_call_target="tpu_custom_call" | custom-call | flops 2113929216 | bytes 11010048 | tf_op jit(solution)/shard_map/pallas_call | solution.py:78
  103.5 1.9 collective-permute-done.5
  106.3 2.9 %collective-permute-start.6 = (bf16[96,3584]{1,0:T(8,128)(2,1)}, bf16[96,3584]{1,0:T(8,128)(2,1)S(1)}, u32[]{:S(2)}, u32[]{:S(2)}) collective-permute-start(bf16[96,3584]{1,0:T(8,128)(2,1)} %add_convert_fusion.1), channel_id=1, source_target_pairs={{0,64},{32,96},{64,128},{96,160},{128,192},{160,224},{192,0},{224,... | collective-permute-start | bytes 2064392 | tf_op jit(solution)/shard_map/ppermute | solution.py:300
  109.2 5.6 %shard_map.102 = (bf16[96,3584]{1,0:T(8,128)(2,1)}, bf16[96,3584]{1,0:T(8,128)(2,1)}, bf16[96,3584]{1,0:T(8,128)(2,1)}, bf16[96,3584]{1,0:T(8,128)(2,1)}) custom-call(bf16[384,384]{1,0:T(8,128)(2,1)} %get-tuple-element.26.h_own.p_a, bf16[384,384]{1,0:T(8,128)(2,1)} %get-tuple-element.27.h_other, bf16[3584,384]{1,0:T(8,128)(2,1)} %bitcast.26, ...), custom_call_target="tpu_custom_call" | custom-call | flops 2113929216 | bytes 8257536 | tf_op jit(solution)/shard_map/pallas_call | solution.py:111
  114.9 13.1 %collective-permute-start.14 = (bf16[384,3584]{1,0:T(8,128)(2,1)}, bf16[384,3584]{1,0:T(8,128)(2,1)}, u32[]{:S(2)}, u32[]{:S(2)}) collective-permute-start(bf16[384,3584]{1,0:T(8,128)(2,1)} %get-tuple-element.32.t_a), channel_id=1, source_target_pairs={{0,32},{32,0},{64,96},{96,64},{128,160},{160,128},{192,224},{224,1... | collective-permute-start | bytes 8257544 | tf_op jit(solution)/shard_map/ppermute | solution.py:303
  128.0 2.9 %collective-permute-start.11 = (bf16[96,3584]{1,0:T(8,128)(2,1)}, bf16[96,3584]{1,0:T(8,128)(2,1)S(1)}, u32[]{:S(2)}, u32[]{:S(2)}) collective-permute-start(bf16[96,3584]{1,0:T(8,128)(2,1)} %get-tuple-element.29), channel_id=1, source_target_pairs={{0,64},{32,96},{64,128},{96,160},{128,192},{160,224},{192,0},{224,... | collective-permute-start | bytes 2064392 | tf_op jit(solution)/shard_map/ppermute | solution.py:300
  132.1 3.0 %shard_map.97 = bf16[256,1408]{1,0:T(8,128)(2,1)} custom-call(bf16[96,3584]{1,0:T(8,128)(2,1)} %get-tuple-element.21.left, bf16[96,3584]{1,0:T(8,128)(2,1)} %copy-done.7, bf16[96,3584]{1,0:T(8,128)(2,1)} %copy-done.4), custom_call_target="tpu_custom_call" | custom-call | flops 184549376 | bytes 2785280 | tf_op jit(solution)/shard_map/pallas_call | solution.py:283
  135.1 4.2 %all-to-all-start.1 = ((bf16[32,8,1408]{2,1,0:T(8,128)(2,1)}), bf16[32,8,1408]{2,1,0:T(8,128)(2,1)S(1)}, u32[]{:S(2)}, u32[]{:S(2)}) async-start(bf16[32,8,1408]{2,1,0:T(8,128)(2,1)} %bitcast.20), calls=%async_computation.1 | async-start | bytes 1441792 | tf_op jit(solution)/shard_map/all_to_all | solution.py:307
  139.6 6.4 %collective-permute-done.11.middle = bf16[96,3584]{1,0:T(8,128)(2,1)S(1)} collective-permute-done((bf16[96,3584]{1,0:T(8,128)(2,1)}, bf16[96,3584]{1,0:T(8,128)(2,1)S(1)}, u32[]{:S(2)}, u32[]{:S(2)}) %collective-permute-start.11) | collective-permute-done | bytes 688160 | tf_op jit(solution)/shard_map/ppermute | solution.py:300
  146.0 6.1 %collective-permute-done.13.right = bf16[96,3584]{1,0:T(8,128)(2,1)S(1)} collective-permute-done((bf16[96,3584]{1,0:T(8,128)(2,1)S(1)}, bf16[96,3584]{1,0:T(8,128)(2,1)S(1)}, u32[]{:S(2)}, u32[]{:S(2)}) %collective-permute-start.13) | collective-permute-done | bytes 688160 | tf_op jit(solution)/shard_map/ppermute | solution.py:300
  152.9 3.1 %shard_map.103 = bf16[256,1408]{1,0:T(8,128)(2,1)} custom-call(bf16[96,3584]{1,0:T(8,128)(2,1)} %get-tuple-element.28.left, bf16[96,3584]{1,0:T(8,128)(2,1)} %copy-done.6, bf16[96,3584]{1,0:T(8,128)(2,1)} %copy-done.9), custom_call_target="tpu_custom_call" | custom-call | flops 184549376 | bytes 2785280 | tf_op jit(solution)/shard_map/pallas_call | solution.py:283
  156.0 8.9 %all-to-all-start.3 = ((bf16[32,8,1408]{2,1,0:T(8,128)(2,1)}), bf16[32,8,1408]{2,1,0:T(8,128)(2,1)S(1)}, u32[]{:S(2)}, u32[]{:S(2)}) async-start(bf16[32,8,1408]{2,1,0:T(8,128)(2,1)} %bitcast.19), calls=%async_computation.3 | async-start | bytes 1441792 | tf_op jit(solution)/shard_map/all_to_all | solution.py:307
  165.0 7.2 %collective-permute-start.15 = (bf16[384,384]{1,0:T(8,128)(2,1)S(1)}, bf16[384,384]{1,0:T(8,128)(2,1)S(1)}, u32[]{:S(2)}, u32[]{:S(2)}) collective-permute-start(bf16[384,384]{1,0:T(8,128)(2,1)S(1)} %copy-done.18), channel_id=1, source_target_pairs={{0,32},{32,0},{64,96},{96,64},{128,160},{160,128},{192,224},{224,1... | collective-permute-start | bytes 884744 | tf_op jit(solution)/shard_map/ppermute | solution.py:303
  174.2 6.3 %wgrad_up.1 = bf16[3584,384]{1,0:T(8,128)(2,1)} custom-call(bf16[384,3584]{1,0:T(8,128)(2,1)} %get-tuple-element.32.t_a, bf16[384,3584]{1,0:T(8,128)(2,1)} %collective-permute-done.14.t_b, bf16[384,384]{1,0:T(8,128)(2,1)} %get-tuple-element.26.h_own.p_a, bf16[384,384]{1,0:T(8,128)(2,1)} %copy-done.16), custom_call_target="tpu_custom_call" | custom-call | flops 2113929216 | bytes 8257536 | tf_op jit(solution)/shard_map/wgrad_up/pallas_call | solution.py:154
  181.2 5.5 %wgrad_down.1 = bf16[384,3584]{1,0:T(8,128)(2,1)} custom-call(bf16[384,384]{1,0:T(8,128)(2,1)} %get-tuple-element.19.h_own.h_a, bf16[384,384]{1,0:T(8,128)(2,1)} %copy-done.15, bf16[384,3584]{1,0:T(8,128)(2,1)} %get-tuple-element.33.g_a, bf16[384,3584]{1,0:T(8,128)(2,1)} %collective-permute-done.17.g_b), custom_call_target="tpu_custom_call" | custom-call | flops 2113929216 | bytes 8257536 | tf_op jit(solution)/shard_map/wgrad_down/pallas_call | solution.py:132
  186.7 4.2 %shard_map.98 = bf16[32,3584]{1,0:T(8,128)(2,1)} custom-call(s32[1,64]{1,0:T(1,128)} %reshape.38.ids_lane, s32[64,1]{1,0:T(8,128)} %reshape.48.ids_row, f32[32,2]{1,0:T(8,128)} %copy.12.refs_0_, bf16[256,1408]{1,0:T(8,128)(2,1)} %bitcast.13), custom_call_target="tpu_custom_call" | custom-call | flops 184549376 | bytes 951040 | tf_op jit(solution)/shard_map/pallas_call | solution.py:283
  191.8 2.5 %shard_map.104 = bf16[32,3584]{1,0:T(8,128)(2,1)} custom-call(s32[1,64]{1,0:T(1,128)} %reshape.38.ids_lane, s32[64,1]{1,0:T(8,128)} %reshape.48.ids_row, bf16[256,1408]{1,0:T(8,128)(2,1)} %bitcast.14), custom_call_target="tpu_custom_call" | custom-call | flops 184549376 | bytes 950784 | tf_op jit(solution)/shard_map/pallas_call | solution.py:283
  (69 shorter events, 14.3 us)
Async XLA Ops:
  5.6 29.5 %all-to-all-start = ((bf16[32,8,1408]{2,1,0:T(8,128)(2,1)}), bf16[32,8,1408]{2,1,0:T(8,128)(2,1)S(1)}, u32[]{:S(2)}, u32[]{:S(2)}) async-start(bf16[32,8,1408]{2,1,0:T(8,128)(2,1)} %bitcast.18), calls=%async_computation | async-start | bytes 1441792 | tf_op jit(solution)/shard_map/all_to_all | solution.py:307
  16.8 62.3 %collective-permute-start.3 = (bf16[3584,384]{1,0:T(8,128)(2,1)}, bf16[3584,384]{1,0:T(8,128)(2,1)}, u32[]{:S(2)}, u32[]{:S(2)}) collective-permute-start(bf16[3584,384]{1,0:T(8,128)(2,1)} %bitcast.24), channel_id=1, source_target_pairs={{0,32},{32,0},{64,96},{96,64},{128,160},{160,128},{192,224},{224,1... | collective-permute-start | bytes 8257544 | tf_op jit(solution)/shard_map/ppermute | solution.py:303
  17.9 69.0 %collective-permute-start.4 = (bf16[384,3584]{1,0:T(8,128)(2,1)}, bf16[384,3584]{1,0:T(8,128)(2,1)}, u32[]{:S(2)}, u32[]{:S(2)}) collective-permute-start(bf16[384,3584]{1,0:T(8,128)(2,1)} %bitcast.21), channel_id=1, source_target_pairs={{0,32},{32,0},{64,96},{96,64},{128,160},{160,128},{192,224},{224,1... | collective-permute-start | bytes 8257544 | tf_op jit(solution)/shard_map/ppermute | solution.py:303
  35.1 8.0 %copy-start.2 = (bf16[32,8,1408]{2,1,0:T(8,128)(2,1)}, bf16[32,8,1408]{2,1,0:T(8,128)(2,1)S(1)}, u32[]{:S(2)}) copy-start(bf16[32,8,1408]{2,1,0:T(8,128)(2,1)S(1)} %all-to-all-done) | copy-start | bytes 2162692
  35.1 26.6 %all-to-all-start.2 = ((bf16[32,8,1408]{2,1,0:T(8,128)(2,1)}), bf16[32,8,1408]{2,1,0:T(8,128)(2,1)S(1)}, u32[]{:S(2)}, u32[]{:S(2)}) async-start(bf16[32,8,1408]{2,1,0:T(8,128)(2,1)} %bitcast.16), calls=%async_computation.2 | async-start | bytes 1441792 | tf_op jit(solution)/shard_map/all_to_all | solution.py:307
  45.6 20.0 %collective-permute-start.1 = (bf16[96,3584]{1,0:T(8,128)(2,1)}, bf16[96,3584]{1,0:T(8,128)(2,1)S(1)}, u32[]{:S(2)}, u32[]{:S(2)}) collective-permute-start(bf16[96,3584]{1,0:T(8,128)(2,1)} %shard_map.94.refs_0_), channel_id=1, source_target_pairs={{0,64},{32,96},{64,128},{96,160},{128,192},{160,224},{192,0},{224,... | collective-permute-start | bytes 2064392 | tf_op jit(solution)/shard_map/ppermute | solution.py:300
  45.8 22.0 %collective-permute-start = (bf16[96,3584]{1,0:T(8,128)(2,1)}, bf16[96,3584]{1,0:T(8,128)(2,1)}, u32[]{:S(2)}, u32[]{:S(2)}) collective-permute-start(bf16[96,3584]{1,0:T(8,128)(2,1)} %shard_map.94.refs_0_), channel_id=1, source_target_pairs={{0,192},{32,224},{64,0},{96,32},{128,64},{160,96},{192,128},{224,1... | collective-permute-start | bytes 2064392 | tf_op jit(solution)/shard_map/ppermute | solution.py:300
  65.1 14.1 %collective-permute-start.8 = (bf16[96,3584]{1,0:T(8,128)(2,1)}, bf16[96,3584]{1,0:T(8,128)(2,1)S(1)}, u32[]{:S(2)}, u32[]{:S(2)}) collective-permute-start(bf16[96,3584]{1,0:T(8,128)(2,1)} %shard_map.100.refs_0_), channel_id=1, source_target_pairs={{0,192},{32,224},{64,0},{96,32},{128,64},{160,96},{192,128},{224,1... | collective-permute-start | bytes 2064392 | tf_op jit(solution)/shard_map/ppermute | solution.py:300
  65.6 13.6 %copy-start.12 = (bf16[96,3584]{1,0:T(8,128)(2,1)}, bf16[96,3584]{1,0:T(8,128)(2,1)S(1)}, u32[]{:S(2)}) copy-start(bf16[96,3584]{1,0:T(8,128)(2,1)S(1)} %collective-permute-done.1.refs_2_) | copy-start | bytes 2064388
  65.6 13.6 %collective-permute-start.2 = (bf16[96,3584]{1,0:T(8,128)(2,1)S(1)}, bf16[96,3584]{1,0:T(8,128)(2,1)S(1)}, u32[]{:S(2)}, u32[]{:S(2)}) collective-permute-start(bf16[96,3584]{1,0:T(8,128)(2,1)S(1)} %collective-permute-done.1.refs_2_), channel_id=1, source_target_pairs={{0,64},{32,96},{64,128},{96,160},{128,192},{160,224},{192,0},{224,... | collective-permute-start | bytes 2064392 | tf_op jit(solution)/shard_map/ppermute | solution.py:300
  67.8 27.3 %collective-permute-start.9 = (bf16[96,3584]{1,0:T(8,128)(2,1)}, bf16[96,3584]{1,0:T(8,128)(2,1)S(1)}, u32[]{:S(2)}, u32[]{:S(2)}) collective-permute-start(bf16[96,3584]{1,0:T(8,128)(2,1)} %shard_map.100.refs_0_), channel_id=1, source_target_pairs={{0,64},{32,96},{64,128},{96,160},{128,192},{160,224},{192,0},{224,... | collective-permute-start | bytes 2064392 | tf_op jit(solution)/shard_map/ppermute | solution.py:300
  79.2 7.7 %copy-start.10 = (bf16[96,3584]{1,0:T(8,128)(2,1)}, bf16[96,3584]{1,0:T(8,128)(2,1)S(1)}, u32[]{:S(2)}) copy-start(bf16[96,3584]{1,0:T(8,128)(2,1)S(1)} %collective-permute-done.8.refs_1_) | copy-start | bytes 2064388
  79.2 15.9 %collective-permute-start.10 = (bf16[96,3584]{1,0:T(8,128)(2,1)S(1)}, bf16[96,3584]{1,0:T(8,128)(2,1)S(1)}, u32[]{:S(2)}, u32[]{:S(2)}) collective-permute-start(bf16[96,3584]{1,0:T(8,128)(2,1)S(1)} %collective-permute-done.8.refs_1_), channel_id=1, source_target_pairs={{0,192},{32,224},{64,0},{96,32},{128,64},{160,96},{192,128},{224,1... | collective-permute-start | bytes 2064392 | tf_op jit(solution)/shard_map/ppermute | solution.py:300
  92.4 12.9 %collective-permute-start.5 = (bf16[96,3584]{1,0:T(8,128)(2,1)}, bf16[96,3584]{1,0:T(8,128)(2,1)S(1)}, u32[]{:S(2)}, u32[]{:S(2)}) collective-permute-start(bf16[96,3584]{1,0:T(8,128)(2,1)} %get-tuple-element.23), channel_id=1, source_target_pairs={{0,64},{32,96},{64,128},{96,160},{128,192},{160,224},{192,0},{224,... | collective-permute-start | bytes 2064392 | tf_op jit(solution)/shard_map/ppermute | solution.py:300
  95.0 35.9 %collective-permute-start.7 = (bf16[96,3584]{1,0:T(8,128)(2,1)}, bf16[96,3584]{1,0:T(8,128)(2,1)S(1)}, u32[]{:S(2)}, u32[]{:S(2)}) collective-permute-start(bf16[96,3584]{1,0:T(8,128)(2,1)} %get-tuple-element.24), channel_id=1, source_target_pairs={{0,192},{32,224},{64,0},{96,32},{128,64},{160,96},{192,128},{224,1... | collective-permute-start | bytes 2064392 | tf_op jit(solution)/shard_map/ppermute | solution.py:300
  95.0 1.1 copy-start.11
  96.1 9.2 %copy-start.8 = (bf16[96,3584]{1,0:T(8,128)(2,1)S(1)}, bf16[96,3584]{1,0:T(8,128)(2,1)}, u32[]{:S(2)}) copy-start(bf16[96,3584]{1,0:T(8,128)(2,1)} %get-tuple-element.22) | copy-start | bytes 2064388
  106.3 24.8 %collective-permute-start.6 = (bf16[96,3584]{1,0:T(8,128)(2,1)}, bf16[96,3584]{1,0:T(8,128)(2,1)S(1)}, u32[]{:S(2)}, u32[]{:S(2)}) collective-permute-start(bf16[96,3584]{1,0:T(8,128)(2,1)} %add_convert_fusion.1), channel_id=1, source_target_pairs={{0,64},{32,96},{64,128},{96,160},{128,192},{160,224},{192,0},{224,... | collective-permute-start | bytes 2064392 | tf_op jit(solution)/shard_map/ppermute | solution.py:300
  114.9 24.5 %copy-start.5 = (bf16[96,3584]{1,0:T(8,128)(2,1)S(1)}, bf16[96,3584]{1,0:T(8,128)(2,1)}, u32[]{:S(2)}) copy-start(bf16[96,3584]{1,0:T(8,128)(2,1)} %get-tuple-element.30) | copy-start | bytes 2064388
  114.9 24.5 %collective-permute-start.12 = (bf16[96,3584]{1,0:T(8,128)(2,1)}, bf16[96,3584]{1,0:T(8,128)(2,1)S(1)}, u32[]{:S(2)}, u32[]{:S(2)}) collective-permute-start(bf16[96,3584]{1,0:T(8,128)(2,1)} %get-tuple-element.31), channel_id=1, source_target_pairs={{0,192},{32,224},{64,0},{96,32},{128,64},{160,96},{192,128},{224,1... | collective-permute-start | bytes 2064392 | tf_op jit(solution)/shard_map/ppermute | solution.py:300
  114.9 58.5 %collective-permute-start.14 = (bf16[384,3584]{1,0:T(8,128)(2,1)}, bf16[384,3584]{1,0:T(8,128)(2,1)}, u32[]{:S(2)}, u32[]{:S(2)}) collective-permute-start(bf16[384,3584]{1,0:T(8,128)(2,1)} %get-tuple-element.32.t_a), channel_id=1, source_target_pairs={{0,32},{32,0},{64,96},{96,64},{128,160},{160,128},{192,224},{224,1... | collective-permute-start | bytes 8257544 | tf_op jit(solution)/shard_map/ppermute | solution.py:303
  128.0 18.0 %collective-permute-start.11 = (bf16[96,3584]{1,0:T(8,128)(2,1)}, bf16[96,3584]{1,0:T(8,128)(2,1)S(1)}, u32[]{:S(2)}, u32[]{:S(2)}) collective-permute-start(bf16[96,3584]{1,0:T(8,128)(2,1)} %get-tuple-element.29), channel_id=1, source_target_pairs={{0,64},{32,96},{64,128},{96,160},{128,192},{160,224},{192,0},{224,... | collective-permute-start | bytes 2064392 | tf_op jit(solution)/shard_map/ppermute | solution.py:300
  130.9 49.6 %collective-permute-start.17 = (bf16[384,3584]{1,0:T(8,128)(2,1)}, bf16[384,3584]{1,0:T(8,128)(2,1)}, u32[]{:S(2)}, u32[]{:S(2)}) collective-permute-start(bf16[384,3584]{1,0:T(8,128)(2,1)} %get-tuple-element.33.g_a), channel_id=1, source_target_pairs={{0,32},{32,0},{64,96},{96,64},{128,160},{160,128},{192,224},{224,1... | collective-permute-start | bytes 8257544 | tf_op jit(solution)/shard_map/ppermute | solution.py:303
  135.1 20.9 %all-to-all-start.1 = ((bf16[32,8,1408]{2,1,0:T(8,128)(2,1)}), bf16[32,8,1408]{2,1,0:T(8,128)(2,1)S(1)}, u32[]{:S(2)}, u32[]{:S(2)}) async-start(bf16[32,8,1408]{2,1,0:T(8,128)(2,1)} %bitcast.20), calls=%async_computation.1 | async-start | bytes 1441792 | tf_op jit(solution)/shard_map/all_to_all | solution.py:307
  139.3 25.7 %copy-start.18 = (bf16[384,384]{1,0:T(8,128)(2,1)S(1)}, bf16[384,384]{1,0:T(8,128)(2,1)}, u32[]{:S(2)}) copy-start(bf16[384,384]{1,0:T(8,128)(2,1)} %get-tuple-element.27.h_other) | copy-start | bytes 884740
  139.4 32.9 %copy-start.17 = (bf16[384,384]{1,0:T(8,128)(2,1)S(1)}, bf16[384,384]{1,0:T(8,128)(2,1)}, u32[]{:S(2)}) copy-start(bf16[384,384]{1,0:T(8,128)(2,1)} %get-tuple-element.20.h_other) | copy-start | bytes 884740
  139.5 12.6 %collective-permute-start.13 = (bf16[96,3584]{1,0:T(8,128)(2,1)S(1)}, bf16[96,3584]{1,0:T(8,128)(2,1)S(1)}, u32[]{:S(2)}, u32[]{:S(2)}) collective-permute-start(bf16[96,3584]{1,0:T(8,128)(2,1)S(1)} %add_convert_fusion), channel_id=1, source_target_pairs={{0,192},{32,224},{64,0},{96,32},{128,64},{160,96},{192,128},{224,1... | collective-permute-start | bytes 2064392 | tf_op jit(solution)/shard_map/ppermute | solution.py:300
  146.0 6.1 %copy-start.6 = (bf16[96,3584]{1,0:T(8,128)(2,1)}, bf16[96,3584]{1,0:T(8,128)(2,1)S(1)}, u32[]{:S(2)}) copy-start(bf16[96,3584]{1,0:T(8,128)(2,1)S(1)} %collective-permute-done.11.middle) | copy-start | bytes 2064388
  156.0 24.4 %copy-start = (bf16[32,8,1408]{2,1,0:T(8,128)(2,1)}, bf16[32,8,1408]{2,1,0:T(8,128)(2,1)S(1)}, u32[]{:S(2)}) copy-start(bf16[32,8,1408]{2,1,0:T(8,128)(2,1)S(1)} %all-to-all-done.1) | copy-start | bytes 2162692
  156.0 34.9 %all-to-all-start.3 = ((bf16[32,8,1408]{2,1,0:T(8,128)(2,1)}), bf16[32,8,1408]{2,1,0:T(8,128)(2,1)S(1)}, u32[]{:S(2)}, u32[]{:S(2)}) async-start(bf16[32,8,1408]{2,1,0:T(8,128)(2,1)} %bitcast.19), calls=%async_computation.3 | async-start | bytes 1441792 | tf_op jit(solution)/shard_map/all_to_all | solution.py:307
  165.0 8.4 %collective-permute-start.15 = (bf16[384,384]{1,0:T(8,128)(2,1)S(1)}, bf16[384,384]{1,0:T(8,128)(2,1)S(1)}, u32[]{:S(2)}, u32[]{:S(2)}) collective-permute-start(bf16[384,384]{1,0:T(8,128)(2,1)S(1)} %copy-done.18), channel_id=1, source_target_pairs={{0,32},{32,0},{64,96},{96,64},{128,160},{160,128},{192,224},{224,1... | collective-permute-start | bytes 884744 | tf_op jit(solution)/shard_map/ppermute | solution.py:303
  172.2 8.2 %collective-permute-start.16 = (bf16[384,384]{1,0:T(8,128)(2,1)S(1)}, bf16[384,384]{1,0:T(8,128)(2,1)S(1)}, u32[]{:S(2)}, u32[]{:S(2)}) collective-permute-start(bf16[384,384]{1,0:T(8,128)(2,1)S(1)} %copy-done.17), channel_id=1, source_target_pairs={{0,32},{32,0},{64,96},{96,64},{128,160},{160,128},{192,224},{224,1... | collective-permute-start | bytes 884744 | tf_op jit(solution)/shard_map/ppermute | solution.py:303
  (9 other events, 7.6 us)
where the time goes:
time: 196 us; the launch traced here: 194 us
  starting transfers between devices  67.1 us (34%)
  Pallas kernels  59.5 us (30%)
  waiting for transfers between devices  54.6 us (28%)
  local copies, waits for them, and re-layouts  11 us (6%)
    all_to_all x4, starting transfers between devices, exchange(): lax.all_to_all(blocks, 'expert', split_axis=0, concat_axis=0, tiled=True)  32.3 us
    all_to_all x4, waiting for transfers between devices, exchange(): lax.all_to_all(blocks, 'expert', split_axis=0, concat_axis=0, tiled=True)  28 us
    ppermute x12, waiting for transfers between devices, shift(): return lax.ppermute(value, 'dp', perm)  25.7 us
    pallas_call x8, Pallas kernels, single(): pl.pallas_call(body, out_shape=jax.ShapeDtypeStruct(shape, BF16), cost_es...  22.5 us
    ppermute x6, starting transfers between devices, swap(): return lax.ppermute(value, 'dp', core_perm)  22.1 us
    pallas_call x2, Pallas kernels, rows_matmul(): pl.pallas_call(functools.partial(gather_body, back), grid=(steps,), in_sp...  14.1 us
    ppermute x12, starting transfers between devices, shift(): return lax.ppermute(value, 'dp', perm)  12.8 us
    pallas_call x2, Pallas kernels, project(): pl.pallas_call(functools.partial(project_body, by_rows), grid=(steps,), i...  11.1 us
  transfers between devices with their start and end apart: 22, of which 7 were waited for; matrix products, arithmetic and copies ran while one was open for 1% of the time, Pallas kernels for 28%

commit v1 on v0

--- a/solution.py
+++ b/solution.py
@@ -26,16 +26,24 @@
     return pl.CostEstimate(flops=flops, transcendentals=0, bytes_accessed=bytes_accessed)
 
 
-def gather_body(back, *refs):
-    pieces, (w_own, w_other) = refs[:4], refs[4:6]
+def gather_body(back, split, *refs):
+    refs, pieces = list(refs), []
+    for halves in split:
+        pieces.append([refs.pop(0) for _ in range(halves)])
+    w_own, w_other = refs[:2]
     if back:
-        pre, (rows_out, first, second), (acc,) = refs[6], refs[7:10], refs[10:]
-    else:
-        rows_out, pre_out, first, second, acc = refs[6:]
+        pre, rows_out, first, second, acc = refs[2:]
+    else:
+        rows_out, pre_out, first, second, acc = refs[2:]
     k = pl.program_id(0)
-    size = pieces[0].shape[0]
+    size = pieces[0][0].shape[0]
     for b, piece in enumerate(pieces):
-        rows_out[b * size : (b + 1) * size, :] = piece[...]
+        for step in range(len(piece)):
+
+            @pl.when((k == step) | (len(piece) == 1))
+            def _():
+                rows_out[b * size : (b + 1) * size, :] = piece[step][...]
+
     if back:
         weight = jnp.concatenate([w_own[...], w_other[...]], axis=0)
         part = dot(rows_out[...], weight, ((1,), (1,)))
@@ -68,23 +76,25 @@
 
 def rows_matmul(pieces, w_own, w_other, pre, steps):
     back = pre is not None
-    size, width = pieces[0].shape
-    rows, cols = 4 * size, width // steps
+    split = tuple(len(piece) for piece in pieces)
+    size, cols = pieces[-1][0].shape
+    rows, width = 4 * size, cols * steps
     units = w_own.shape[0] if back else w_own.shape[1]
-    piece = pl.BlockSpec((size, cols), lambda k: (0, k))
+    whole, half = pl.BlockSpec((size, cols), lambda k: (0, k)), full((size, cols))
+    piece_specs = [half if n > 1 else whole for n in split for _ in range(n)]
     weight = pl.BlockSpec((units, cols), lambda k: (0, k)) if back else pl.BlockSpec((cols, units), lambda k: (k, 0))
     wide, narrow = full((rows, 2 * units)), full((rows, units))
     narrow_shape = jax.ShapeDtypeStruct((rows, units), BF16)
     return pl.pallas_call(
-        functools.partial(gather_body, back),
+        functools.partial(gather_body, back, split),
         grid=(steps,),
-        in_specs=[piece] * 4 + [weight, weight] + [wide] * back,
+        in_specs=piece_specs + [weight, weight] + [wide] * back,
         out_specs=[pl.BlockSpec((rows, cols), lambda k: (0, k))] + [wide] * (not back) + [narrow, narrow],
         out_shape=[jax.ShapeDtypeStruct((rows, width), BF16)]
         + [jax.ShapeDtypeStruct((rows, 2 * units), F32)] * (not back) + [narrow_shape, narrow_shape],
         scratch_shapes=[pltpu.VMEM((rows, 2 * units), F32)],
         cost_estimate=cost(4 * rows * width * units, 4 * (rows * width + width * units)),
-    )(*pieces, w_own, w_other, *([pre] * back))
+    )(*[part for piece in pieces for part in piece], w_own, w_other, *([pre] * back))
 
 
 def project_body(by_rows, h_own, h_other, w_own, w_other, *outs):
@@ -96,8 +106,12 @@
         weight = jnp.concatenate([w_own[...], w_other[...]], axis=0)
         value = dot(hidden, weight).astype(BF16)
     size = outs[0].shape[0]
-    for b, out in enumerate(outs):
-        out[...] = value[b * size : (b + 1) * size, :]
+    for step in range(2):
+
+        @pl.when(pl.program_id(0) == step)
+        def _():
+            for b in range(4):
+                outs[2 * b + step][...] = value[b * size : (b + 1) * size, :]
 
 
 def project(h_own, h_other, w_own, w_other, by_rows, steps):
@@ -112,8 +126,8 @@
         functools.partial(project_body, by_rows),
         grid=(steps,),
         in_specs=[full((rows, units))] * 2 + [weight, weight],
-        out_specs=[pl.BlockSpec((size, cols), lambda k: (0, k))] * 4,
-        out_shape=[jax.ShapeDtypeStruct((size, width), BF16)] * 4,
+        out_specs=[full((size, cols))] * 8,
+        out_shape=[jax.ShapeDtypeStruct((size, cols), BF16)] * 8,
         cost_estimate=cost(4 * rows * width * units, 2 * (rows * width + 2 * width * units)),
     )(h_own, h_other, w_own, w_other)
 
@@ -194,23 +208,30 @@
         [rows[:, end:wide], rows[:, wide + end : start]], axis=0)).astype(BF16)
 
 
-def read_blocks(out, place, block, precision=None):
-    wide, rest = sizes(out.shape[1])
-    half, start = rest // 2, 2 * wide
+def read_blocks(width, place, block, parts=1):
+    _, rest = sizes(width)
+    half = rest // 2
 
     def pick(a, b):
-        return lax.dot_general(
-            a, b, (((1,), (0,)), ((), ())), precision=precision, preferred_element_type=F32)
-
-    out[:, :wide] = pick(place[0], block).astype(BF16)
-    out[:, wide:start] = pick(place[1], block).astype(BF16)
+        value = dot(a, b)
+        size = value.shape[0] // parts
+        total = value[(parts - 1) * size :]
+        for part in range(parts - 2, -1, -1):
+            total = total + value[part * size : (part + 1) * size]
+        return total.astype(BF16)
+
     both = jnp.concatenate([place[2], place[3]], axis=1)
     other = jnp.concatenate([place[2], place[4]], axis=1)
     side = block[:, rest : rest + half]
-    out[:, start : start + half] = pick(
-        both, jnp.concatenate([block[:, :half], side], axis=0)).astype(BF16)
-    out[:, start + half :] = pick(
-        other, jnp.concatenate([block[:, half:rest], side], axis=0)).astype(BF16)
+    return jnp.concatenate(
+        [
+            pick(place[0], block),
+            pick(place[1], block),
+            pick(both, jnp.concatenate([block[:, :half], side], axis=0)),
+            pick(other, jnp.concatenate([block[:, half:rest], side], axis=0)),
+        ],
+        axis=1,
+    )
 
 
 def pair_slots(by_lane, by_row):
@@ -245,19 +266,25 @@
     return owner * GROUP, index - owner * CAP
 
 
-def collect_body(left, middle, right, out):
-    total = left[...].astype(F32) + middle[...].astype(F32) + right[...].astype(F32)
-    rows = total.astype(BF16)
+def collect_body(*refs):
+    halves = []
+    for own, right, left in (refs[0:3], refs[3:6]):
+        total = own[...].astype(F32) + right[...].astype(F32) + left[...].astype(F32)
+        halves.append(total.astype(BF16))
+    rows, out = jnp.concatenate(halves, axis=1), refs[6]
     shape = (out.shape[0], rows.shape[0])
     base, slot = static_slots(1, shape)
     write_blocks(out, placements(lax.broadcasted_iota(I32, shape, 0), base, slot), rows)
 
 
-def unpack_body(block, out):
-    shape = (out.shape[0], block.shape[0])
+def unpack_body(block, *outs):
+    count, cols = outs[0].shape
+    shape = (count, block.shape[0])
     base, slot = static_slots(0, shape)
     place = placements(lax.broadcasted_iota(I32, shape, 1), base, slot)
-    read_blocks(out, place, block[...])
+    rows = read_blocks(len(outs) * cols, place, block[...])
+    for i, out in enumerate(outs):
+        out[...] = rows[:, i * cols : (i + 1) * cols]
 
 
 def combine_body(weighted, ids_lane, ids_row, *refs):
@@ -269,19 +296,24 @@
     count = out.shape[0]
     if weighted:
         mix = refs[0][...]
-        place = [
-            p[:count].astype(F32) * mix[:, 0:1] + p[count:].astype(F32) * mix[:, 1:2]
-            for p in place
-        ]
-        read_blocks(out, place, block[...].astype(F32), lax.Precision.HIGHEST)
-    else:
-        read_blocks(out, [p[:count] + p[count:] for p in place], block[...])
-
-
-def single(body, shape, flops, *args):
-    moved = sum(a.size * a.dtype.itemsize for a in args) + 2 * shape[0] * shape[1]
+        split = []
+        for p in place:
+            weight = p[:count].astype(F32) * mix[:, 0:1] + p[count:].astype(F32) * mix[:, 1:2]
+            pieces = []
+            for _ in range(3):
+                pieces.append(weight.astype(BF16))
+                weight = weight - pieces[-1].astype(F32)
+            split.append(jnp.concatenate(pieces, axis=0))
+        out[...] = read_blocks(out.shape[1], split, block[...], 3)
+    else:
+        out[...] = read_blocks(out.shape[1], [p[:count] + p[count:] for p in place], block[...])
+
+
+def single(body, shape, flops, *args, outs=None):
+    moved = sum(a.size * a.dtype.itemsize for a in args) + 2 * shape[0] * shape[1] * (outs or 1)
+    out_shape = jax.ShapeDtypeStruct(shape, BF16)
     return pl.pallas_call(
-        body, out_shape=jax.ShapeDtypeStruct(shape, BF16), cost_estimate=cost(flops, moved)
+        body, out_shape=[out_shape] * outs if outs else out_shape, cost_estimate=cost(flops, moved)
     )(*args)
 
 
@@ -291,7 +323,7 @@
     ring = dp_count // 2
     experts = lax.axis_size("expert") * w_up.shape[0]
     block_shape = (experts * GROUP, block_width(width))
-    rows_shape = (experts * CAP, width)
+    half_shape = (experts * CAP, width // 2)
     small = 2 * block_shape[0] * block_shape[1] * 256
     core_perm = [(i, i ^ 1) for i in range(dp_count)]
 
@@ -307,22 +339,30 @@
         moved = lax.all_to_all(blocks, "expert", split_axis=0, concat_axis=0, tiled=True)
         return moved.reshape(block_shape)
 
-    def small_call(body, shape, *args):
-        return single(body, shape, small, *args)
-
-    def gather_x(own, forward):
-        left, right = shift(own, -1), shift(own, 1)
-        relayed = right if forward == 1 else left
-        return own, left, right, shift(relayed, forward)
-
-    def scatter_x(parts, forward):
-        own, left, right, far = parts
-        via = shift(far, forward)
-        if forward == 1:
-            left = (left.astype(F32) + via.astype(F32)).astype(BF16)
-        else:
-            right = (right.astype(F32) + via.astype(F32)).astype(BF16)
-        return own, shift(left, 1), shift(right, -1)
+    def small_call(body, shape, *args, outs=None):
+        return single(body, shape, small, *args, outs=outs)
+
+    def gather_x(low, high):
+        right, left = shift(low, 1), shift(high, -1)
+        right_high, left_low = shift(high, 1), shift(low, -1)
+        far_low, far_high = shift(right, 1), shift(left, -1)
+        return (low, high), (right, right_high), (left_low, left), (far_low, far_high)
+
+    def gather_whole(own):
+        right, left = shift(own, 1), shift(own, -1)
+        far_low = shift(right[:, : width // 2], 1)
+        far_high = shift(left[:, width // 2 :], -1)
+        return (own,), (right,), (left,), (far_low, far_high)
+
+    def scatter_x(parts):
+        low, high, to_left, to_left_high, to_right, to_right_high, far_low, far_high = parts
+        via_low, via_high = shift(far_low, 1), shift(far_high, -1)
+        high_in, low_in = shift(to_right_high, 1), shift(to_left, -1)
+        on_right = (to_right.astype(F32) + via_low.astype(F32)).astype(BF16)
+        on_left = (to_left_high.astype(F32) + via_high.astype(F32)).astype(BF16)
+        low_other = shift(on_right, 1)
+        high_other = shift(on_left, -1)
+        return low, low_in, low_other, high, high_in, high_other
 
     up_own, down_own = w_up[0], w_down[0]
     by_choice = expert_ids.T
@@ -337,10 +377,10 @@
     grad_moved = exchange(grad_send)
 
     up_other, down_other = swap(up_own), swap(down_own)
-    token_own = small_call(unpack_body, rows_shape, token_moved)
-    grad_own = small_call(unpack_body, rows_shape, grad_moved)
-    token_parts = gather_x(token_own, 1)
-    grad_parts = gather_x(grad_own, -1)
+    token_own = small_call(unpack_body, (half_shape[0], width), token_moved)
+    grad_own = small_call(unpack_body, half_shape, grad_moved, outs=2)
+    token_parts = gather_whole(token_own)
+    grad_parts = gather_x(*grad_own)
 
     token_rows, pre_act, h_own, h_other = rows_matmul(
         token_parts, up_own, up_other, None, STEPS)
@@ -349,8 +389,8 @@
         grad_parts, down_own, down_other, pre_act, STEPS)
     in_parts = project(p_own, p_other, up_own, up_other, True, STEPS)
 
-    out_send = small_call(collect_body, block_shape, *scatter_x(out_parts, 1))
-    in_send = small_call(collect_body, block_shape, *scatter_x(in_parts, -1))
+    out_send = small_call(collect_body, block_shape, *scatter_x(out_parts))
+    in_send = small_call(collect_body, block_shape, *scatter_x(in_parts))
     out_back = exchange(out_send)
     in_back = exchange(in_send)
 

time: 196 us -> 225 us (1.15)
  the two profiles are of different devices: /device:TPU:7 before, /device:TPU:6 now
where the time goes in v1:
time: 225 us
  waiting for transfers between devices  92.1 us (41%)
  starting transfers between devices  61.1 us (27%)
  Pallas kernels  60.2 us (27%)
  local copies, waits for them, and re-layouts  9.95 us (4%)
    all_to_all x4, waiting for transfers between devices, exchange(): lax.all_to_all(blocks, 'expert', split_axis=0, concat_axis=0, tiled=True)  51.4 us
    ppermute x22, waiting for transfers between devices, shift(): return lax.ppermute(value, 'dp', perm)  40.6 us
    all_to_all x4, starting transfers between devices, exchange(): lax.all_to_all(blocks, 'expert', split_axis=0, concat_axis=0, tiled=True)  31 us
    ppermute x22, starting transfers between devices, shift(): return lax.ppermute(value, 'dp', perm)  28.8 us
    pallas_call x8, Pallas kernels, single(): pl.pallas_call(body, out_shape=[out_shape] * outs if outs else out_shape,...  20.6 us
    pallas_call x2, Pallas kernels, rows_matmul(): pl.pallas_call(functools.partial(gather_body, back, split), grid=(steps,)...  15.2 us
    pallas_call x2, Pallas kernels, project(): pl.pallas_call(functools.partial(project_body, by_rows), grid=(steps,), i...  12.5 us
    unnamed x61, local copies, waits for them, and re-layouts  7.21 us
  transfers between devices with their start and end apart: 32, of which 10 were waited for; matrix products, arithmetic and copies ran while one was open for 1% of the time, Pallas kernels for 23%

profile of v1, /device:TPU:6, one launch (start us, length us, event | category | flops | bytes accessed | tf_op | source)
XLA Modules:
  0.0 224.7 jit_solution(9563528214725918359)
XLA Ops:
  3.3 2.3 %shard_map.93 = bf16[256,1408]{1,0:T(8,128)(2,1)} custom-call(s32[1,64]{1,0:T(1,128)} %reshape.38.ids_lane, s32[64,1]{1,0:T(8,128)} %reshape.48.ids_row, bf16[32,3584]{1,0:T(8,128)(2,1)} %refs_0_.3), custom_call_target="tpu_custom_call" | custom-call | flops 184549376 | bytes 950784 | tf_op jit(solution)/shard_map/pallas_call | solution.py:315
  5.7 11.5 %all-to-all-start = ((bf16[32,8,1408]{2,1,0:T(8,128)(2,1)}), bf16[32,8,1408]{2,1,0:T(8,128)(2,1)S(1)}, u32[]{:S(2)}, u32[]{:S(2)}) async-start(bf16[32,8,1408]{2,1,0:T(8,128)(2,1)} %bitcast.18), calls=%async_computation | async-start | bytes 1441792 | tf_op jit(solution)/shard_map/all_to_all | solution.py:339
  19.1 2.4 %shard_map.99 = bf16[256,1408]{1,0:T(8,128)(2,1)} custom-call(s32[1,64]{1,0:T(1,128)} %reshape.38.ids_lane, s32[64,1]{1,0:T(8,128)} %reshape.48.ids_row, f32[32,2]{1,0:T(8,128)} %copy.12.refs_0_, bf16[32,3584]{1,0:T(8,128)(2,1)} %refs_1_.1), custom_call_target="tpu_custom_call" | custom-call | flops 184549376 | bytes 951040 | tf_op jit(solution)/shard_map/pallas_call | solution.py:315
  21.5 17.1 %all-to-all-done = bf16[32,8,1408]{2,1,0:T(8,128)(2,1)S(1)} async-done(((bf16[32,8,1408]{2,1,0:T(8,128)(2,1)}), bf16[32,8,1408]{2,1,0:T(8,128)(2,1)S(1)}, u32[]{:S(2)}, u32[]{:S(2)}) %all-to-all-start) | async-done | bytes 720928 | tf_op jit(solution)/shard_map/all_to_all | solution.py:339
  38.5 5.3 %all-to-all-start.2 = ((bf16[32,8,1408]{2,1,0:T(8,128)(2,1)}), bf16[32,8,1408]{2,1,0:T(8,128)(2,1)S(1)}, u32[]{:S(2)}, u32[]{:S(2)}) async-start(bf16[32,8,1408]{2,1,0:T(8,128)(2,1)} %bitcast.17), calls=%async_computation.2 | async-start | bytes 1441792 | tf_op jit(solution)/shard_map/all_to_all | solution.py:339
  43.9 2.5 %shard_map.94.refs_0_ = bf16[96,3584]{1,0:T(8,128)(2,1)} custom-call(bf16[256,1408]{1,0:T(8,128)(2,1)} %bitcast.14), custom_call_target="tpu_custom_call" | custom-call | flops 184549376 | bytes 1409024 | tf_op jit(solution)/shard_map/pallas_call | solution.py:315
  48.4 17.0 %all-to-all-done.2 = bf16[32,8,1408]{2,1,0:T(8,128)(2,1)S(1)} async-done(((bf16[32,8,1408]{2,1,0:T(8,128)(2,1)}), bf16[32,8,1408]{2,1,0:T(8,128)(2,1)S(1)}, u32[]{:S(2)}, u32[]{:S(2)}) %all-to-all-start.2) | async-done | bytes 720928 | tf_op jit(solution)/shard_map/all_to_all | solution.py:339
  66.2 2.4 %shard_map.100 = (bf16[96,1792]{1,0:T(8,128)(2,1)}, bf16[96,1792]{1,0:T(8,128)(2,1)}) custom-call(bf16[256,1408]{1,0:T(8,128)(2,1)} %bitcast.16), custom_call_target="tpu_custom_call" | custom-call | flops 184549376 | bytes 1409024 | tf_op jit(solution)/shard_map/pallas_call | solution.py:315
  72.5 7.3 %collective-permute-done.12.refs_2_ = bf16[96,1792]{1,0:T(8,128)(2,1)S(1)} collective-permute-done((bf16[96,1792]{1,0:T(8,128)(2,1)}, bf16[96,1792]{1,0:T(8,128)(2,1)S(1)}, u32[]{:S(2)}, u32[]{:S(2)}) %collective-permute-start.12) | collective-permute-done | bytes 344096 | tf_op jit(solution)/shard_map/ppermute | solution.py:332
  80.6 2.4 %collective-permute-start.13 = (bf16[96,1792]{1,0:T(8,128)(2,1)}, bf16[96,1792]{1,0:T(8,128)(2,1)S(1)}, u32[]{:S(2)}, u32[]{:S(2)}) collective-permute-start(bf16[96,1792]{1,0:T(8,128)(2,1)} %get-tuple-element.40.refs_1_), channel_id=1, source_target_pairs={{0,64},{32,96},{64,128},{96,160},{128,192},{160,224},{192,0},{224,... | collective-permute-start | bytes 1032200 | tf_op jit(solution)/shard_map/ppermute | solution.py:332
  83.0 4.1 %collective-permute-done.2.refs_3_ = bf16[96,1792]{1,0:T(8,128)(2,1)S(1)} collective-permute-done((bf16[96,1792]{1,0:T(8,128)(2,1)S(1)}, bf16[96,1792]{1,0:T(8,128)(2,1)S(1)}, u32[]{:S(2)}, u32[]{:S(2)}) %collective-permute-start.2) | collective-permute-done | bytes 344096 | tf_op jit(solution)/shard_map/ppermute | solution.py:332
  87.9 4.0 %collective-permute-done.3.refs_4_ = bf16[96,1792]{1,0:T(8,128)(2,1)S(1)} collective-permute-done((bf16[96,1792]{1,0:T(8,128)(2,1)S(1)}, bf16[96,1792]{1,0:T(8,128)(2,1)S(1)}, u32[]{:S(2)}, u32[]{:S(2)}) %collective-permute-start.3) | collective-permute-done | bytes 344096 | tf_op jit(solution)/shard_map/ppermute | solution.py:332
  94.2 7.6 %shard_map.95 = (bf16[384,3584]{1,0:T(8,128)(2,1)}, f32[384,768]{1,0:T(8,128)}, bf16[384,384]{1,0:T(8,128)(2,1)}, bf16[384,384]{1,0:T(8,128)(2,1)}) custom-call(bf16[96,3584]{1,0:T(8,128)(2,1)} %shard_map.94.refs_0_, bf16[96,3584]{1,0:T(8,128)(2,1)} %copy-done.4, bf16[96,3584]{1,0:T(8,128)(2,1)} %copy-done.5, bf16[96,1792]{1,0:T(8,128)(2,1)} %copy-done.12, ...), custom_call_target="tpu_custom_call" | custom-call | flops 2113929216 | bytes 11010048 | tf_op jit(solution)/shard_map/pallas_call | solution.py:88
  101.8 6.2 %shard_map.96 = (bf16[96,1792]{1,0:T(8,128)(2,1)}, bf16[96,1792]{1,0:T(8,128)(2,1)}, bf16[96,1792]{1,0:T(8,128)(2,1)}, bf16[96,1792]{1,0:T(8,128)(2,1)}, bf16[96...) custom-call(bf16[384,384]{1,0:T(8,128)(2,1)} %get-tuple-element.29.h_own.h_a,, ...), custom_call_target="tpu_custom_call" | custom-call | flops 2113929216 | bytes 8257536 | tf_op jit(solution)/shard_map/pallas_call | solution.py:125
  110.1 2.9 %collective-permute-start.9 = (bf16[96,1792]{1,0:T(8,128)(2,1)}, bf16[96,1792]{1,0:T(8,128)(2,1)}, u32[]{:S(2)}, u32[]{:S(2)}) collective-permute-start(bf16[96,1792]{1,0:T(8,128)(2,1)} %get-tuple-element.36), channel_id=1, source_target_pairs={{0,64},{32,96},{64,128},{96,160},{128,192},{160,224},{192,0},{224,... | collective-permute-start | bytes 1032200 | tf_op jit(solution)/shard_map/ppermute | solution.py:332
  113.8 7.6 %shard_map.101 = (bf16[384,3584]{1,0:T(8,128)(2,1)}, bf16[384,384]{1,0:T(8,128)(2,1)}, bf16[384,384]{1,0:T(8,128)(2,1)}) custom-call(bf16[96,1792]{1,0:T(8,128)(2,1)} %get-tuple-element.39.refs_0_, bf16[96,1792]{1,0:T(8,128)(2,1)} %get-tuple-element.40.refs_1_, bf16[96,1792]{1,0:T(8,128)(2,1)} %copy-done.6, bf16[96,1792]{1,0:T(8,128)(2,1)} %copy-done.8, ...), custom_call_target="tpu_custom_call" | custom-call | flops 2113929216 | bytes 11010048 | tf_op jit(solution)/shard_map/pallas_call | solution.py:88
  121.6 3.2 %collective-permute-start.8 = (bf16[96,1792]{1,0:T(8,128)(2,1)S(1)}, bf16[96,1792]{1,0:T(8,128)(2,1)S(1)}, u32[]{:S(2)}, u32[]{:S(2)}) collective-permute-start(bf16[96,1792]{1,0:T(8,128)(2,1)S(1)} %add_convert_fusion.3), channel_id=1, source_target_pairs={{0,64},{32,96},{64,128},{96,160},{128,192},{160,224},{192,0},{224,... | collective-permute-start | bytes 1032200 | tf_op jit(solution)/shard_map/ppermute | solution.py:332
  125.9 6.3 %shard_map.102 = (bf16[96,1792]{1,0:T(8,128)(2,1)}, bf16[96,1792]{1,0:T(8,128)(2,1)}, bf16[96,1792]{1,0:T(8,128)(2,1)}, bf16[96,1792]{1,0:T(8,128)(2,1)}, bf16[9...) custom-call(bf16[384,384]{1,0:T(8,128)(2,1)} %get-tuple-element.42.h_own.p_a, ...), custom_call_target="tpu_custom_call" | custom-call | flops 2113929216 | bytes 8257536 | tf_op jit(solution)/shard_map/pallas_call | solution.py:125
  132.3 3.3 %collective-permute-start.19 = (bf16[96,1792]{1,0:T(8,128)(2,1)}, bf16[96,1792]{1,0:T(8,128)(2,1)S(1)}, u32[]{:S(2)}, u32[]{:S(2)}) collective-permute-start(bf16[96,1792]{1,0:T(8,128)(2,1)} %get-tuple-element.47), channel_id=1, source_target_pairs={{0,64},{32,96},{64,128},{96,160},{128,192},{160,224},{192,0},{224,... | collective-permute-start | bytes 1032200 | tf_op jit(solution)/shard_map/ppermute | solution.py:332
  136.5 3.0 %shard_map.97 = bf16[256,1408]{1,0:T(8,128)(2,1)} custom-call(bf16[96,1792]{1,0:T(8,128)(2,1)} %get-tuple-element.31.refs_0_, bf16[96,1792]{1,0:T(8,128)(2,1)} %collective-permute-done.6.refs_1_, bf16[96,1792]{1,0:T(8,128)(2,1)} %copy-done.20, bf16[96,1792]{1,0:T(8,128)(2,1)} %get-tuple-element.35.refs_3_, bf16[96,1792]{1,0:T(8,128)(2,1)} %collective-permute-done.9.refs_4_, ...), custom_call_target="tpu_custom_call" | custom-call | flops 184549376 | bytes 2785280 | tf_op jit(solution)/shard_map/pallas_call | solution.py:315
  139.5 4.4 %all-to-all-start.1 = ((bf16[32,8,1408]{2,1,0:T(8,128)(2,1)}), bf16[32,8,1408]{2,1,0:T(8,128)(2,1)S(1)}, u32[]{:S(2)}, u32[]{:S(2)}) async-start(bf16[32,8,1408]{2,1,0:T(8,128)(2,1)} %bitcast.19), calls=%async_computation.1 | async-start | bytes 1441792 | tf_op jit(solution)/shard_map/all_to_all | solution.py:339
  144.1 3.2 %collective-permute-start.21 = (bf16[96,1792]{1,0:T(8,128)(2,1)S(1)}, bf16[96,1792]{1,0:T(8,128)(2,1)S(1)}, u32[]{:S(2)}, u32[]{:S(2)}) collective-permute-start(bf16[96,1792]{1,0:T(8,128)(2,1)S(1)} %copy-done.26), channel_id=1, source_target_pairs={{0,64},{32,96},{64,128},{96,160},{128,192},{160,224},{192,0},{224,... | collective-permute-start | bytes 1032200 | tf_op jit(solution)/shard_map/ppermute | solution.py:332
  147.5 15.5 %collective-permute-done.22 = bf16[96,1792]{1,0:T(8,128)(2,1)S(1)} collective-permute-done((bf16[96,1792]{1,0:T(8,128)(2,1)S(1)}, bf16[96,1792]{1,0:T(8,128)(2,1)S(1)}, u32[]{:S(2)}, u32[]{:S(2)}) %collective-permute-start.22) | collective-permute-done | bytes 344096 | tf_op jit(solution)/shard_map/ppermute | solution.py:332
  163.2 2.1 collective-permute-start.23
  165.3 7.3 %collective-permute-done.20.refs_2_ = bf16[96,1792]{1,0:T(8,128)(2,1)S(1)} collective-permute-done((bf16[96,1792]{1,0:T(8,128)(2,1)S(1)}, bf16[96,1792]{1,0:T(8,128)(2,1)S(1)}, u32[]{:S(2)}, u32[]{:S(2)}) %collective-permute-start.20) | collective-permute-done | bytes 344096 | tf_op jit(solution)/shard_map/ppermute | solution.py:332
  174.7 3.0 %shard_map.103 = bf16[256,1408]{1,0:T(8,128)(2,1)} custom-call(bf16[96,1792]{1,0:T(8,128)(2,1)} %get-tuple-element.44.refs_0_, bf16[96,1792]{1,0:T(8,128)(2,1)} %copy-done.18, bf16[96,1792]{1,0:T(8,128)(2,1)} %copy-done.22, bf16[96,1792]{1,0:T(8,128)(2,1)} %get-tuple-element.48.refs_3_, bf16[96,1792]{1,0:T(8,128)(2,1)} %copy-done.19, bf16[96,1792]{1,0:T(8,128)(2,1)} %copy-done.23), custom_call_target="tpu_custom_call" | custom-call | flops 184549376 | bytes 2785280 | tf_op jit(solution)/shard_map/pallas_call | solution.py:315
  177.7 9.8 %all-to-all-start.3 = ((bf16[32,8,1408]{2,1,0:T(8,128)(2,1)}), bf16[32,8,1408]{2,1,0:T(8,128)(2,1)S(1)}, u32[]{:S(2)}, u32[]{:S(2)}) async-start(bf16[32,8,1408]{2,1,0:T(8,128)(2,1)} %bitcast.20), calls=%async_computation.3 | async-start | bytes 1441792 | tf_op jit(solution)/shard_map/all_to_all | solution.py:339
  188.1 2.5 %shard_map.98 = bf16[32,3584]{1,0:T(8,128)(2,1)} custom-call(s32[1,64]{1,0:T(1,128)} %reshape.38.ids_lane, s32[64,1]{1,0:T(8,128)} %reshape.48.ids_row, f32[32,2]{1,0:T(8,128)} %copy.12.refs_0_, bf16[256,1408]{1,0:T(8,128)(2,1)} %bitcast.13), custom_call_target="tpu_custom_call" | custom-call | flops 184549376 | bytes 951040 | tf_op jit(solution)/shard_map/pallas_call | solution.py:315
  190.7 17.4 %all-to-all-done.3 = bf16[32,8,1408]{2,1,0:T(8,128)(2,1)S(1)} async-done(((bf16[32,8,1408]{2,1,0:T(8,128)(2,1)}), bf16[32,8,1408]{2,1,0:T(8,128)(2,1)S(1)}, u32[]{:S(2)}, u32[]{:S(2)}) %all-to-all-start.3) | async-done | bytes 720928 | tf_op jit(solution)/shard_map/all_to_all | solution.py:339
  209.0 2.5 %shard_map.104 = bf16[32,3584]{1,0:T(8,128)(2,1)} custom-call(s32[1,64]{1,0:T(1,128)} %reshape.38.ids_lane, s32[64,1]{1,0:T(8,128)} %reshape.48.ids_row, bf16[256,1408]{1,0:T(8,128)(2,1)} %bitcast.15), custom_call_target="tpu_custom_call" | custom-call | flops 184549376 | bytes 950784 | tf_op jit(solution)/shard_map/pallas_call | solution.py:315
  212.2 6.2 %wgrad_up.1 = bf16[3584,384]{1,0:T(8,128)(2,1)} custom-call(bf16[384,3584]{1,0:T(8,128)(2,1)} %get-tuple-element.52.t_a, bf16[384,3584]{1,0:T(8,128)(2,1)} %collective-permute-done.24.t_b, bf16[384,384]{1,0:T(8,128)(2,1)} %get-tuple-element.42.h_own.p_a, bf16[384,384]{1,0:T(8,128)(2,1)} %copy-done.25), custom_call_target="tpu_custom_call" | custom-call | flops 2113929216 | bytes 8257536 | tf_op jit(solution)/shard_map/wgrad_up/pallas_call | solution.py:168
  219.1 5.5 %wgrad_down.1 = bf16[384,3584]{1,0:T(8,128)(2,1)} custom-call(bf16[384,384]{1,0:T(8,128)(2,1)} %get-tuple-element.29.h_own.h_a, bf16[384,384]{1,0:T(8,128)(2,1)} %copy-done.24, bf16[384,3584]{1,0:T(8,128)(2,1)} %get-tuple-element.53.g_a, bf16[384,3584]{1,0:T(8,128)(2,1)} %collective-permute-done.27.g_b), custom_call_target="tpu_custom_call" | custom-call | flops 2113929216 | bytes 8257536 | tf_op jit(solution)/shard_map/wgrad_down/pallas_call | solution.py:146
  (115 shorter events, 25.8 us)
Async XLA Ops:
  5.7 32.9 %all-to-all-start = ((bf16[32,8,1408]{2,1,0:T(8,128)(2,1)}), bf16[32,8,1408]{2,1,0:T(8,128)(2,1)S(1)}, u32[]{:S(2)}, u32[]{:S(2)}) async-start(bf16[32,8,1408]{2,1,0:T(8,128)(2,1)} %bitcast.18), calls=%async_computation | async-start | bytes 1441792 | tf_op jit(solution)/shard_map/all_to_all | solution.py:339
  17.1 75.2 %collective-permute-start.4 = (bf16[3584,384]{1,0:T(8,128)(2,1)}, bf16[3584,384]{1,0:T(8,128)(2,1)}, u32[]{:S(2)}, u32[]{:S(2)}) collective-permute-start(bf16[3584,384]{1,0:T(8,128)(2,1)} %bitcast.24), channel_id=1, source_target_pairs={{0,32},{32,0},{64,96},{96,64},{128,160},{160,128},{192,224},{224,1... | collective-permute-start | bytes 8257544 | tf_op jit(solution)/shard_map/ppermute | solution.py:335
  17.3 84.5 %collective-permute-start.5 = (bf16[384,3584]{1,0:T(8,128)(2,1)}, bf16[384,3584]{1,0:T(8,128)(2,1)}, u32[]{:S(2)}, u32[]{:S(2)}) collective-permute-start(bf16[384,3584]{1,0:T(8,128)(2,1)} %bitcast.21), channel_id=1, source_target_pairs={{0,32},{32,0},{64,96},{96,64},{128,160},{160,128},{192,224},{224,1... | collective-permute-start | bytes 8257544 | tf_op jit(solution)/shard_map/ppermute | solution.py:335
  38.5 26.8 %all-to-all-start.2 = ((bf16[32,8,1408]{2,1,0:T(8,128)(2,1)}), bf16[32,8,1408]{2,1,0:T(8,128)(2,1)S(1)}, u32[]{:S(2)}, u32[]{:S(2)}) async-start(bf16[32,8,1408]{2,1,0:T(8,128)(2,1)} %bitcast.17), calls=%async_computation.2 | async-start | bytes 1441792 | tf_op jit(solution)/shard_map/all_to_all | solution.py:339
  46.4 22.7 %collective-permute-start = (bf16[96,3584]{1,0:T(8,128)(2,1)}, bf16[96,3584]{1,0:T(8,128)(2,1)S(1)}, u32[]{:S(2)}, u32[]{:S(2)}) collective-permute-start(bf16[96,3584]{1,0:T(8,128)(2,1)} %shard_map.94.refs_0_), channel_id=1, source_target_pairs={{0,64},{32,96},{64,128},{96,160},{128,192},{160,224},{192,0},{224,... | collective-permute-start | bytes 2064392 | tf_op jit(solution)/shard_map/ppermute | solution.py:332
  46.9 23.8 %collective-permute-start.1 = (bf16[96,3584]{1,0:T(8,128)(2,1)}, bf16[96,3584]{1,0:T(8,128)(2,1)S(1)}, u32[]{:S(2)}, u32[]{:S(2)}) collective-permute-start(bf16[96,3584]{1,0:T(8,128)(2,1)} %shard_map.94.refs_0_), channel_id=1, source_target_pairs={{0,192},{32,224},{64,0},{96,32},{128,64},{160,96},{192,128},{224,1... | collective-permute-start | bytes 2064392 | tf_op jit(solution)/shard_map/ppermute | solution.py:332
  68.6 11.1 %collective-permute-start.12 = (bf16[96,1792]{1,0:T(8,128)(2,1)}, bf16[96,1792]{1,0:T(8,128)(2,1)S(1)}, u32[]{:S(2)}, u32[]{:S(2)}) collective-permute-start(bf16[96,1792]{1,0:T(8,128)(2,1)} %get-tuple-element.39.refs_0_), channel_id=1, source_target_pairs={{0,64},{32,96},{64,128},{96,160},{128,192},{160,224},{192,0},{224,... | collective-permute-start | bytes 1032200 | tf_op jit(solution)/shard_map/ppermute | solution.py:332
  69.1 11.5 %collective-permute-start.15 = (bf16[96,1792]{1,0:T(8,128)(2,1)}, bf16[96,1792]{1,0:T(8,128)(2,1)S(1)}, u32[]{:S(2)}, u32[]{:S(2)}) collective-permute-start(bf16[96,1792]{1,0:T(8,128)(2,1)} %get-tuple-element.40.refs_1_), channel_id=1, source_target_pairs={{0,192},{32,224},{64,0},{96,32},{128,64},{160,96},{192,128},{224,1... | collective-permute-start | bytes 1032200 | tf_op jit(solution)/shard_map/ppermute | solution.py:332
  70.7 16.4 %collective-permute-start.2 = (bf16[96,1792]{1,0:T(8,128)(2,1)S(1)}, bf16[96,1792]{1,0:T(8,128)(2,1)S(1)}, u32[]{:S(2)}, u32[]{:S(2)}) collective-permute-start(bf16[96,1792]{1,0:T(8,128)(2,1)S(1)} %slice.8), channel_id=1, source_target_pairs={{0,64},{32,96},{64,128},{96,160},{128,192},{160,224},{192,0},{224,... | collective-permute-start | bytes 1032200 | tf_op jit(solution)/shard_map/ppermute | solution.py:332
  79.7 12.1 %collective-permute-start.3 = (bf16[96,1792]{1,0:T(8,128)(2,1)S(1)}, bf16[96,1792]{1,0:T(8,128)(2,1)S(1)}, u32[]{:S(2)}, u32[]{:S(2)}) collective-permute-start(bf16[96,1792]{1,0:T(8,128)(2,1)S(1)} %slice.9), channel_id=1, source_target_pairs={{0,192},{32,224},{64,0},{96,32},{128,64},{160,96},{192,128},{224,1... | collective-permute-start | bytes 1032200 | tf_op jit(solution)/shard_map/ppermute | solution.py:332
  80.6 29.1 %collective-permute-start.13 = (bf16[96,1792]{1,0:T(8,128)(2,1)}, bf16[96,1792]{1,0:T(8,128)(2,1)S(1)}, u32[]{:S(2)}, u32[]{:S(2)}) collective-permute-start(bf16[96,1792]{1,0:T(8,128)(2,1)} %get-tuple-element.40.refs_1_), channel_id=1, source_target_pairs={{0,64},{32,96},{64,128},{96,160},{128,192},{160,224},{192,0},{224,... | collective-permute-start | bytes 1032200 | tf_op jit(solution)/shard_map/ppermute | solution.py:332
  87.1 23.0 %collective-permute-start.14 = (bf16[96,1792]{1,0:T(8,128)(2,1)}, bf16[96,1792]{1,0:T(8,128)(2,1)S(1)}, u32[]{:S(2)}, u32[]{:S(2)}) collective-permute-start(bf16[96,1792]{1,0:T(8,128)(2,1)} %get-tuple-element.39.refs_0_), channel_id=1, source_target_pairs={{0,192},{32,224},{64,0},{96,32},{128,64},{160,96},{192,128},{224,1... | collective-permute-start | bytes 1032200 | tf_op jit(solution)/shard_map/ppermute | solution.py:332
  91.9 21.1 %collective-permute-start.16 = (bf16[96,1792]{1,0:T(8,128)(2,1)S(1)}, bf16[96,1792]{1,0:T(8,128)(2,1)S(1)}, u32[]{:S(2)}, u32[]{:S(2)}) collective-permute-start(bf16[96,1792]{1,0:T(8,128)(2,1)S(1)} %collective-permute-done.12.refs_2_), channel_id=1, source_target_pairs={{0,64},{32,96},{64,128},{96,160},{128,192},{160,224},{192,0},{224,... | collective-permute-start | bytes 1032200 | tf_op jit(solution)/shard_map/ppermute | solution.py:332
  92.6 20.4 %collective-permute-start.17 = (bf16[96,1792]{1,0:T(8,128)(2,1)S(1)}, bf16[96,1792]{1,0:T(8,128)(2,1)S(1)}, u32[]{:S(2)}, u32[]{:S(2)}) collective-permute-start(bf16[96,1792]{1,0:T(8,128)(2,1)S(1)} %collective-permute-done.15.refs_5_), channel_id=1, source_target_pairs={{0,192},{32,224},{64,0},{96,32},{128,64},{160,96},{192,128},{224,1... | collective-permute-start | bytes 1032200 | tf_op jit(solution)/shard_map/ppermute | solution.py:332
  108.0 13.4 %collective-permute-start.7 = (bf16[96,1792]{1,0:T(8,128)(2,1)}, bf16[96,1792]{1,0:T(8,128)(2,1)S(1)}, u32[]{:S(2)}, u32[]{:S(2)}) collective-permute-start(bf16[96,1792]{1,0:T(8,128)(2,1)} %get-tuple-element.34), channel_id=1, source_target_pairs={{0,64},{32,96},{64,128},{96,160},{128,192},{160,224},{192,0},{224,... | collective-permute-start | bytes 1032200 | tf_op jit(solution)/shard_map/ppermute | solution.py:332
  109.7 25.9 %collective-permute-start.6 = (bf16[96,1792]{1,0:T(8,128)(2,1)}, bf16[96,1792]{1,0:T(8,128)(2,1)}, u32[]{:S(2)}, u32[]{:S(2)}) collective-permute-start(bf16[96,1792]{1,0:T(8,128)(2,1)} %get-tuple-element.32), channel_id=1, source_target_pairs={{0,192},{32,224},{64,0},{96,32},{128,64},{160,96},{192,128},{224,1... | collective-permute-start | bytes 1032200 | tf_op jit(solution)/shard_map/ppermute | solution.py:332
  110.1 25.5 %collective-permute-start.9 = (bf16[96,1792]{1,0:T(8,128)(2,1)}, bf16[96,1792]{1,0:T(8,128)(2,1)}, u32[]{:S(2)}, u32[]{:S(2)}) collective-permute-start(bf16[96,1792]{1,0:T(8,128)(2,1)} %get-tuple-element.36), channel_id=1, source_target_pairs={{0,64},{32,96},{64,128},{96,160},{128,192},{160,224},{192,0},{224,... | collective-permute-start | bytes 1032200 | tf_op jit(solution)/shard_map/ppermute | solution.py:332
  113.0 12.8 %collective-permute-start.10 = (bf16[96,1792]{1,0:T(8,128)(2,1)}, bf16[96,1792]{1,0:T(8,128)(2,1)S(1)}, u32[]{:S(2)}, u32[]{:S(2)}) collective-permute-start(bf16[96,1792]{1,0:T(8,128)(2,1)} %get-tuple-element.38), channel_id=1, source_target_pairs={{0,192},{32,224},{64,0},{96,32},{128,64},{160,96},{192,128},{224,1... | collective-permute-start | bytes 1032200 | tf_op jit(solution)/shard_map/ppermute | solution.py:332
  121.6 14.0 %collective-permute-start.8 = (bf16[96,1792]{1,0:T(8,128)(2,1)S(1)}, bf16[96,1792]{1,0:T(8,128)(2,1)S(1)}, u32[]{:S(2)}, u32[]{:S(2)}) collective-permute-start(bf16[96,1792]{1,0:T(8,128)(2,1)S(1)} %add_convert_fusion.3), channel_id=1, source_target_pairs={{0,64},{32,96},{64,128},{96,160},{128,192},{160,224},{192,0},{224,... | collective-permute-start | bytes 1032200 | tf_op jit(solution)/shard_map/ppermute | solution.py:332
  125.8 9.8 %collective-permute-start.11 = (bf16[96,1792]{1,0:T(8,128)(2,1)S(1)}, bf16[96,1792]{1,0:T(8,128)(2,1)S(1)}, u32[]{:S(2)}, u32[]{:S(2)}) collective-permute-start(bf16[96,1792]{1,0:T(8,128)(2,1)S(1)} %add_convert_fusion.2), channel_id=1, source_target_pairs={{0,192},{32,224},{64,0},{96,32},{128,64},{160,96},{192,128},{224,1... | collective-permute-start | bytes 1032200 | tf_op jit(solution)/shard_map/ppermute | solution.py:332
  132.3 15.0 %collective-permute-start.19 = (bf16[96,1792]{1,0:T(8,128)(2,1)}, bf16[96,1792]{1,0:T(8,128)(2,1)S(1)}, u32[]{:S(2)}, u32[]{:S(2)}) collective-permute-start(bf16[96,1792]{1,0:T(8,128)(2,1)} %get-tuple-element.47), channel_id=1, source_target_pairs={{0,64},{32,96},{64,128},{96,160},{128,192},{160,224},{192,0},{224,... | collective-permute-start | bytes 1032200 | tf_op jit(solution)/shard_map/ppermute | solution.py:332
  139.5 38.2 %all-to-all-start.1 = ((bf16[32,8,1408]{2,1,0:T(8,128)(2,1)}), bf16[32,8,1408]{2,1,0:T(8,128)(2,1)S(1)}, u32[]{:S(2)}, u32[]{:S(2)}) async-start(bf16[32,8,1408]{2,1,0:T(8,128)(2,1)} %bitcast.19), calls=%async_computation.1 | async-start | bytes 1441792 | tf_op jit(solution)/shard_map/all_to_all | solution.py:339
  143.9 67.6 %collective-permute-start.24 = (bf16[384,3584]{1,0:T(8,128)(2,1)}, bf16[384,3584]{1,0:T(8,128)(2,1)}, u32[]{:S(2)}, u32[]{:S(2)}) collective-permute-start(bf16[384,3584]{1,0:T(8,128)(2,1)} %get-tuple-element.52.t_a), channel_id=1, source_target_pairs={{0,32},{32,0},{64,96},{96,64},{128,160},{160,128},{192,224},{224,1... | collective-permute-start | bytes 8257544 | tf_op jit(solution)/shard_map/ppermute | solution.py:335
  144.0 19.1 %collective-permute-start.18 = (bf16[96,1792]{1,0:T(8,128)(2,1)S(1)}, bf16[96,1792]{1,0:T(8,128)(2,1)S(1)}, u32[]{:S(2)}, u32[]{:S(2)}) collective-permute-start(bf16[96,1792]{1,0:T(8,128)(2,1)S(1)} %copy-done.27), channel_id=1, source_target_pairs={{0,192},{32,224},{64,0},{96,32},{128,64},{160,96},{192,128},{224,1... | collective-permute-start | bytes 1032200 | tf_op jit(solution)/shard_map/ppermute | solution.py:332
  144.1 21.2 %collective-permute-start.21 = (bf16[96,1792]{1,0:T(8,128)(2,1)S(1)}, bf16[96,1792]{1,0:T(8,128)(2,1)S(1)}, u32[]{:S(2)}, u32[]{:S(2)}) collective-permute-start(bf16[96,1792]{1,0:T(8,128)(2,1)S(1)} %copy-done.26), channel_id=1, source_target_pairs={{0,64},{32,96},{64,128},{96,160},{128,192},{160,224},{192,0},{224,... | collective-permute-start | bytes 1032200 | tf_op jit(solution)/shard_map/ppermute | solution.py:332
  147.3 15.7 %collective-permute-start.22 = (bf16[96,1792]{1,0:T(8,128)(2,1)S(1)}, bf16[96,1792]{1,0:T(8,128)(2,1)S(1)}, u32[]{:S(2)}, u32[]{:S(2)}) collective-permute-start(bf16[96,1792]{1,0:T(8,128)(2,1)S(1)} %copy-done.28), channel_id=1, source_target_pairs={{0,192},{32,224},{64,0},{96,32},{128,64},{160,96},{192,128},{224,1... | collective-permute-start | bytes 1032200 | tf_op jit(solution)/shard_map/ppermute | solution.py:332
  147.3 71.1 %collective-permute-start.27 = (bf16[384,3584]{1,0:T(8,128)(2,1)}, bf16[384,3584]{1,0:T(8,128)(2,1)}, u32[]{:S(2)}, u32[]{:S(2)}) collective-permute-start(bf16[384,3584]{1,0:T(8,128)(2,1)} %get-tuple-element.53.g_a), channel_id=1, source_target_pairs={{0,32},{32,0},{64,96},{96,64},{128,160},{160,128},{192,224},{224,1... | collective-permute-start | bytes 8257544 | tf_op jit(solution)/shard_map/ppermute | solution.py:335
  163.0 9.5 %collective-permute-start.20 = (bf16[96,1792]{1,0:T(8,128)(2,1)S(1)}, bf16[96,1792]{1,0:T(8,128)(2,1)S(1)}, u32[]{:S(2)}, u32[]{:S(2)}) collective-permute-start(bf16[96,1792]{1,0:T(8,128)(2,1)S(1)} %add_convert_fusion.1), channel_id=1, source_target_pairs={{0,64},{32,96},{64,128},{96,160},{128,192},{160,224},{192,0},{224,... | collective-permute-start | bytes 1032200 | tf_op jit(solution)/shard_map/ppermute | solution.py:332
  163.2 10.8 %collective-permute-start.23 = (bf16[96,1792]{1,0:T(8,128)(2,1)S(1)}, bf16[96,1792]{1,0:T(8,128)(2,1)S(1)}, u32[]{:S(2)}, u32[]{:S(2)}) collective-permute-start(bf16[96,1792]{1,0:T(8,128)(2,1)S(1)} %add_convert_fusion), channel_id=1, source_target_pairs={{0,192},{32,224},{64,0},{96,32},{128,64},{160,96},{192,128},{224,1... | collective-permute-start | bytes 1032200 | tf_op jit(solution)/shard_map/ppermute | solution.py:332
  177.7 30.4 %all-to-all-start.3 = ((bf16[32,8,1408]{2,1,0:T(8,128)(2,1)}), bf16[32,8,1408]{2,1,0:T(8,128)(2,1)S(1)}, u32[]{:S(2)}, u32[]{:S(2)}) async-start(bf16[32,8,1408]{2,1,0:T(8,128)(2,1)} %bitcast.20), calls=%async_computation.3 | async-start | bytes 1441792 | tf_op jit(solution)/shard_map/all_to_all | solution.py:339
  187.5 23.9 %collective-permute-start.25 = (bf16[384,384]{1,0:T(8,128)(2,1)}, bf16[384,384]{1,0:T(8,128)(2,1)S(1)}, u32[]{:S(2)}, u32[]{:S(2)}) collective-permute-start(bf16[384,384]{1,0:T(8,128)(2,1)} %get-tuple-element.43.h_other), channel_id=1, source_target_pairs={{0,32},{32,0},{64,96},{96,64},{128,160},{160,128},{192,224},{224,1... | collective-permute-start | bytes 884744 | tf_op jit(solution)/shard_map/ppermute | solution.py:335
  187.6 30.8 %collective-permute-start.26 = (bf16[384,384]{1,0:T(8,128)(2,1)S(1)}, bf16[384,384]{1,0:T(8,128)(2,1)S(1)}, u32[]{:S(2)}, u32[]{:S(2)}) collective-permute-start(bf16[384,384]{1,0:T(8,128)(2,1)S(1)} %copy-done.29), channel_id=1, source_target_pairs={{0,32},{32,0},{64,96},{96,64},{128,160},{160,128},{192,224},{224,1... | collective-permute-start | bytes 884744 | tf_op jit(solution)/shard_map/ppermute | solution.py:335
  (30 other events, 276.6 us)

commit v2 on v1

--- a/solution.py
+++ b/solution.py
@@ -32,7 +32,7 @@
         pieces.append([refs.pop(0) for _ in range(halves)])
     w_own, w_other = refs[:2]
     if back:
-        pre, rows_out, first, second, acc = refs[2:]
+        pre, hidden, rows_out, first, second, acc = refs[2:]
     else:
         rows_out, pre_out, first, second, acc = refs[2:]
     k = pl.program_id(0)
@@ -71,11 +71,16 @@
             pre_out[...] = pre_act
             value = (pre_act * jax.nn.sigmoid(pre_act)).astype(BF16)
         first[...] = value[:, :units]
-        second[...] = value[:, units:]
-
-
-def rows_matmul(pieces, w_own, w_other, pre, steps):
-    back = pre is not None
+        if back:
+            count = value.shape[0]
+            second[:count, :] = hidden[...]
+            second[count:, :] = value[:, units:]
+        else:
+            second[...] = value[:, units:]
+
+
+def rows_matmul(pieces, w_own, w_other, saved, steps):
+    back = len(saved) > 0
     split = tuple(len(piece) for piece in pieces)
     size, cols = pieces[-1][0].shape
     rows, width = 4 * size, cols * steps
@@ -84,17 +89,19 @@
     piece_specs = [half if n > 1 else whole for n in split for _ in range(n)]
     weight = pl.BlockSpec((units, cols), lambda k: (0, k)) if back else pl.BlockSpec((cols, units), lambda k: (k, 0))
     wide, narrow = full((rows, 2 * units)), full((rows, units))
-    narrow_shape = jax.ShapeDtypeStruct((rows, units), BF16)
+    other_shape = (2 * rows if back else rows, units)
+    small_shapes = [jax.ShapeDtypeStruct(shape, BF16) for shape in ((rows, units), other_shape)]
     return pl.pallas_call(
         functools.partial(gather_body, back, split),
         grid=(steps,),
-        in_specs=piece_specs + [weight, weight] + [wide] * back,
-        out_specs=[pl.BlockSpec((rows, cols), lambda k: (0, k))] + [wide] * (not back) + [narrow, narrow],
+        in_specs=piece_specs + [weight, weight] + [wide, narrow] * back,
+        out_specs=[pl.BlockSpec((rows, cols), lambda k: (0, k))] + [wide] * (not back)
+        + [narrow, full(other_shape)],
         out_shape=[jax.ShapeDtypeStruct((rows, width), BF16)]
-        + [jax.ShapeDtypeStruct((rows, 2 * units), F32)] * (not back) + [narrow_shape, narrow_shape],
+        + [jax.ShapeDtypeStruct((rows, 2 * units), F32)] * (not back) + small_shapes,
         scratch_shapes=[pltpu.VMEM((rows, 2 * units), F32)],
         cost_estimate=cost(4 * rows * width * units, 4 * (rows * width + width * units)),
-    )(*[part for piece in pieces for part in piece], w_own, w_other, *([pre] * back))
+    )(*[part for piece in pieces for part in piece], w_own, w_other, *saved)
 
 
 def project_body(by_rows, h_own, h_other, w_own, w_other, *outs):
@@ -114,7 +121,7 @@
                 outs[2 * b + step][...] = value[b * size : (b + 1) * size, :]
 
 
-def project(h_own, h_other, w_own, w_other, by_rows, steps):
+def project(h_own, h_other, w_own, w_other, by_rows, steps, row_block=0):
     rows, units = h_own.shape
     width = w_own.shape[0] if by_rows else w_own.shape[1]
     cols, size = width // steps, rows // 4
@@ -125,7 +132,7 @@
     return pl.pallas_call(
         functools.partial(project_body, by_rows),
         grid=(steps,),
-        in_specs=[full((rows, units))] * 2 + [weight, weight],
+        in_specs=[full((rows, units)), pl.BlockSpec((rows, units), lambda k: (row_block, 0)), weight, weight],
         out_specs=[full((size, cols))] * 8,
         out_shape=[jax.ShapeDtypeStruct((size, cols), BF16)] * 8,
         cost_estimate=cost(4 * rows * width * units, 2 * (rows * width + 2 * width * units)),
@@ -168,7 +175,7 @@
     return pl.pallas_call(
         up_grad_body,
         grid=(steps,),
-        in_specs=[t_spec, t_spec] + [full((rows, units))] * 2,
+        in_specs=[t_spec, t_spec, full((rows, units)), pl.BlockSpec((rows, units), lambda k: (1, 0))],
         out_specs=pl.BlockSpec((cols, units), lambda k: (k, 0)),
         out_shape=jax.ShapeDtypeStruct((width, units), BF16),
         cost_estimate=cost(4 * rows * width * units, 2 * (2 * rows * width + width * units)),
@@ -234,19 +241,21 @@
     )
 
 
-def pair_slots(by_lane, by_row):
-    count = by_lane.shape[1]
-    same = by_lane == by_row
+def pair_slots(ids):
+    by_row = jnp.concatenate([ids[:, 0:1], ids[:, 1:2]], axis=0)
+    count = by_row.shape[0]
     first = lax.broadcasted_iota(I32, (count, count), 0)
     second = lax.broadcasted_iota(I32, (count, count), 1)
+    wide = jnp.broadcast_to(by_row.astype(F32), (count, count))
+    by_lane = jnp.sum(jnp.where(first == second, wide, 0.0), axis=0, keepdims=True)
+    same = wide == by_lane
     along_lane = jnp.sum((same & (first < second)).astype(F32), axis=0, keepdims=True)
     along_row = jnp.sum((same & (second < first)).astype(F32), axis=1, keepdims=True)
-    return along_lane.astype(I32), along_row.astype(I32)
-
-
-def dispatch_body(scaled, ids_lane, ids_row, *refs):
-    by_lane = ids_lane[...]
-    slot, _ = pair_slots(by_lane, ids_row[...])
+    return by_lane.astype(I32), along_lane.astype(I32), by_row, along_row.astype(I32)
+
+
+def dispatch_body(scaled, ids, *refs):
+    by_lane, slot, _, _ = pair_slots(ids[...])
     out = refs[-1]
     row = lax.broadcasted_iota(I32, (out.shape[0], by_lane.shape[1]), 0)
     place = placements(row, by_lane * GROUP, slot)
@@ -277,6 +286,11 @@
     write_blocks(out, placements(lax.broadcasted_iota(I32, shape, 0), base, slot), rows)
 
 
+def relay_body(first, first_via, second, second_via, first_out, second_out):
+    first_out[...] = (first[...].astype(F32) + first_via[...].astype(F32)).astype(BF16)
+    second_out[...] = (second[...].astype(F32) + second_via[...].astype(F32)).astype(BF16)
+
+
 def unpack_body(block, *outs):
     count, cols = outs[0].shape
     shape = (count, block.shape[0])
@@ -287,10 +301,9 @@
         out[...] = rows[:, i * cols : (i + 1) * cols]
 
 
-def combine_body(weighted, ids_lane, ids_row, *refs):
+def combine_body(weighted, ids, *refs):
     block, out = refs[-2], refs[-1]
-    by_row = ids_row[...]
-    _, slot = pair_slots(ids_lane[...], by_row)
+    _, _, by_row, slot = pair_slots(ids[...])
     shape = (by_row.shape[0], block.shape[0])
     place = placements(lax.broadcasted_iota(I32, shape, 1), by_row * GROUP, slot)
     count = out.shape[0]
@@ -348,63 +361,57 @@
         far_low, far_high = shift(right, 1), shift(left, -1)
         return (low, high), (right, right_high), (left_low, left), (far_low, far_high)
 
-    def gather_whole(own):
-        right, left = shift(own, 1), shift(own, -1)
-        far_low = shift(right[:, : width // 2], 1)
-        far_high = shift(left[:, width // 2 :], -1)
-        return (own,), (right,), (left,), (far_low, far_high)
-
     def scatter_x(parts):
         low, high, to_left, to_left_high, to_right, to_right_high, far_low, far_high = parts
         via_low, via_high = shift(far_low, 1), shift(far_high, -1)
         high_in, low_in = shift(to_right_high, 1), shift(to_left, -1)
-        on_right = (to_right.astype(F32) + via_low.astype(F32)).astype(BF16)
-        on_left = (to_left_high.astype(F32) + via_high.astype(F32)).astype(BF16)
+        on_right, on_left = small_call(
+            relay_body, half_shape, to_right, via_low, to_left_high, via_high,
+            outs=2)
         low_other = shift(on_right, 1)
         high_other = shift(on_left, -1)
         return low, low_in, low_other, high, high_in, high_other
 
     up_own, down_own = w_up[0], w_down[0]
-    by_choice = expert_ids.T
-    ids_lane, ids_row = by_choice.reshape(1, -1), by_choice.reshape(-1, 1)
 
     token_send = small_call(
-        functools.partial(dispatch_body, False), block_shape, ids_lane, ids_row, tokens)
+        functools.partial(dispatch_body, False), block_shape, expert_ids, tokens)
     token_moved = exchange(token_send)
     grad_send = small_call(
         functools.partial(dispatch_body, True), block_shape,
-        ids_lane, ids_row, mix_weights, out_grad)
+        expert_ids, mix_weights, out_grad)
     grad_moved = exchange(grad_send)
 
     up_other, down_other = swap(up_own), swap(down_own)
-    token_own = small_call(unpack_body, (half_shape[0], width), token_moved)
+    token_own = small_call(unpack_body, half_shape, token_moved, outs=2)
     grad_own = small_call(unpack_body, half_shape, grad_moved, outs=2)
-    token_parts = gather_whole(token_own)
+    token_parts = gather_x(*token_own)
     grad_parts = gather_x(*grad_own)
 
     token_rows, pre_act, h_own, h_other = rows_matmul(
-        token_parts, up_own, up_other, None, STEPS)
+        token_parts, up_own, up_other, (), STEPS)
     out_parts = project(h_own, h_other, down_own, down_other, False, STEPS)
-    grad_rows, p_own, p_other = rows_matmul(
-        grad_parts, down_own, down_other, pre_act, STEPS)
-    in_parts = project(p_own, p_other, up_own, up_other, True, STEPS)
+    grad_rows, p_own, both_other = rows_matmul(
+        grad_parts, down_own, down_other, (pre_act, h_other), STEPS)
+
+    in_parts = project(p_own, both_other, up_own, up_other, True, STEPS, 1)
 
     out_send = small_call(collect_body, block_shape, *scatter_x(out_parts))
     in_send = small_call(collect_body, block_shape, *scatter_x(in_parts))
     out_back = exchange(out_send)
     in_back = exchange(in_send)
 
-    h_in, g_in = swap(h_other), swap(grad_rows)
-    p_in, t_in = swap(p_other), swap(token_rows)
-    grad_down = down_grad(h_own, h_in, grad_rows, g_in, STEPS)
-    grad_up = up_grad(token_rows, t_in, p_own, p_in, STEPS)
+    both_in = swap(both_other)
+    g_in, t_in = swap(grad_rows), swap(token_rows)
+    grad_down = down_grad(h_own, both_in, grad_rows, g_in, 2 * STEPS)
+    grad_up = up_grad(token_rows, t_in, p_own, both_in, 2 * STEPS)
 
     layer_out = small_call(
         functools.partial(combine_body, True), (tok_count, width),
-        ids_lane, ids_row, mix_weights, out_back)
+        expert_ids, mix_weights, out_back)
     token_grad = small_call(
         functools.partial(combine_body, False), (tok_count, width),
-        ids_lane, ids_row, in_back)
+        expert_ids, in_back)
     return layer_out, token_grad, grad_up[None], grad_down[None]
 
 

time: 225 us -> 234 us (1.040)
  the two profiles are of different devices: /device:TPU:6 before, /device:TPU:32 now
where the time goes in v2:
time: 234 us; the launch traced here: 233 us
  waiting for transfers between devices  86.1 us (37%)
  starting transfers between devices  69.5 us (30%)
  Pallas kernels  66.3 us (28%)
  local copies, waits for them, and re-layouts  10.1 us (4%)
    ppermute x24, waiting for transfers between devices, shift(): return lax.ppermute(value, 'dp', perm)  50.3 us
    all_to_all x4, starting transfers between devices, exchange(): lax.all_to_all(blocks, 'expert', split_axis=0, concat_axis=0, tiled=True)  35.9 us
    all_to_all x4, waiting for transfers between devices, exchange(): lax.all_to_all(blocks, 'expert', split_axis=0, concat_axis=0, tiled=True)  35.7 us
    ppermute x24, starting transfers between devices, shift(): return lax.ppermute(value, 'dp', perm)  32 us
    pallas_call x10, Pallas kernels, single(): pl.pallas_call(body, out_shape=[out_shape] * outs if outs else out_shape,...  25.5 us
    pallas_call x2, Pallas kernels, rows_matmul(): pl.pallas_call(functools.partial(gather_body, back, split), grid=(steps,)...  15 us
    pallas_call x2, Pallas kernels, project(): pl.pallas_call(functools.partial(project_body, by_rows), grid=(steps,), i...  12.6 us
    unnamed x62, local copies, waits for them, and re-layouts  10.1 us
  transfers between devices with their start and end apart: 33, of which 16 were waited for; matrix products, arithmetic and copies ran while one was open for 1% of the time, Pallas kernels for 26%

profile of v2, /device:TPU:32, one launch (start us, length us, event | category | flops | bytes accessed | tf_op | source)
XLA Modules:
  0.0 232.9 jit_solution(17776154153581543945)
XLA Ops:
  5.0 11.4 %all-to-all-start = ((bf16[32,8,1408]{2,1,0:T(8,128)(2,1)}), bf16[32,8,1408]{2,1,0:T(8,128)(2,1)S(1)}, u32[]{:S(2)}, u32[]{:S(2)}) async-start(bf16[32,8,1408]{2,1,0:T(8,128)(2,1)} %bitcast.17), calls=%async_computation | async-start | bytes 1441792 | tf_op jit(solution)/shard_map/all_to_all | solution.py:352
  17.8 2.5 %shard_map.100 = bf16[256,1408]{1,0:T(8,128)(2,1)} custom-call(s32[32,2]{1,0:T(8,128)} %copy.11.ids, f32[32,2]{1,0:T(8,128)} %copy.12.refs_0_, bf16[32,3584]{1,0:T(8,128)(2,1)} %refs_1_.1), custom_call_target="tpu_custom_call" | custom-call | flops 184549376 | bytes 950784 | tf_op jit(solution)/shard_map/pallas_call | solution.py:328
  20.2 18.2 %all-to-all-done = bf16[32,8,1408]{2,1,0:T(8,128)(2,1)S(1)} async-done(((bf16[32,8,1408]{2,1,0:T(8,128)(2,1)}), bf16[32,8,1408]{2,1,0:T(8,128)(2,1)S(1)}, u32[]{:S(2)}, u32[]{:S(2)}) %all-to-all-start) | async-done | bytes 720928 | tf_op jit(solution)/shard_map/all_to_all | solution.py:352
  38.4 5.0 %all-to-all-start.2 = ((bf16[32,8,1408]{2,1,0:T(8,128)(2,1)}), bf16[32,8,1408]{2,1,0:T(8,128)(2,1)S(1)}, u32[]{:S(2)}, u32[]{:S(2)}) async-start(bf16[32,8,1408]{2,1,0:T(8,128)(2,1)} %bitcast.14), calls=%async_computation.2 | async-start | bytes 1441792 | tf_op jit(solution)/shard_map/all_to_all | solution.py:352
  50.5 7.6 %collective-permute-done.refs_2_ = bf16[96,1792]{1,0:T(8,128)(2,1)S(1)} collective-permute-done((bf16[96,1792]{1,0:T(8,128)(2,1)}, bf16[96,1792]{1,0:T(8,128)(2,1)S(1)}, u32[]{:S(2)}, u32[]{:S(2)}) %collective-permute-start) | collective-permute-done | bytes 344096 | tf_op jit(solution)/shard_map/ppermute | solution.py:345
  59.6 3.8 %collective-permute-done.1.refs_3_ = bf16[96,1792]{1,0:T(8,128)(2,1)S(1)} collective-permute-done((bf16[96,1792]{1,0:T(8,128)(2,1)}, bf16[96,1792]{1,0:T(8,128)(2,1)S(1)}, u32[]{:S(2)}, u32[]{:S(2)}) %collective-permute-start.1) | collective-permute-done | bytes 344096 | tf_op jit(solution)/shard_map/ppermute | solution.py:345
  63.7 3.0 %collective-permute-start.5 = (bf16[96,1792]{1,0:T(8,128)(2,1)S(1)}, bf16[96,1792]{1,0:T(8,128)(2,1)S(1)}, u32[]{:S(2)}, u32[]{:S(2)}) collective-permute-start(bf16[96,1792]{1,0:T(8,128)(2,1)S(1)} %collective-permute-done.3.refs_5_), channel_id=1, source_target_pairs={{0,192},{32,224},{64,0},{96,32},{128,64},{160,96},{192,128},{224,1... | collective-permute-start | bytes 1032200 | tf_op jit(solution)/shard_map/ppermute | solution.py:345
  66.9 5.7 %collective-permute-done.4.refs_6_ = bf16[96,1792]{1,0:T(8,128)(2,1)S(1)} collective-permute-done((bf16[96,1792]{1,0:T(8,128)(2,1)S(1)}, bf16[96,1792]{1,0:T(8,128)(2,1)S(1)}, u32[]{:S(2)}, u32[]{:S(2)}) %collective-permute-start.4) | collective-permute-done | bytes 344096 | tf_op jit(solution)/shard_map/ppermute | solution.py:345
  73.7 7.3 %shard_map.95 = (bf16[384,3584]{1,0:T(8,128)(2,1)}, f32[384,768]{1,0:T(8,128)}, bf16[384,384]{1,0:T(8,128)(2,1)}, bf16[384,384]{1,0:T(8,128)(2,1)}) custom-call(bf16[96,1792]{1,0:T(8,128)(2,1)} %get-tuple-element.35.refs_0_, bf16[96,1792]{1,0:T(8,128)(2,1)} %get-tuple-element.36.refs_1_, bf16[96,1792]{1,0:T(8,128)(2,1)} %copy-done.10, ...), custom_call_target="tpu_custom_call" | custom-call | flops 2113929216 | bytes 11010048 | tf_op jit(solution)/shard_map/pallas_call | solution.py:94
  81.0 6.3 %shard_map.96 = (bf16[96,1792]{1,0:T(8,128)(2,1)}, bf16[96,1792]{1,0:T(8,128)(2,1)}, bf16[96,1792]{1,0:T(8,128)(2,1)}, bf16[96,1792]{1,0:T(8,128)(2,1)}, bf16[96...) custom-call(bf16[384,384]{1,0:T(8,128)(2,1)} %get-tuple-element.37.h_own.h_a,, ...), custom_call_target="tpu_custom_call" | custom-call | flops 2113929216 | bytes 8257536 | tf_op jit(solution)/shard_map/pallas_call | solution.py:132
  87.6 3.0 %collective-permute-start.10 = (bf16[96,1792]{1,0:T(8,128)(2,1)}, bf16[96,1792]{1,0:T(8,128)(2,1)S(1)}, u32[]{:S(2)}, u32[]{:S(2)}) collective-permute-start(bf16[96,1792]{1,0:T(8,128)(2,1)} %get-tuple-element.44), channel_id=1, source_target_pairs={{0,192},{32,224},{64,0},{96,32},{128,64},{160,96},{192,128},{224,1... | collective-permute-start | bytes 1032200 | tf_op jit(solution)/shard_map/ppermute | solution.py:345
  93.8 3.2 %collective-permute-start.17 = (bf16[96,1792]{1,0:T(8,128)(2,1)}, bf16[96,1792]{1,0:T(8,128)(2,1)S(1)}, u32[]{:S(2)}, u32[]{:S(2)}) collective-permute-start(bf16[96,1792]{1,0:T(8,128)(2,1)} %get-tuple-element.50.refs_1_), channel_id=1, source_target_pairs={{0,192},{32,224},{64,0},{96,32},{128,64},{160,96},{192,128},{224,1... | collective-permute-start | bytes 1032200 | tf_op jit(solution)/shard_map/ppermute | solution.py:345
  102.7 3.4 %collective-permute-done.14.refs_2_ = bf16[96,1792]{1,0:T(8,128)(2,1)S(1)} collective-permute-done((bf16[96,1792]{1,0:T(8,128)(2,1)}, bf16[96,1792]{1,0:T(8,128)(2,1)S(1)}, u32[]{:S(2)}, u32[]{:S(2)}) %collective-permute-start.14) | collective-permute-done | bytes 344096 | tf_op jit(solution)/shard_map/ppermute | solution.py:345
  108.2 5.0 %collective-permute-done.8.refs_1_ = bf16[96,1792]{1,0:T(8,128)(2,1)S(1)} collective-permute-done((bf16[96,1792]{1,0:T(8,128)(2,1)}, bf16[96,1792]{1,0:T(8,128)(2,1)S(1)}, u32[]{:S(2)}, u32[]{:S(2)}) %collective-permute-start.8) | collective-permute-done | bytes 344096 | tf_op jit(solution)/shard_map/ppermute | solution.py:345
  113.2 3.6 %collective-permute-start.16 = (bf16[96,1792]{1,0:T(8,128)(2,1)}, bf16[96,1792]{1,0:T(8,128)(2,1)S(1)}, u32[]{:S(2)}, u32[]{:S(2)}) collective-permute-start(bf16[96,1792]{1,0:T(8,128)(2,1)} %get-tuple-element.49.refs_0_), channel_id=1, source_target_pairs={{0,192},{32,224},{64,0},{96,32},{128,64},{160,96},{192,128},{224,1... | collective-permute-start | bytes 1032200 | tf_op jit(solution)/shard_map/ppermute | solution.py:345
  116.8 4.1 %collective-permute-done.11.refs_2_ = bf16[96,1792]{1,0:T(8,128)(2,1)S(1)} collective-permute-done((bf16[96,1792]{1,0:T(8,128)(2,1)}, bf16[96,1792]{1,0:T(8,128)(2,1)S(1)}, u32[]{:S(2)}, u32[]{:S(2)}) %collective-permute-start.11) | collective-permute-done | bytes 344096 | tf_op jit(solution)/shard_map/ppermute | solution.py:345
  123.2 3.1 %shard_map.98 = bf16[256,1408]{1,0:T(8,128)(2,1)} custom-call(bf16[96,1792]{1,0:T(8,128)(2,1)} %get-tuple-element.39.refs_0_, bf16[96,1792]{1,0:T(8,128)(2,1)} %copy-done.21, bf16[96,1792]{1,0:T(8,128)(2,1)} %copy-done.23, bf16[96,1792]{1,0:T(8,128)(2,1)} %get-tuple-element.46.refs_3_, bf16[96,1792]{1,0:T(8,128)(2,1)} %copy-done.22, bf16[96,1792]{1,0:T(8,128)(2,1)} %copy-done.25), custom_call_target="tpu_custom_call" | custom-call | flops 184549376 | bytes 2785280 | tf_op jit(solution)/shard_map/pallas_call | solution.py:328
  126.3 9.8 %all-to-all-start.1 = ((bf16[32,8,1408]{2,1,0:T(8,128)(2,1)}), bf16[32,8,1408]{2,1,0:T(8,128)(2,1)S(1)}, u32[]{:S(2)}, u32[]{:S(2)}) async-start(bf16[32,8,1408]{2,1,0:T(8,128)(2,1)} %bitcast.18), calls=%async_computation.1 | async-start | bytes 1441792 | tf_op jit(solution)/shard_map/all_to_all | solution.py:352
  137.3 7.7 %shard_map.102 = (bf16[384,3584]{1,0:T(8,128)(2,1)}, bf16[384,384]{1,0:T(8,128)(2,1)}, bf16[768,384]{1,0:T(8,128)(2,1)}) custom-call(bf16[96,1792]{1,0:T(8,128)(2,1)} %get-tuple-element.49.refs_0_, bf16[96,1792]{1,0:T(8,128)(2,1)} %get-tuple-element.50.refs_1_, bf16[96,1792]{1,0:T(8,128)(2,1)} %copy-done.5, bf16[96,1792]{1,0:T(8,128)(2,1)} %copy-done.7, ...), custom_call_target="tpu_custom_call" | custom-call | flops 2113929216 | bytes 11010048 | tf_op jit(solution)/shard_map/pallas_call | solution.py:94
  145.8 6.3 %shard_map.103 = (bf16[96,1792]{1,0:T(8,128)(2,1)}, bf16[96,1792]{1,0:T(8,128)(2,1)}, bf16[96,1792]{1,0:T(8,128)(2,1)}, bf16[96,1792]{1,0:T(8,128)(2,1)}, bf16[9...) custom-call(bf16[384,384]{1,0:T(8,128)(2,1)} %get-tuple-element.52.h_own.p_a, ...), custom_call_target="tpu_custom_call" | custom-call | flops 2113929216 | bytes 8257536 | tf_op jit(solution)/shard_map/pallas_call | solution.py:132
  152.5 2.8 %collective-permute-start.22 = (bf16[96,1792]{1,0:T(8,128)(2,1)}, bf16[96,1792]{1,0:T(8,128)(2,1)S(1)}, u32[]{:S(2)}, u32[]{:S(2)}) collective-permute-start(bf16[96,1792]{1,0:T(8,128)(2,1)} %get-tuple-element.59), channel_id=1, source_target_pairs={{0,192},{32,224},{64,0},{96,32},{128,64},{160,96},{192,128},{224,1... | collective-permute-start | bytes 1032200 | tf_op jit(solution)/shard_map/ppermute | solution.py:345
  155.7 7.8 %collective-permute-done.21.first_via = bf16[96,1792]{1,0:T(8,128)(2,1)S(1)} collective-permute-done((bf16[96,1792]{1,0:T(8,128)(2,1)}, bf16[96,1792]{1,0:T(8,128)(2,1)S(1)}, u32[]{:S(2)}, u32[]{:S(2)}) %collective-permute-start.21) | collective-permute-done | bytes 344096 | tf_op jit(solution)/shard_map/ppermute | solution.py:345
  167.3 2.9 %collective-permute-done.20.refs_1_ = bf16[96,1792]{1,0:T(8,128)(2,1)S(1)} collective-permute-done((bf16[96,1792]{1,0:T(8,128)(2,1)}, bf16[96,1792]{1,0:T(8,128)(2,1)S(1)}, u32[]{:S(2)}, u32[]{:S(2)}) %collective-permute-start.20) | collective-permute-done | bytes 344096 | tf_op jit(solution)/shard_map/ppermute | solution.py:345
  170.3 3.6 %collective-permute-start.25 = (bf16[96,1792]{1,0:T(8,128)(2,1)}, bf16[96,1792]{1,0:T(8,128)(2,1)S(1)}, u32[]{:S(2)}, u32[]{:S(2)}) collective-permute-start(bf16[96,1792]{1,0:T(8,128)(2,1)} %get-tuple-element.63), channel_id=1, source_target_pairs={{0,192},{32,224},{64,0},{96,32},{128,64},{160,96},{192,128},{224,1... | collective-permute-start | bytes 1032200 | tf_op jit(solution)/shard_map/ppermute | solution.py:345
  175.9 5.6 %collective-permute-done.23.refs_2_ = bf16[96,1792]{1,0:T(8,128)(2,1)S(1)} collective-permute-done((bf16[96,1792]{1,0:T(8,128)(2,1)}, bf16[96,1792]{1,0:T(8,128)(2,1)S(1)}, u32[]{:S(2)}, u32[]{:S(2)}) %collective-permute-start.23) | collective-permute-done | bytes 344096 | tf_op jit(solution)/shard_map/ppermute | solution.py:345
  182.3 3.1 %shard_map.105 = bf16[256,1408]{1,0:T(8,128)(2,1)} custom-call(bf16[96,1792]{1,0:T(8,128)(2,1)} %get-tuple-element.54.refs_0_, bf16[96,1792]{1,0:T(8,128)(2,1)} %copy-done.24, bf16[96,1792]{1,0:T(8,128)(2,1)} %copy-done.27, bf16[96,1792]{1,0:T(8,128)(2,1)} %get-tuple-element.61.refs_3_, bf16[96,1792]{1,0:T(8,128)(2,1)} %copy-done.26, bf16[96,1792]{1,0:T(8,128)(2,1)} %copy-done.28), custom_call_target="tpu_custom_call" | custom-call | flops 184549376 | bytes 2785280 | tf_op jit(solution)/shard_map/pallas_call | solution.py:328
  185.4 9.8 %all-to-all-start.3 = ((bf16[32,8,1408]{2,1,0:T(8,128)(2,1)}), bf16[32,8,1408]{2,1,0:T(8,128)(2,1)S(1)}, u32[]{:S(2)}, u32[]{:S(2)}) async-start(bf16[32,8,1408]{2,1,0:T(8,128)(2,1)} %bitcast.19), calls=%async_computation.3 | async-start | bytes 1441792 | tf_op jit(solution)/shard_map/all_to_all | solution.py:352
  195.3 2.6 %shard_map.99 = bf16[32,3584]{1,0:T(8,128)(2,1)} custom-call(s32[32,2]{1,0:T(8,128)} %copy.11.ids, f32[32,2]{1,0:T(8,128)} %copy.12.refs_0_, bf16[256,1408]{1,0:T(8,128)(2,1)} %bitcast.12), custom_call_target="tpu_custom_call" | custom-call | flops 184549376 | bytes 950784 | tf_op jit(solution)/shard_map/pallas_call | solution.py:328
  197.9 17.6 %all-to-all-done.3 = bf16[32,8,1408]{2,1,0:T(8,128)(2,1)S(1)} async-done(((bf16[32,8,1408]{2,1,0:T(8,128)(2,1)}), bf16[32,8,1408]{2,1,0:T(8,128)(2,1)S(1)}, u32[]{:S(2)}, u32[]{:S(2)}) %all-to-all-start.3) | async-done | bytes 720928 | tf_op jit(solution)/shard_map/all_to_all | solution.py:352
  216.3 2.5 %shard_map.106 = bf16[32,3584]{1,0:T(8,128)(2,1)} custom-call(s32[32,2]{1,0:T(8,128)} %copy.11.ids, bf16[256,1408]{1,0:T(8,128)(2,1)} %bitcast.16), custom_call_target="tpu_custom_call" | custom-call | flops 184549376 | bytes 950528 | tf_op jit(solution)/shard_map/pallas_call | solution.py:328
  219.7 6.7 %wgrad_up.1 = bf16[3584,384]{1,0:T(8,128)(2,1)} custom-call(bf16[384,3584]{1,0:T(8,128)(2,1)} %get-tuple-element.64.t_a, bf16[384,3584]{1,0:T(8,128)(2,1)} %collective-permute-done.26.t_b, bf16[384,384]{1,0:T(8,128)(2,1)} %get-tuple-element.52.h_own.p_a, bf16[768,384]{1,0:T(8,128)(2,1)} %copy-done.4), custom_call_target="tpu_custom_call" | custom-call | flops 2113929216 | bytes 8257536 | tf_op jit(solution)/shard_map/wgrad_up/pallas_call | solution.py:175
  226.5 6.5 %wgrad_down.1 = bf16[384,3584]{1,0:T(8,128)(2,1)} custom-call(bf16[384,384]{1,0:T(8,128)(2,1)} %get-tuple-element.37.h_own.h_a, bf16[768,384]{1,0:T(8,128)(2,1)} %copy-done.4, bf16[384,3584]{1,0:T(8,128)(2,1)} %get-tuple-element.65.g_a, bf16[384,3584]{1,0:T(8,128)(2,1)} %collective-permute-done.28.g_b), custom_call_target="tpu_custom_call" | custom-call | flops 2113929216 | bytes 8257536 | tf_op jit(solution)/shard_map/wgrad_down/pallas_call | solution.py:153
  (112 shorter events, 40.7 us)
Async XLA Ops:
  0.6 72.3 %collective-permute-start.6 = (bf16[3584,384]{1,0:T(8,128)(2,1)}, bf16[3584,384]{1,0:T(8,128)(2,1)}, u32[]{:S(2)}, u32[]{:S(2)}) collective-permute-start(bf16[3584,384]{1,0:T(8,128)(2,1)} %bitcast.23), channel_id=1, source_target_pairs={{0,32},{32,0},{64,96},{96,64},{128,160},{160,128},{192,224},{224,1... | collective-permute-start | bytes 8257544 | tf_op jit(solution)/shard_map/ppermute | solution.py:348
  0.7 80.3 %collective-permute-start.7 = (bf16[384,3584]{1,0:T(8,128)(2,1)}, bf16[384,3584]{1,0:T(8,128)(2,1)}, u32[]{:S(2)}, u32[]{:S(2)}) collective-permute-start(bf16[384,3584]{1,0:T(8,128)(2,1)} %bitcast.20), channel_id=1, source_target_pairs={{0,32},{32,0},{64,96},{96,64},{128,160},{160,128},{192,224},{224,1... | collective-permute-start | bytes 8257544 | tf_op jit(solution)/shard_map/ppermute | solution.py:348
  5.0 33.4 %all-to-all-start = ((bf16[32,8,1408]{2,1,0:T(8,128)(2,1)}), bf16[32,8,1408]{2,1,0:T(8,128)(2,1)S(1)}, u32[]{:S(2)}, u32[]{:S(2)}) async-start(bf16[32,8,1408]{2,1,0:T(8,128)(2,1)} %bitcast.17), calls=%async_computation | async-start | bytes 1441792 | tf_op jit(solution)/shard_map/all_to_all | solution.py:352
  38.4 52.2 %all-to-all-start.2 = ((bf16[32,8,1408]{2,1,0:T(8,128)(2,1)}), bf16[32,8,1408]{2,1,0:T(8,128)(2,1)S(1)}, u32[]{:S(2)}, u32[]{:S(2)}) async-start(bf16[32,8,1408]{2,1,0:T(8,128)(2,1)} %bitcast.14), calls=%async_computation.2 | async-start | bytes 1441792 | tf_op jit(solution)/shard_map/all_to_all | solution.py:352
  45.7 12.4 %collective-permute-start = (bf16[96,1792]{1,0:T(8,128)(2,1)}, bf16[96,1792]{1,0:T(8,128)(2,1)S(1)}, u32[]{:S(2)}, u32[]{:S(2)}) collective-permute-start(bf16[96,1792]{1,0:T(8,128)(2,1)} %get-tuple-element.35.refs_0_), channel_id=1, source_target_pairs={{0,64},{32,96},{64,128},{96,160},{128,192},{160,224},{192,0},{224,... | collective-permute-start | bytes 1032200 | tf_op jit(solution)/shard_map/ppermute | solution.py:345
  47.2 16.2 %collective-permute-start.1 = (bf16[96,1792]{1,0:T(8,128)(2,1)}, bf16[96,1792]{1,0:T(8,128)(2,1)S(1)}, u32[]{:S(2)}, u32[]{:S(2)}) collective-permute-start(bf16[96,1792]{1,0:T(8,128)(2,1)} %get-tuple-element.36.refs_1_), channel_id=1, source_target_pairs={{0,64},{32,96},{64,128},{96,160},{128,192},{160,224},{192,0},{224,... | collective-permute-start | bytes 1032200 | tf_op jit(solution)/shard_map/ppermute | solution.py:345
  48.7 15.0 %collective-permute-start.3 = (bf16[96,1792]{1,0:T(8,128)(2,1)}, bf16[96,1792]{1,0:T(8,128)(2,1)S(1)}, u32[]{:S(2)}, u32[]{:S(2)}) collective-permute-start(bf16[96,1792]{1,0:T(8,128)(2,1)} %get-tuple-element.36.refs_1_), channel_id=1, source_target_pairs={{0,192},{32,224},{64,0},{96,32},{128,64},{160,96},{192,128},{224,1... | collective-permute-start | bytes 1032200 | tf_op jit(solution)/shard_map/ppermute | solution.py:345
  63.4 9.2 %collective-permute-start.4 = (bf16[96,1792]{1,0:T(8,128)(2,1)S(1)}, bf16[96,1792]{1,0:T(8,128)(2,1)S(1)}, u32[]{:S(2)}, u32[]{:S(2)}) collective-permute-start(bf16[96,1792]{1,0:T(8,128)(2,1)S(1)} %collective-permute-done.refs_2_), channel_id=1, source_target_pairs={{0,64},{32,96},{64,128},{96,160},{128,192},{160,224},{192,0},{224,... | collective-permute-start | bytes 1032200 | tf_op jit(solution)/shard_map/ppermute | solution.py:345
  63.7 9.2 %collective-permute-start.5 = (bf16[96,1792]{1,0:T(8,128)(2,1)S(1)}, bf16[96,1792]{1,0:T(8,128)(2,1)S(1)}, u32[]{:S(2)}, u32[]{:S(2)}) collective-permute-start(bf16[96,1792]{1,0:T(8,128)(2,1)S(1)} %collective-permute-done.3.refs_5_), channel_id=1, source_target_pairs={{0,192},{32,224},{64,0},{96,32},{128,64},{160,96},{192,128},{224,1... | collective-permute-start | bytes 1032200 | tf_op jit(solution)/shard_map/ppermute | solution.py:345
  87.3 11.2 %collective-permute-start.9 = (bf16[96,1792]{1,0:T(8,128)(2,1)}, bf16[96,1792]{1,0:T(8,128)(2,1)S(1)}, u32[]{:S(2)}, u32[]{:S(2)}) collective-permute-start(bf16[96,1792]{1,0:T(8,128)(2,1)} %get-tuple-element.42), channel_id=1, source_target_pairs={{0,64},{32,96},{64,128},{96,160},{128,192},{160,224},{192,0},{224,... | collective-permute-start | bytes 1032200 | tf_op jit(solution)/shard_map/ppermute | solution.py:345
  87.6 11.5 %collective-permute-start.10 = (bf16[96,1792]{1,0:T(8,128)(2,1)}, bf16[96,1792]{1,0:T(8,128)(2,1)S(1)}, u32[]{:S(2)}, u32[]{:S(2)}) collective-permute-start(bf16[96,1792]{1,0:T(8,128)(2,1)} %get-tuple-element.44), channel_id=1, source_target_pairs={{0,192},{32,224},{64,0},{96,32},{128,64},{160,96},{192,128},{224,1... | collective-permute-start | bytes 1032200 | tf_op jit(solution)/shard_map/ppermute | solution.py:345
  93.8 12.4 %collective-permute-start.14 = (bf16[96,1792]{1,0:T(8,128)(2,1)}, bf16[96,1792]{1,0:T(8,128)(2,1)S(1)}, u32[]{:S(2)}, u32[]{:S(2)}) collective-permute-start(bf16[96,1792]{1,0:T(8,128)(2,1)} %get-tuple-element.49.refs_0_), channel_id=1, source_target_pairs={{0,64},{32,96},{64,128},{96,160},{128,192},{160,224},{192,0},{224,... | collective-permute-start | bytes 1032200 | tf_op jit(solution)/shard_map/ppermute | solution.py:345
  93.8 13.9 %collective-permute-start.17 = (bf16[96,1792]{1,0:T(8,128)(2,1)}, bf16[96,1792]{1,0:T(8,128)(2,1)S(1)}, u32[]{:S(2)}, u32[]{:S(2)}) collective-permute-start(bf16[96,1792]{1,0:T(8,128)(2,1)} %get-tuple-element.50.refs_1_), channel_id=1, source_target_pairs={{0,192},{32,224},{64,0},{96,32},{128,64},{160,96},{192,128},{224,1... | collective-permute-start | bytes 1032200 | tf_op jit(solution)/shard_map/ppermute | solution.py:345
  97.0 16.1 %collective-permute-start.8 = (bf16[96,1792]{1,0:T(8,128)(2,1)}, bf16[96,1792]{1,0:T(8,128)(2,1)S(1)}, u32[]{:S(2)}, u32[]{:S(2)}) collective-permute-start(bf16[96,1792]{1,0:T(8,128)(2,1)} %get-tuple-element.40), channel_id=1, source_target_pairs={{0,192},{32,224},{64,0},{96,32},{128,64},{160,96},{192,128},{224,1... | collective-permute-start | bytes 1032200 | tf_op jit(solution)/shard_map/ppermute | solution.py:345
  98.6 18.2 %collective-permute-start.12 = (bf16[96,1792]{1,0:T(8,128)(2,1)}, bf16[96,1792]{1,0:T(8,128)(2,1)S(1)}, u32[]{:S(2)}, u32[]{:S(2)}) collective-permute-start(bf16[96,1792]{1,0:T(8,128)(2,1)} %get-tuple-element.47), channel_id=1, source_target_pairs={{0,64},{32,96},{64,128},{96,160},{128,192},{160,224},{192,0},{224,... | collective-permute-start | bytes 1032200 | tf_op jit(solution)/shard_map/ppermute | solution.py:345
  102.0 18.8 %collective-permute-start.11 = (bf16[96,1792]{1,0:T(8,128)(2,1)}, bf16[96,1792]{1,0:T(8,128)(2,1)S(1)}, u32[]{:S(2)}, u32[]{:S(2)}) collective-permute-start(bf16[96,1792]{1,0:T(8,128)(2,1)} %get-tuple-element.45), channel_id=1, source_target_pairs={{0,64},{32,96},{64,128},{96,160},{128,192},{160,224},{192,0},{224,... | collective-permute-start | bytes 1032200 | tf_op jit(solution)/shard_map/ppermute | solution.py:345
  106.1 16.3 %collective-permute-start.13 = (bf16[96,1792]{1,0:T(8,128)(2,1)}, bf16[96,1792]{1,0:T(8,128)(2,1)S(1)}, u32[]{:S(2)}, u32[]{:S(2)}) collective-permute-start(bf16[96,1792]{1,0:T(8,128)(2,1)} %get-tuple-element.48), channel_id=1, source_target_pairs={{0,192},{32,224},{64,0},{96,32},{128,64},{160,96},{192,128},{224,1... | collective-permute-start | bytes 1032200 | tf_op jit(solution)/shard_map/ppermute | solution.py:345
  107.7 28.5 %collective-permute-start.15 = (bf16[96,1792]{1,0:T(8,128)(2,1)}, bf16[96,1792]{1,0:T(8,128)(2,1)S(1)}, u32[]{:S(2)}, u32[]{:S(2)}) collective-permute-start(bf16[96,1792]{1,0:T(8,128)(2,1)} %get-tuple-element.50.refs_1_), channel_id=1, source_target_pairs={{0,64},{32,96},{64,128},{96,160},{128,192},{160,224},{192,0},{224,... | collective-permute-start | bytes 1032200 | tf_op jit(solution)/shard_map/ppermute | solution.py:345
  113.2 23.0 %collective-permute-start.16 = (bf16[96,1792]{1,0:T(8,128)(2,1)}, bf16[96,1792]{1,0:T(8,128)(2,1)S(1)}, u32[]{:S(2)}, u32[]{:S(2)}) collective-permute-start(bf16[96,1792]{1,0:T(8,128)(2,1)} %get-tuple-element.49.refs_0_), channel_id=1, source_target_pairs={{0,192},{32,224},{64,0},{96,32},{128,64},{160,96},{192,128},{224,1... | collective-permute-start | bytes 1032200 | tf_op jit(solution)/shard_map/ppermute | solution.py:345
  116.8 19.5 %collective-permute-start.18 = (bf16[96,1792]{1,0:T(8,128)(2,1)S(1)}, bf16[96,1792]{1,0:T(8,128)(2,1)S(1)}, u32[]{:S(2)}, u32[]{:S(2)}) collective-permute-start(bf16[96,1792]{1,0:T(8,128)(2,1)S(1)} %collective-permute-done.14.refs_2_), channel_id=1, source_target_pairs={{0,64},{32,96},{64,128},{96,160},{128,192},{160,224},{192,0},{224,... | collective-permute-start | bytes 1032200 | tf_op jit(solution)/shard_map/ppermute | solution.py:345
  120.9 15.4 %collective-permute-start.19 = (bf16[96,1792]{1,0:T(8,128)(2,1)S(1)}, bf16[96,1792]{1,0:T(8,128)(2,1)S(1)}, u32[]{:S(2)}, u32[]{:S(2)}) collective-permute-start(bf16[96,1792]{1,0:T(8,128)(2,1)S(1)} %collective-permute-done.17.refs_5_), channel_id=1, source_target_pairs={{0,192},{32,224},{64,0},{96,32},{128,64},{160,96},{192,128},{224,1... | collective-permute-start | bytes 1032200 | tf_op jit(solution)/shard_map/ppermute | solution.py:345
  126.3 59.1 %all-to-all-start.1 = ((bf16[32,8,1408]{2,1,0:T(8,128)(2,1)}), bf16[32,8,1408]{2,1,0:T(8,128)(2,1)S(1)}, u32[]{:S(2)}, u32[]{:S(2)}) async-start(bf16[32,8,1408]{2,1,0:T(8,128)(2,1)} %bitcast.18), calls=%async_computation.1 | async-start | bytes 1441792 | tf_op jit(solution)/shard_map/all_to_all | solution.py:352
  136.1 82.8 %collective-permute-start.26 = (bf16[384,3584]{1,0:T(8,128)(2,1)}, bf16[384,3584]{1,0:T(8,128)(2,1)}, u32[]{:S(2)}, u32[]{:S(2)}) collective-permute-start(bf16[384,3584]{1,0:T(8,128)(2,1)} %get-tuple-element.64.t_a), channel_id=1, source_target_pairs={{0,32},{32,0},{64,96},{96,64},{128,160},{160,128},{192,224},{224,1... | collective-permute-start | bytes 8257544 | tf_op jit(solution)/shard_map/ppermute | solution.py:348
  145.0 81.4 %collective-permute-start.28 = (bf16[384,3584]{1,0:T(8,128)(2,1)}, bf16[384,3584]{1,0:T(8,128)(2,1)}, u32[]{:S(2)}, u32[]{:S(2)}) collective-permute-start(bf16[384,3584]{1,0:T(8,128)(2,1)} %get-tuple-element.65.g_a), channel_id=1, source_target_pairs={{0,32},{32,0},{64,96},{96,64},{128,160},{160,128},{192,224},{224,1... | collective-permute-start | bytes 8257544 | tf_op jit(solution)/shard_map/ppermute | solution.py:348
  152.1 11.4 %collective-permute-start.21 = (bf16[96,1792]{1,0:T(8,128)(2,1)}, bf16[96,1792]{1,0:T(8,128)(2,1)S(1)}, u32[]{:S(2)}, u32[]{:S(2)}) collective-permute-start(bf16[96,1792]{1,0:T(8,128)(2,1)} %get-tuple-element.57), channel_id=1, source_target_pairs={{0,64},{32,96},{64,128},{96,160},{128,192},{160,224},{192,0},{224,... | collective-permute-start | bytes 1032200 | tf_op jit(solution)/shard_map/ppermute | solution.py:345
  152.5 11.6 %collective-permute-start.22 = (bf16[96,1792]{1,0:T(8,128)(2,1)}, bf16[96,1792]{1,0:T(8,128)(2,1)S(1)}, u32[]{:S(2)}, u32[]{:S(2)}) collective-permute-start(bf16[96,1792]{1,0:T(8,128)(2,1)} %get-tuple-element.59), channel_id=1, source_target_pairs={{0,192},{32,224},{64,0},{96,32},{128,64},{160,96},{192,128},{224,1... | collective-permute-start | bytes 1032200 | tf_op jit(solution)/shard_map/ppermute | solution.py:345
  155.3 14.9 %collective-permute-start.20 = (bf16[96,1792]{1,0:T(8,128)(2,1)}, bf16[96,1792]{1,0:T(8,128)(2,1)S(1)}, u32[]{:S(2)}, u32[]{:S(2)}) collective-permute-start(bf16[96,1792]{1,0:T(8,128)(2,1)} %get-tuple-element.55), channel_id=1, source_target_pairs={{0,192},{32,224},{64,0},{96,32},{128,64},{160,96},{192,128},{224,1... | collective-permute-start | bytes 1032200 | tf_op jit(solution)/shard_map/ppermute | solution.py:345
  163.5 12.4 %collective-permute-start.24 = (bf16[96,1792]{1,0:T(8,128)(2,1)}, bf16[96,1792]{1,0:T(8,128)(2,1)S(1)}, u32[]{:S(2)}, u32[]{:S(2)}) collective-permute-start(bf16[96,1792]{1,0:T(8,128)(2,1)} %get-tuple-element.62), channel_id=1, source_target_pairs={{0,64},{32,96},{64,128},{96,160},{128,192},{160,224},{192,0},{224,... | collective-permute-start | bytes 1032200 | tf_op jit(solution)/shard_map/ppermute | solution.py:345
  167.2 14.3 %collective-permute-start.23 = (bf16[96,1792]{1,0:T(8,128)(2,1)}, bf16[96,1792]{1,0:T(8,128)(2,1)S(1)}, u32[]{:S(2)}, u32[]{:S(2)}) collective-permute-start(bf16[96,1792]{1,0:T(8,128)(2,1)} %get-tuple-element.60), channel_id=1, source_target_pairs={{0,64},{32,96},{64,128},{96,160},{128,192},{160,224},{192,0},{224,... | collective-permute-start | bytes 1032200 | tf_op jit(solution)/shard_map/ppermute | solution.py:345
  170.3 11.2 %collective-permute-start.25 = (bf16[96,1792]{1,0:T(8,128)(2,1)}, bf16[96,1792]{1,0:T(8,128)(2,1)S(1)}, u32[]{:S(2)}, u32[]{:S(2)}) collective-permute-start(bf16[96,1792]{1,0:T(8,128)(2,1)} %get-tuple-element.63), channel_id=1, source_target_pairs={{0,192},{32,224},{64,0},{96,32},{128,64},{160,96},{192,128},{224,1... | collective-permute-start | bytes 1032200 | tf_op jit(solution)/shard_map/ppermute | solution.py:345
  185.4 30.1 %all-to-all-start.3 = ((bf16[32,8,1408]{2,1,0:T(8,128)(2,1)}), bf16[32,8,1408]{2,1,0:T(8,128)(2,1)S(1)}, u32[]{:S(2)}, u32[]{:S(2)}) async-start(bf16[32,8,1408]{2,1,0:T(8,128)(2,1)} %bitcast.19), calls=%async_computation.3 | async-start | bytes 1441792 | tf_op jit(solution)/shard_map/all_to_all | solution.py:352
  195.2 23.7 %collective-permute-start.27 = (bf16[768,384]{1,0:T(8,128)(2,1)S(1)}, bf16[768,384]{1,0:T(8,128)(2,1)S(1)}, u32[]{:S(2)}, u32[]{:S(2)}) collective-permute-start(bf16[768,384]{1,0:T(8,128)(2,1)S(1)} %copy-done.29), channel_id=1, source_target_pairs={{0,32},{32,0},{64,96},{96,64},{128,160},{160,128},{192,224},{224,1... | collective-permute-start | bytes 1769480 | tf_op jit(solution)/shard_map/ppermute | solution.py:348
  (31 other events, 198.7 us)

commit v3 on v2

--- a/solution.py
+++ b/solution.py
@@ -26,117 +26,167 @@
     return pl.CostEstimate(flops=flops, transcendentals=0, bytes_accessed=bytes_accessed)
 
 
-def gather_body(back, split, *refs):
-    refs, pieces = list(refs), []
-    for halves in split:
-        pieces.append([refs.pop(0) for _ in range(halves)])
-    w_own, w_other = refs[:2]
+def layer_body(back, *refs):
+    refs = list(refs)
+    take = lambda n: [refs.pop(0) for _ in range(n)]
+    pieces, (up_own, up_other, down_own, down_other) = take(8), take(4)
     if back:
-        pre, hidden, rows_out, first, second, acc = refs[2:]
+        pre_in, hidden_in = take(2)
+        rows_out, own_out, other_out = take(3)
     else:
-        rows_out, pre_out, first, second, acc = refs[2:]
-    k = pl.program_id(0)
-    size = pieces[0][0].shape[0]
-    for b, piece in enumerate(pieces):
-        for step in range(len(piece)):
-
-            @pl.when((k == step) | (len(piece) == 1))
-            def _():
-                rows_out[b * size : (b + 1) * size, :] = piece[step][...]
-
+        rows_out, pre_out, own_out, other_out = take(4)
+    parts = take(8)
+    rows, up, down, pre, acc, own, other, result, sems = refs
+    size, half = pieces[0].shape
+    count, _ = rows.shape
+    units = up_own.shape[1]
+    used = []
+
+    def copy(source, target):
+        used.append(None)
+        return pltpu.make_async_copy(source, target, sems.at[len(used) - 1])
+
+    def begin(tasks):
+        for task in tasks:
+            task.start()
+
+    def finish(tasks):
+        for task in tasks:
+            task.wait()
+
+    def columns(k):
+        return slice(k * half, (k + 1) * half)
+
+    up_tasks, down_tasks, row_tasks, part_tasks = [], [], [], []
+    for k in range(2):
+        cols = columns(k)
+        up_tasks.append([
+            copy(up_own.at[cols, :], up.at[cols, :units]),
+            copy(up_other.at[cols, :], up.at[cols, units:])])
+        down_tasks.append([
+            copy(down_own.at[:, cols], down.at[:units, cols]),
+            copy(down_other.at[:, cols], down.at[units:, cols])])
+        blocks = [slice(b * size, (b + 1) * size) for b in range(4)]
+        row_tasks.append([
+            copy(pieces[2 * b + k], rows.at[block, cols]) for b, block in enumerate(blocks)])
+        part_tasks.append([
+            copy(result.at[block, cols], parts[2 * b + k]) for b, block in enumerate(blocks)])
+    first_tasks, second_tasks = (down_tasks, up_tasks) if back else (up_tasks, down_tasks)
+    rows_task = copy(rows, rows_out)
+    own_task = copy(own, own_out)
+    other_task = copy(other, other_out.at[count:, :] if back else other_out)
     if back:
-        weight = jnp.concatenate([w_own[...], w_other[...]], axis=0)
-        part = dot(rows_out[...], weight, ((1,), (1,)))
+        extra = [copy(pre_in, pre), copy(hidden_in, other_out.at[:count, :])]
     else:
-        weight = jnp.concatenate([w_own[...], w_other[...]], axis=1)
-        part = dot(rows_out[...], weight)
-
-    @pl.when(k == 0)
-    def _():
-        acc[...] = part
-
-    @pl.when(k > 0)
-    def _():
-        acc[...] += part
-
-    @pl.when(k == pl.num_programs(0) - 1)
-    def _():
-        units = first.shape[1]
+        extra = [copy(acc, pre_out)]
+
+    begin(row_tasks[0] + first_tasks[0] + row_tasks[1] + first_tasks[1])
+    if back:
+        begin(extra)
+
+    def first_half(k, carry):
+        @pl.when(k == 0)
+        def _():
+            finish(row_tasks[0] + first_tasks[0])
+
+        @pl.when(k == 1)
+        def _():
+            finish(row_tasks[1] + first_tasks[1])
+            rows_task.start()
+            begin(second_tasks[0] + second_tasks[1])
+
+        at = pl.ds(pl.multiple_of(k * half, 128), half)
         if back:
-            pre_act = pre[...]
-            squash = jax.nn.sigmoid(pre_act)
-            value = (acc[...] * (squash * (1.0 + pre_act * (1.0 - squash)))).astype(BF16)
+            value = dot(rows[:, at], down[:, at], ((1,), (1,)))
         else:
-            pre_act = acc[...]
-            pre_out[...] = pre_act
-            value = (pre_act * jax.nn.sigmoid(pre_act)).astype(BF16)
-        first[...] = value[:, :units]
+            value = dot(rows[:, at], up[at, :])
+
+        @pl.when(k == 0)
+        def _():
+            acc[...] = value
+
+        @pl.when(k == 1)
+        def _():
+            acc[...] += value
+
+        return carry
+
+    lax.fori_loop(0, 2, first_half, 0)
+    total = acc[...]
+    if back:
+        extra[0].wait()
+        pre_act = pre[...]
+        squash = jax.nn.sigmoid(pre_act)
+        active = (total * (squash * (1.0 + pre_act * (1.0 - squash)))).astype(BF16)
+    else:
+        begin(extra)
+        active = (total * jax.nn.sigmoid(total)).astype(BF16)
+    own[...] = active[:, :units]
+    other[...] = active[:, units:]
+    begin([own_task, other_task])
+
+    def second_half(k, carry):
+        @pl.when(k == 0)
+        def _():
+            finish(second_tasks[0])
+
+        @pl.when(k == 1)
+        def _():
+            finish(second_tasks[1])
+
+        at = pl.ds(pl.multiple_of(k * half, 128), half)
+        both = jnp.concatenate([own[...], other[...]], axis=1)
         if back:
-            count = value.shape[0]
-            second[:count, :] = hidden[...]
-            second[count:, :] = value[:, units:]
+            value = dot(both, up[at, :], ((1,), (1,)))
         else:
-            second[...] = value[:, units:]
-
-
-def rows_matmul(pieces, w_own, w_other, saved, steps):
+            value = dot(both, down[:, at])
+        result[:, at] = value.astype(BF16)
+
+        @pl.when(k == 0)
+        def _():
+            begin(part_tasks[0])
+
+        @pl.when(k == 1)
+        def _():
+            begin(part_tasks[1])
+
+        return carry
+
+    lax.fori_loop(0, 2, second_half, 0)
+    finish([rows_task, own_task, other_task] + (extra[1:] if back else extra))
+    finish(part_tasks[0] + part_tasks[1])
+
+
+def layer_call(pieces, weights, saved):
     back = len(saved) > 0
-    split = tuple(len(piece) for piece in pieces)
-    size, cols = pieces[-1][0].shape
-    rows, width = 4 * size, cols * steps
-    units = w_own.shape[0] if back else w_own.shape[1]
-    whole, half = pl.BlockSpec((size, cols), lambda k: (0, k)), full((size, cols))
-    piece_specs = [half if n > 1 else whole for n in split for _ in range(n)]
-    weight = pl.BlockSpec((units, cols), lambda k: (0, k)) if back else pl.BlockSpec((cols, units), lambda k: (k, 0))
-    wide, narrow = full((rows, 2 * units)), full((rows, units))
-    other_shape = (2 * rows if back else rows, units)
-    small_shapes = [jax.ShapeDtypeStruct(shape, BF16) for shape in ((rows, units), other_shape)]
+    size, half = pieces[0].shape
+    rows, width = 4 * size, 2 * half
+    units = weights[0].shape[1]
+    shape = jax.ShapeDtypeStruct
+    outs = [shape((rows, width), BF16)]
+    if not back:
+        outs.append(shape((rows, 2 * units), F32))
+    outs += [shape((rows, units), BF16), shape((2 * rows if back else rows, units), BF16)]
+    outs += [shape((size, half), BF16)] * 8
+    anywhere = pl.BlockSpec(memory_space=pl.ANY)
     return pl.pallas_call(
-        functools.partial(gather_body, back, split),
-        grid=(steps,),
-        in_specs=piece_specs + [weight, weight] + [wide, narrow] * back,
-        out_specs=[pl.BlockSpec((rows, cols), lambda k: (0, k))] + [wide] * (not back)
-        + [narrow, full(other_shape)],
-        out_shape=[jax.ShapeDtypeStruct((rows, width), BF16)]
-        + [jax.ShapeDtypeStruct((rows, 2 * units), F32)] * (not back) + small_shapes,
-        scratch_shapes=[pltpu.VMEM((rows, 2 * units), F32)],
-        cost_estimate=cost(4 * rows * width * units, 4 * (rows * width + width * units)),
-    )(*[part for piece in pieces for part in piece], w_own, w_other, *saved)
-
-
-def project_body(by_rows, h_own, h_other, w_own, w_other, *outs):
-    hidden = jnp.concatenate([h_own[...], h_other[...]], axis=1)
-    if by_rows:
-        weight = jnp.concatenate([w_own[...], w_other[...]], axis=1)
-        value = dot(hidden, weight, ((1,), (1,))).astype(BF16)
-    else:
-        weight = jnp.concatenate([w_own[...], w_other[...]], axis=0)
-        value = dot(hidden, weight).astype(BF16)
-    size = outs[0].shape[0]
-    for step in range(2):
-
-        @pl.when(pl.program_id(0) == step)
-        def _():
-            for b in range(4):
-                outs[2 * b + step][...] = value[b * size : (b + 1) * size, :]
-
-
-def project(h_own, h_other, w_own, w_other, by_rows, steps, row_block=0):
-    rows, units = h_own.shape
-    width = w_own.shape[0] if by_rows else w_own.shape[1]
-    cols, size = width // steps, rows // 4
-    if by_rows:
-        weight = pl.BlockSpec((cols, units), lambda k: (k, 0))
-    else:
-        weight = pl.BlockSpec((units, cols), lambda k: (0, k))
-    return pl.pallas_call(
-        functools.partial(project_body, by_rows),
-        grid=(steps,),
-        in_specs=[full((rows, units)), pl.BlockSpec((rows, units), lambda k: (row_block, 0)), weight, weight],
-        out_specs=[full((size, cols))] * 8,
-        out_shape=[jax.ShapeDtypeStruct((size, cols), BF16)] * 8,
-        cost_estimate=cost(4 * rows * width * units, 2 * (rows * width + 2 * width * units)),
-    )(h_own, h_other, w_own, w_other)
+        functools.partial(layer_body, back),
+        in_specs=[anywhere] * (12 + len(saved)),
+        out_specs=[anywhere] * len(outs),
+        out_shape=outs,
+        scratch_shapes=[
+            pltpu.VMEM((rows, width), BF16),
+            pltpu.VMEM((width, 2 * units), BF16),
+            pltpu.VMEM((2 * units, width), BF16),
+            pltpu.VMEM((rows, 2 * units), F32),
+            pltpu.VMEM((rows, 2 * units), F32),
+            pltpu.VMEM((rows, units), BF16),
+            pltpu.VMEM((rows, units), BF16),
+            pltpu.VMEM((rows, width), BF16),
+            pltpu.SemaphoreType.DMA((48,)),
+        ],
+        cost_estimate=cost(8 * rows * width * units, 6 * rows * width + 8 * width * units),
+    )(*pieces, *weights, *saved)
 
 
 def down_grad_body(h_a, h_b, g_a, g_b, out):
@@ -359,7 +409,7 @@
         right, left = shift(low, 1), shift(high, -1)
         right_high, left_low = shift(high, 1), shift(low, -1)
         far_low, far_high = shift(right, 1), shift(left, -1)
-        return (low, high), (right, right_high), (left_low, left), (far_low, far_high)
+        return low, high, right, right_high, left_low, left, far_low, far_high
 
     def scatter_x(parts):
         low, high, to_left, to_left_high, to_right, to_right_high, far_low, far_high = parts
@@ -388,13 +438,11 @@
     token_parts = gather_x(*token_own)
     grad_parts = gather_x(*grad_own)
 
-    token_rows, pre_act, h_own, h_other = rows_matmul(
-        token_parts, up_own, up_other, (), STEPS)
-    out_parts = project(h_own, h_other, down_own, down_other, False, STEPS)
-    grad_rows, p_own, both_other = rows_matmul(
-        grad_parts, down_own, down_other, (pre_act, h_other), STEPS)
-
-    in_parts = project(p_own, both_other, up_own, up_other, True, STEPS, 1)
+    weights = up_own, up_other, down_own, down_other
+    token_rows, pre_act, h_own, h_other, *out_parts = layer_call(
+        token_parts, weights, ())
+    grad_rows, p_own, both_other, *in_parts = layer_call(
+        grad_parts, weights, (pre_act, h_other))
 
     out_send = small_call(collect_body, block_shape, *scatter_x(out_parts))
     in_send = small_call(collect_body, block_shape, *scatter_x(in_parts))

time: 234 us -> 230 us (0.983)
  Pallas kernels: 66.3 us -> 60.2 us
  local copies, waits for them, and re-layouts: 10.1 us -> 12.5 us
    pallas_call x4 -> x2, Pallas kernels: 27.6 us -> 21.6 us  [layer_call(): pl.pallas_call(functools.partial(layer_body, back), in_specs=[anywhere] *...]
    all_to_all x4, waiting for transfers between devices: 35.7 us -> 38.6 us  [exchange(): lax.all_to_all(blocks, 'expert', split_axis=0, concat_axis=0, tiled=True)]
    ppermute x24, waiting for transfers between devices: 50.3 us -> 47.7 us  [shift(): return lax.ppermute(value, 'dp', perm)]
    unnamed x62 -> x58, local copies, waits for them, and re-layouts: 10.1 us -> 12.5 us
  transfers between devices with their start and end apart: 33 -> 33, of which waited for: 16 -> 14; matrix products, arithmetic and copies ran while one was open for 1% -> 1% of each run, Pallas kernels for 26% -> 24%
where the time goes in v3:
time: 230 us; the launch traced here: 229 us
  waiting for transfers between devices  86.3 us (38%)
  starting transfers between devices  68.7 us (30%)
  Pallas kernels  60.2 us (26%)
  local copies, waits for them, and re-layouts  12.5 us (5%)
    ppermute x24, waiting for transfers between devices, shift(): return lax.ppermute(value, 'dp', perm)  47.7 us
    all_to_all x4, waiting for transfers between devices, exchange(): lax.all_to_all(blocks, 'expert', split_axis=0, concat_axis=0, tiled=True)  38.6 us
    all_to_all x4, starting transfers between devices, exchange(): lax.all_to_all(blocks, 'expert', split_axis=0, concat_axis=0, tiled=True)  34.8 us
    ppermute x24, starting transfers between devices, shift(): return lax.ppermute(value, 'dp', perm)  33.1 us
    pallas_call x10, Pallas kernels, single(): pl.pallas_call(body, out_shape=[out_shape] * outs if outs else out_shape,...  25.4 us
    pallas_call x2, Pallas kernels, layer_call(): pl.pallas_call(functools.partial(layer_body, back), in_specs=[anywhere] *...  21.6 us
    unnamed x58, local copies, waits for them, and re-layouts  12.5 us
    pallas_call x1, Pallas kernels, up_grad(): pl.pallas_call(up_grad_body, grid=(steps,), in_specs=[t_spec, t_spec, ful...  6.74 us
  transfers between devices with their start and end apart: 33, of which 14 were waited for; matrix products, arithmetic and copies ran while one was open for 1% of the time, Pallas kernels for 24%

profile of v3, /device:TPU:32, one launch (start us, length us, event | category | flops | bytes accessed | tf_op | source)
XLA Modules:
  0.0 228.6 jit_solution(2284247325646818909)
XLA Ops:
  5.0 11.4 %all-to-all-start = ((bf16[32,8,1408]{2,1,0:T(8,128)(2,1)}), bf16[32,8,1408]{2,1,0:T(8,128)(2,1)S(1)}, u32[]{:S(2)}, u32[]{:S(2)}) async-start(bf16[32,8,1408]{2,1,0:T(8,128)(2,1)} %bitcast.17), calls=%async_computation | async-start | bytes 1441792 | tf_op jit(solution)/shard_map/all_to_all | solution.py:402
  17.8 20.6 %all-to-all-done = bf16[32,8,1408]{2,1,0:T(8,128)(2,1)S(1)} async-done(((bf16[32,8,1408]{2,1,0:T(8,128)(2,1)}), bf16[32,8,1408]{2,1,0:T(8,128)(2,1)S(1)}, u32[]{:S(2)}, u32[]{:S(2)}) %all-to-all-start) | async-done | bytes 720928 | tf_op jit(solution)/shard_map/all_to_all | solution.py:402
  45.2 2.5 %shard_map.99 = bf16[256,1408]{1,0:T(8,128)(2,1)} custom-call(s32[32,2]{1,0:T(8,128)} %copy.11.ids, f32[32,2]{1,0:T(8,128)} %copy.12.refs_0_, bf16[32,3584]{1,0:T(8,128)(2,1)} %refs_1_.1), custom_call_target="tpu_custom_call" | custom-call | flops 184549376 | bytes 950784 | tf_op jit(solution)/shard_map/pallas_call | solution.py:378
  47.7 5.0 %all-to-all-start.2 = ((bf16[32,8,1408]{2,1,0:T(8,128)(2,1)}), bf16[32,8,1408]{2,1,0:T(8,128)(2,1)S(1)}, u32[]{:S(2)}, u32[]{:S(2)}) async-start(bf16[32,8,1408]{2,1,0:T(8,128)(2,1)} %bitcast.14), calls=%async_computation.2 | async-start | bytes 1441792 | tf_op jit(solution)/shard_map/all_to_all | solution.py:402
  52.6 5.7 %collective-permute-done.refs_2_ = bf16[96,1792]{1,0:T(8,128)(2,1)} collective-permute-done((bf16[96,1792]{1,0:T(8,128)(2,1)}, bf16[96,1792]{1,0:T(8,128)(2,1)}, u32[]{:S(2)}, u32[]{:S(2)}) %collective-permute-start) | collective-permute-done | bytes 344096 | tf_op jit(solution)/shard_map/ppermute | solution.py:395
  60.4 2.8 %collective-permute-start.5 = (bf16[96,1792]{1,0:T(8,128)(2,1)}, bf16[96,1792]{1,0:T(8,128)(2,1)S(1)}, u32[]{:S(2)}, u32[]{:S(2)}) collective-permute-start(bf16[96,1792]{1,0:T(8,128)(2,1)} %collective-permute-done.3.refs_5_), channel_id=1, source_target_pairs={{0,192},{32,224},{64,0},{96,32},{128,64},{160,96},{192,128},{224,1... | collective-permute-start | bytes 1032200 | tf_op jit(solution)/shard_map/ppermute | solution.py:395
  63.1 6.0 %collective-permute-done.2.refs_4_ = bf16[96,1792]{1,0:T(8,128)(2,1)S(1)} collective-permute-done((bf16[96,1792]{1,0:T(8,128)(2,1)}, bf16[96,1792]{1,0:T(8,128)(2,1)S(1)}, u32[]{:S(2)}, u32[]{:S(2)}) %collective-permute-start.2) | collective-permute-done | bytes 344096 | tf_op jit(solution)/shard_map/ppermute | solution.py:395
  69.2 3.7 %collective-permute-done.5.refs_7_ = bf16[96,1792]{1,0:T(8,128)(2,1)S(1)} collective-permute-done((bf16[96,1792]{1,0:T(8,128)(2,1)}, bf16[96,1792]{1,0:T(8,128)(2,1)S(1)}, u32[]{:S(2)}, u32[]{:S(2)}) %collective-permute-start.5) | collective-permute-done | bytes 344096 | tf_op jit(solution)/shard_map/ppermute | solution.py:395
  75.1 10.9 %shard_map.95 = (bf16[384,3584]{1,0:T(8,128)(2,1)}, f32[384,768]{1,0:T(8,128)}, bf16[384,384]{1,0:T(8,128)(2,1)}, bf16[384,384]{1,0:T(8,128)(2,1)}, bf16[96,1792...) custom-call(bf16[96,1792]{1,0:T(8,128)(2,1)} %get-tuple-element.35.r, ...), custom_call_target="tpu_custom_call" | custom-call | flops 4227858432 | bytes 19267584 | tf_op jit(solution)/shard_map/pallas_call | solution.py:172
  86.4 2.9 %collective-permute-start.10 = (bf16[96,1792]{1,0:T(8,128)(2,1)}, bf16[96,1792]{1,0:T(8,128)(2,1)S(1)}, u32[]{:S(2)}, u32[]{:S(2)}) collective-permute-start(bf16[96,1792]{1,0:T(8,128)(2,1)} %get-tuple-element.42), channel_id=1, source_target_pairs={{0,192},{32,224},{64,0},{96,32},{128,64},{160,96},{192,128},{224,1... | collective-permute-start | bytes 1032200 | tf_op jit(solution)/shard_map/ppermute | solution.py:395
  92.6 3.2 %collective-permute-start.17 = (bf16[96,1792]{1,0:T(8,128)(2,1)}, bf16[96,1792]{1,0:T(8,128)(2,1)S(1)}, u32[]{:S(2)}, u32[]{:S(2)}) collective-permute-start(bf16[96,1792]{1,0:T(8,128)(2,1)} %get-tuple-element.48.refs_1_), channel_id=1, source_target_pairs={{0,192},{32,224},{64,0},{96,32},{128,64},{160,96},{192,128},{224,1... | collective-permute-start | bytes 1032200 | tf_op jit(solution)/shard_map/ppermute | solution.py:395
  102.5 2.5 %collective-permute-done.14.refs_2_ = bf16[96,1792]{1,0:T(8,128)(2,1)S(1)} collective-permute-done((bf16[96,1792]{1,0:T(8,128)(2,1)}, bf16[96,1792]{1,0:T(8,128)(2,1)S(1)}, u32[]{:S(2)}, u32[]{:S(2)}) %collective-permute-start.14) | collective-permute-done | bytes 344096 | tf_op jit(solution)/shard_map/ppermute | solution.py:395
  104.9 2.5 %collective-permute-start.13 = (bf16[96,1792]{1,0:T(8,128)(2,1)}, bf16[96,1792]{1,0:T(8,128)(2,1)S(1)}, u32[]{:S(2)}, u32[]{:S(2)}) collective-permute-start(bf16[96,1792]{1,0:T(8,128)(2,1)} %get-tuple-element.46), channel_id=1, source_target_pairs={{0,192},{32,224},{64,0},{96,32},{128,64},{160,96},{192,128},{224,1... | collective-permute-start | bytes 1032200 | tf_op jit(solution)/shard_map/ppermute | solution.py:395
  107.4 4.5 %collective-permute-done.8.refs_1_ = bf16[96,1792]{1,0:T(8,128)(2,1)S(1)} collective-permute-done((bf16[96,1792]{1,0:T(8,128)(2,1)}, bf16[96,1792]{1,0:T(8,128)(2,1)S(1)}, u32[]{:S(2)}, u32[]{:S(2)}) %collective-permute-start.8) | collective-permute-done | bytes 344096 | tf_op jit(solution)/shard_map/ppermute | solution.py:395
  112.0 3.6 %collective-permute-start.16 = (bf16[96,1792]{1,0:T(8,128)(2,1)}, bf16[96,1792]{1,0:T(8,128)(2,1)S(1)}, u32[]{:S(2)}, u32[]{:S(2)}) collective-permute-start(bf16[96,1792]{1,0:T(8,128)(2,1)} %get-tuple-element.47.refs_0_), channel_id=1, source_target_pairs={{0,192},{32,224},{64,0},{96,32},{128,64},{160,96},{192,128},{224,1... | collective-permute-start | bytes 1032200 | tf_op jit(solution)/shard_map/ppermute | solution.py:395
  115.6 4.1 %collective-permute-done.11.refs_2_ = bf16[96,1792]{1,0:T(8,128)(2,1)S(1)} collective-permute-done((bf16[96,1792]{1,0:T(8,128)(2,1)}, bf16[96,1792]{1,0:T(8,128)(2,1)S(1)}, u32[]{:S(2)}, u32[]{:S(2)}) %collective-permute-start.11) | collective-permute-done | bytes 344096 | tf_op jit(solution)/shard_map/ppermute | solution.py:395
  119.7 2.5 %collective-permute-start.19 = (bf16[96,1792]{1,0:T(8,128)(2,1)S(1)}, bf16[96,1792]{1,0:T(8,128)(2,1)S(1)}, u32[]{:S(2)}, u32[]{:S(2)}) collective-permute-start(bf16[96,1792]{1,0:T(8,128)(2,1)S(1)} %collective-permute-done.17.refs_5_), channel_id=1, source_target_pairs={{0,192},{32,224},{64,0},{96,32},{128,64},{160,96},{192,128},{224,1... | collective-permute-start | bytes 1032200 | tf_op jit(solution)/shard_map/ppermute | solution.py:395
  122.9 3.0 %shard_map.97 = bf16[256,1408]{1,0:T(8,128)(2,1)} custom-call(bf16[96,1792]{1,0:T(8,128)(2,1)} %get-tuple-element.37.refs_0_, bf16[96,1792]{1,0:T(8,128)(2,1)} %copy-done.9, bf16[96,1792]{1,0:T(8,128)(2,1)} %copy-done.11, bf16[96,1792]{1,0:T(8,128)(2,1)} %get-tuple-element.44.refs_3_, bf16[96,1792]{1,0:T(8,128)(2,1)} %copy-done.10, bf16[96,1792]{1,0:T(8,128)(2,1)} %copy-done.13), custom_call_target="tpu_custom_call" | custom-call | flops 184549376 | bytes 2785280 | tf_op jit(solution)/shard_map/pallas_call | solution.py:378
  126.0 8.7 %all-to-all-start.1 = ((bf16[32,8,1408]{2,1,0:T(8,128)(2,1)}), bf16[32,8,1408]{2,1,0:T(8,128)(2,1)S(1)}, u32[]{:S(2)}, u32[]{:S(2)}) async-start(bf16[32,8,1408]{2,1,0:T(8,128)(2,1)} %bitcast.18), calls=%async_computation.1 | async-start | bytes 1441792 | tf_op jit(solution)/shard_map/all_to_all | solution.py:402
  135.9 10.6 %shard_map.101 = (bf16[384,3584]{1,0:T(8,128)(2,1)}, bf16[384,384]{1,0:T(8,128)(2,1)}, bf16[768,384]{1,0:T(8,128)(2,1)}, bf16[96,1792]{1,0:T(8,128)(2,1)}, bf16[...) custom-call(bf16[96,1792]{1,0:T(8,128)(2,1)} %get-tuple-element.47.r, ...), custom_call_target="tpu_custom_call" | custom-call | flops 4227858432 | bytes 19267584 | tf_op jit(solution)/shard_map/pallas_call | solution.py:172
  146.7 3.2 %collective-permute-start.22 = (bf16[96,1792]{1,0:T(8,128)(2,1)}, bf16[96,1792]{1,0:T(8,128)(2,1)S(1)}, u32[]{:S(2)}, u32[]{:S(2)}) collective-permute-start(bf16[96,1792]{1,0:T(8,128)(2,1)} %get-tuple-element.56), channel_id=1, source_target_pairs={{0,192},{32,224},{64,0},{96,32},{128,64},{160,96},{192,128},{224,1... | collective-permute-start | bytes 1032200 | tf_op jit(solution)/shard_map/ppermute | solution.py:395
  150.0 8.5 %collective-permute-done.21.first_via = bf16[96,1792]{1,0:T(8,128)(2,1)S(1)} collective-permute-done((bf16[96,1792]{1,0:T(8,128)(2,1)}, bf16[96,1792]{1,0:T(8,128)(2,1)S(1)}, u32[]{:S(2)}, u32[]{:S(2)}) %collective-permute-start.21) | collective-permute-done | bytes 344096 | tf_op jit(solution)/shard_map/ppermute | solution.py:395
  162.0 3.3 %collective-permute-done.20.refs_1_ = bf16[96,1792]{1,0:T(8,128)(2,1)S(1)} collective-permute-done((bf16[96,1792]{1,0:T(8,128)(2,1)}, bf16[96,1792]{1,0:T(8,128)(2,1)S(1)}, u32[]{:S(2)}, u32[]{:S(2)}) %collective-permute-start.20) | collective-permute-done | bytes 344096 | tf_op jit(solution)/shard_map/ppermute | solution.py:395
  165.2 3.6 %collective-permute-start.25 = (bf16[96,1792]{1,0:T(8,128)(2,1)}, bf16[96,1792]{1,0:T(8,128)(2,1)S(1)}, u32[]{:S(2)}, u32[]{:S(2)}) collective-permute-start(bf16[96,1792]{1,0:T(8,128)(2,1)} %get-tuple-element.60), channel_id=1, source_target_pairs={{0,192},{32,224},{64,0},{96,32},{128,64},{160,96},{192,128},{224,1... | collective-permute-start | bytes 1032200 | tf_op jit(solution)/shard_map/ppermute | solution.py:395
  170.9 6.0 %collective-permute-done.23.refs_2_ = bf16[96,1792]{1,0:T(8,128)(2,1)S(1)} collective-permute-done((bf16[96,1792]{1,0:T(8,128)(2,1)}, bf16[96,1792]{1,0:T(8,128)(2,1)S(1)}, u32[]{:S(2)}, u32[]{:S(2)}) %collective-permute-start.23) | collective-permute-done | bytes 344096 | tf_op jit(solution)/shard_map/ppermute | solution.py:395
  177.7 3.0 %shard_map.103 = bf16[256,1408]{1,0:T(8,128)(2,1)} custom-call(bf16[96,1792]{1,0:T(8,128)(2,1)} %get-tuple-element.51.refs_0_, bf16[96,1792]{1,0:T(8,128)(2,1)} %copy-done.12, bf16[96,1792]{1,0:T(8,128)(2,1)} %copy-done.15, bf16[96,1792]{1,0:T(8,128)(2,1)} %get-tuple-element.58.refs_3_, bf16[96,1792]{1,0:T(8,128)(2,1)} %copy-done.14, bf16[96,1792]{1,0:T(8,128)(2,1)} %copy-done.16), custom_call_target="tpu_custom_call" | custom-call | flops 184549376 | bytes 2785280 | tf_op jit(solution)/shard_map/pallas_call | solution.py:378
  180.7 9.8 %all-to-all-start.3 = ((bf16[32,8,1408]{2,1,0:T(8,128)(2,1)}), bf16[32,8,1408]{2,1,0:T(8,128)(2,1)S(1)}, u32[]{:S(2)}, u32[]{:S(2)}) async-start(bf16[32,8,1408]{2,1,0:T(8,128)(2,1)} %bitcast.19), calls=%async_computation.3 | async-start | bytes 1441792 | tf_op jit(solution)/shard_map/all_to_all | solution.py:402
  190.6 2.6 %shard_map.98 = bf16[32,3584]{1,0:T(8,128)(2,1)} custom-call(s32[32,2]{1,0:T(8,128)} %copy.11.ids, f32[32,2]{1,0:T(8,128)} %copy.12.refs_0_, bf16[256,1408]{1,0:T(8,128)(2,1)} %bitcast.12), custom_call_target="tpu_custom_call" | custom-call | flops 184549376 | bytes 950784 | tf_op jit(solution)/shard_map/pallas_call | solution.py:378
  193.2 18.0 %all-to-all-done.3 = bf16[32,8,1408]{2,1,0:T(8,128)(2,1)S(1)} async-done(((bf16[32,8,1408]{2,1,0:T(8,128)(2,1)}), bf16[32,8,1408]{2,1,0:T(8,128)(2,1)S(1)}, u32[]{:S(2)}, u32[]{:S(2)}) %all-to-all-start.3) | async-done | bytes 720928 | tf_op jit(solution)/shard_map/all_to_all | solution.py:402
  212.1 2.5 %shard_map.104 = bf16[32,3584]{1,0:T(8,128)(2,1)} custom-call(s32[32,2]{1,0:T(8,128)} %copy.11.ids, bf16[256,1408]{1,0:T(8,128)(2,1)} %bitcast.15), custom_call_target="tpu_custom_call" | custom-call | flops 184549376 | bytes 950528 | tf_op jit(solution)/shard_map/pallas_call | solution.py:378
  215.4 6.7 %wgrad_up.1 = bf16[3584,384]{1,0:T(8,128)(2,1)} custom-call(bf16[384,3584]{1,0:T(8,128)(2,1)} %get-tuple-element.61.t_a, bf16[384,3584]{1,0:T(8,128)(2,1)} %collective-permute-done.26.t_b, bf16[384,384]{1,0:T(8,128)(2,1)} %get-tuple-element.62.p_a, bf16[768,384]{1,0:T(8,128)(2,1)} %copy-done.4), custom_call_target="tpu_custom_call" | custom-call | flops 2113929216 | bytes 8257536 | tf_op jit(solution)/shard_map/wgrad_up/pallas_call | solution.py:225
  222.2 6.5 %wgrad_down.1 = bf16[384,3584]{1,0:T(8,128)(2,1)} custom-call(bf16[384,384]{1,0:T(8,128)(2,1)} %get-tuple-element.64.h_a, bf16[768,384]{1,0:T(8,128)(2,1)} %copy-done.4, bf16[384,3584]{1,0:T(8,128)(2,1)} %get-tuple-element.65.g_a, bf16[384,3584]{1,0:T(8,128)(2,1)} %collective-permute-done.28.g_b), custom_call_target="tpu_custom_call" | custom-call | flops 2113929216 | bytes 8257536 | tf_op jit(solution)/shard_map/wgrad_down/pallas_call | solution.py:203
  (106 shorter events, 37.2 us)
Async XLA Ops:
  0.6 72.2 %collective-permute-start.6 = (bf16[3584,384]{1,0:T(8,128)(2,1)}, bf16[3584,384]{1,0:T(8,128)(2,1)S(1)}, u32[]{:S(2)}, u32[]{:S(2)}) collective-permute-start(bf16[3584,384]{1,0:T(8,128)(2,1)} %bitcast.22), channel_id=1, source_target_pairs={{0,32},{32,0},{64,96},{96,64},{128,160},{160,128},{192,224},{224,1... | collective-permute-start | bytes 8257544 | tf_op jit(solution)/shard_map/ppermute | solution.py:398
  0.7 72.9 %collective-permute-start.7 = (bf16[384,3584]{1,0:T(8,128)(2,1)}, bf16[384,3584]{1,0:T(8,128)(2,1)}, u32[]{:S(2)}, u32[]{:S(2)}) collective-permute-start(bf16[384,3584]{1,0:T(8,128)(2,1)} %bitcast.25), channel_id=1, source_target_pairs={{0,32},{32,0},{64,96},{96,64},{128,160},{160,128},{192,224},{224,1... | collective-permute-start | bytes 8257544 | tf_op jit(solution)/shard_map/ppermute | solution.py:398
  5.0 33.4 %all-to-all-start = ((bf16[32,8,1408]{2,1,0:T(8,128)(2,1)}), bf16[32,8,1408]{2,1,0:T(8,128)(2,1)S(1)}, u32[]{:S(2)}, u32[]{:S(2)}) async-start(bf16[32,8,1408]{2,1,0:T(8,128)(2,1)} %bitcast.17), calls=%async_computation | async-start | bytes 1441792 | tf_op jit(solution)/shard_map/all_to_all | solution.py:402
  41.6 18.3 %collective-permute-start.1 = (bf16[96,1792]{1,0:T(8,128)(2,1)}, bf16[96,1792]{1,0:T(8,128)(2,1)}, u32[]{:S(2)}, u32[]{:S(2)}) collective-permute-start(bf16[96,1792]{1,0:T(8,128)(2,1)} %get-tuple-element.36.refs_1_), channel_id=1, source_target_pairs={{0,64},{32,96},{64,128},{96,160},{128,192},{160,224},{192,0},{224,... | collective-permute-start | bytes 1032200 | tf_op jit(solution)/shard_map/ppermute | solution.py:395
  43.1 17.2 %collective-permute-start.3 = (bf16[96,1792]{1,0:T(8,128)(2,1)}, bf16[96,1792]{1,0:T(8,128)(2,1)}, u32[]{:S(2)}, u32[]{:S(2)}) collective-permute-start(bf16[96,1792]{1,0:T(8,128)(2,1)} %get-tuple-element.36.refs_1_), channel_id=1, source_target_pairs={{0,192},{32,224},{64,0},{96,32},{128,64},{160,96},{192,128},{224,1... | collective-permute-start | bytes 1032200 | tf_op jit(solution)/shard_map/ppermute | solution.py:395
  44.9 13.5 %collective-permute-start = (bf16[96,1792]{1,0:T(8,128)(2,1)}, bf16[96,1792]{1,0:T(8,128)(2,1)}, u32[]{:S(2)}, u32[]{:S(2)}) collective-permute-start(bf16[96,1792]{1,0:T(8,128)(2,1)} %get-tuple-element.35.refs_0_), channel_id=1, source_target_pairs={{0,64},{32,96},{64,128},{96,160},{128,192},{160,224},{192,0},{224,... | collective-permute-start | bytes 1032200 | tf_op jit(solution)/shard_map/ppermute | solution.py:395
  47.7 41.7 %all-to-all-start.2 = ((bf16[32,8,1408]{2,1,0:T(8,128)(2,1)}), bf16[32,8,1408]{2,1,0:T(8,128)(2,1)S(1)}, u32[]{:S(2)}, u32[]{:S(2)}) async-start(bf16[32,8,1408]{2,1,0:T(8,128)(2,1)} %bitcast.14), calls=%async_computation.2 | async-start | bytes 1441792 | tf_op jit(solution)/shard_map/all_to_all | solution.py:402
  58.3 10.8 %collective-permute-start.2 = (bf16[96,1792]{1,0:T(8,128)(2,1)}, bf16[96,1792]{1,0:T(8,128)(2,1)S(1)}, u32[]{:S(2)}, u32[]{:S(2)}) collective-permute-start(bf16[96,1792]{1,0:T(8,128)(2,1)} %get-tuple-element.35.refs_0_), channel_id=1, source_target_pairs={{0,192},{32,224},{64,0},{96,32},{128,64},{160,96},{192,128},{224,1... | collective-permute-start | bytes 1032200 | tf_op jit(solution)/shard_map/ppermute | solution.py:395
  60.4 12.5 %collective-permute-start.5 = (bf16[96,1792]{1,0:T(8,128)(2,1)}, bf16[96,1792]{1,0:T(8,128)(2,1)S(1)}, u32[]{:S(2)}, u32[]{:S(2)}) collective-permute-start(bf16[96,1792]{1,0:T(8,128)(2,1)} %collective-permute-done.3.refs_5_), channel_id=1, source_target_pairs={{0,192},{32,224},{64,0},{96,32},{128,64},{160,96},{192,128},{224,1... | collective-permute-start | bytes 1032200 | tf_op jit(solution)/shard_map/ppermute | solution.py:395
  86.0 11.3 %collective-permute-start.9 = (bf16[96,1792]{1,0:T(8,128)(2,1)}, bf16[96,1792]{1,0:T(8,128)(2,1)S(1)}, u32[]{:S(2)}, u32[]{:S(2)}) collective-permute-start(bf16[96,1792]{1,0:T(8,128)(2,1)} %get-tuple-element.40), channel_id=1, source_target_pairs={{0,64},{32,96},{64,128},{96,160},{128,192},{160,224},{192,0},{224,... | collective-permute-start | bytes 1032200 | tf_op jit(solution)/shard_map/ppermute | solution.py:395
  86.4 11.5 %collective-permute-start.10 = (bf16[96,1792]{1,0:T(8,128)(2,1)}, bf16[96,1792]{1,0:T(8,128)(2,1)S(1)}, u32[]{:S(2)}, u32[]{:S(2)}) collective-permute-start(bf16[96,1792]{1,0:T(8,128)(2,1)} %get-tuple-element.42), channel_id=1, source_target_pairs={{0,192},{32,224},{64,0},{96,32},{128,64},{160,96},{192,128},{224,1... | collective-permute-start | bytes 1032200 | tf_op jit(solution)/shard_map/ppermute | solution.py:395
  92.6 12.4 %collective-permute-start.14 = (bf16[96,1792]{1,0:T(8,128)(2,1)}, bf16[96,1792]{1,0:T(8,128)(2,1)S(1)}, u32[]{:S(2)}, u32[]{:S(2)}) collective-permute-start(bf16[96,1792]{1,0:T(8,128)(2,1)} %get-tuple-element.47.refs_0_), channel_id=1, source_target_pairs={{0,64},{32,96},{64,128},{96,160},{128,192},{160,224},{192,0},{224,... | collective-permute-start | bytes 1032200 | tf_op jit(solution)/shard_map/ppermute | solution.py:395
  92.6 14.8 %collective-permute-start.17 = (bf16[96,1792]{1,0:T(8,128)(2,1)}, bf16[96,1792]{1,0:T(8,128)(2,1)S(1)}, u32[]{:S(2)}, u32[]{:S(2)}) collective-permute-start(bf16[96,1792]{1,0:T(8,128)(2,1)} %get-tuple-element.48.refs_1_), channel_id=1, source_target_pairs={{0,192},{32,224},{64,0},{96,32},{128,64},{160,96},{192,128},{224,1... | collective-permute-start | bytes 1032200 | tf_op jit(solution)/shard_map/ppermute | solution.py:395
  95.8 16.2 %collective-permute-start.8 = (bf16[96,1792]{1,0:T(8,128)(2,1)}, bf16[96,1792]{1,0:T(8,128)(2,1)S(1)}, u32[]{:S(2)}, u32[]{:S(2)}) collective-permute-start(bf16[96,1792]{1,0:T(8,128)(2,1)} %get-tuple-element.38), channel_id=1, source_target_pairs={{0,192},{32,224},{64,0},{96,32},{128,64},{160,96},{192,128},{224,1... | collective-permute-start | bytes 1032200 | tf_op jit(solution)/shard_map/ppermute | solution.py:395
  97.3 18.3 %collective-permute-start.12 = (bf16[96,1792]{1,0:T(8,128)(2,1)}, bf16[96,1792]{1,0:T(8,128)(2,1)S(1)}, u32[]{:S(2)}, u32[]{:S(2)}) collective-permute-start(bf16[96,1792]{1,0:T(8,128)(2,1)} %get-tuple-element.45), channel_id=1, source_target_pairs={{0,64},{32,96},{64,128},{96,160},{128,192},{160,224},{192,0},{224,... | collective-permute-start | bytes 1032200 | tf_op jit(solution)/shard_map/ppermute | solution.py:395
  100.9 18.8 %collective-permute-start.11 = (bf16[96,1792]{1,0:T(8,128)(2,1)}, bf16[96,1792]{1,0:T(8,128)(2,1)S(1)}, u32[]{:S(2)}, u32[]{:S(2)}) collective-permute-start(bf16[96,1792]{1,0:T(8,128)(2,1)} %get-tuple-element.43), channel_id=1, source_target_pairs={{0,64},{32,96},{64,128},{96,160},{128,192},{160,224},{192,0},{224,... | collective-permute-start | bytes 1032200 | tf_op jit(solution)/shard_map/ppermute | solution.py:395
  104.9 17.2 %collective-permute-start.13 = (bf16[96,1792]{1,0:T(8,128)(2,1)}, bf16[96,1792]{1,0:T(8,128)(2,1)S(1)}, u32[]{:S(2)}, u32[]{:S(2)}) collective-permute-start(bf16[96,1792]{1,0:T(8,128)(2,1)} %get-tuple-element.46), channel_id=1, source_target_pairs={{0,192},{32,224},{64,0},{96,32},{128,64},{160,96},{192,128},{224,1... | collective-permute-start | bytes 1032200 | tf_op jit(solution)/shard_map/ppermute | solution.py:395
  107.4 27.3 %collective-permute-start.15 = (bf16[96,1792]{1,0:T(8,128)(2,1)}, bf16[96,1792]{1,0:T(8,128)(2,1)S(1)}, u32[]{:S(2)}, u32[]{:S(2)}) collective-permute-start(bf16[96,1792]{1,0:T(8,128)(2,1)} %get-tuple-element.48.refs_1_), channel_id=1, source_target_pairs={{0,64},{32,96},{64,128},{96,160},{128,192},{160,224},{192,0},{224,... | collective-permute-start | bytes 1032200 | tf_op jit(solution)/shard_map/ppermute | solution.py:395
  112.0 22.8 %collective-permute-start.16 = (bf16[96,1792]{1,0:T(8,128)(2,1)}, bf16[96,1792]{1,0:T(8,128)(2,1)S(1)}, u32[]{:S(2)}, u32[]{:S(2)}) collective-permute-start(bf16[96,1792]{1,0:T(8,128)(2,1)} %get-tuple-element.47.refs_0_), channel_id=1, source_target_pairs={{0,192},{32,224},{64,0},{96,32},{128,64},{160,96},{192,128},{224,1... | collective-permute-start | bytes 1032200 | tf_op jit(solution)/shard_map/ppermute | solution.py:395
  115.6 19.2 %collective-permute-start.18 = (bf16[96,1792]{1,0:T(8,128)(2,1)S(1)}, bf16[96,1792]{1,0:T(8,128)(2,1)S(1)}, u32[]{:S(2)}, u32[]{:S(2)}) collective-permute-start(bf16[96,1792]{1,0:T(8,128)(2,1)S(1)} %collective-permute-done.14.refs_2_), channel_id=1, source_target_pairs={{0,64},{32,96},{64,128},{96,160},{128,192},{160,224},{192,0},{224,... | collective-permute-start | bytes 1032200 | tf_op jit(solution)/shard_map/ppermute | solution.py:395
  119.7 15.1 %collective-permute-start.19 = (bf16[96,1792]{1,0:T(8,128)(2,1)S(1)}, bf16[96,1792]{1,0:T(8,128)(2,1)S(1)}, u32[]{:S(2)}, u32[]{:S(2)}) collective-permute-start(bf16[96,1792]{1,0:T(8,128)(2,1)S(1)} %collective-permute-done.17.refs_5_), channel_id=1, source_target_pairs={{0,192},{32,224},{64,0},{96,32},{128,64},{160,96},{192,128},{224,1... | collective-permute-start | bytes 1032200 | tf_op jit(solution)/shard_map/ppermute | solution.py:395
  122.2 92.4 %collective-permute-start.26 = (bf16[384,3584]{1,0:T(8,128)(2,1)}, bf16[384,3584]{1,0:T(8,128)(2,1)}, u32[]{:S(2)}, u32[]{:S(2)}) collective-permute-start(bf16[384,3584]{1,0:T(8,128)(2,1)} %get-tuple-element.61.t_a), channel_id=1, source_target_pairs={{0,32},{32,0},{64,96},{96,64},{128,160},{160,128},{192,224},{224,1... | collective-permute-start | bytes 8257544 | tf_op jit(solution)/shard_map/ppermute | solution.py:398
  126.0 54.8 %all-to-all-start.1 = ((bf16[32,8,1408]{2,1,0:T(8,128)(2,1)}), bf16[32,8,1408]{2,1,0:T(8,128)(2,1)S(1)}, u32[]{:S(2)}, u32[]{:S(2)}) async-start(bf16[32,8,1408]{2,1,0:T(8,128)(2,1)} %bitcast.18), calls=%async_computation.1 | async-start | bytes 1441792 | tf_op jit(solution)/shard_map/all_to_all | solution.py:402
  146.5 75.7 %collective-permute-start.28 = (bf16[384,3584]{1,0:T(8,128)(2,1)}, bf16[384,3584]{1,0:T(8,128)(2,1)}, u32[]{:S(2)}, u32[]{:S(2)}) collective-permute-start(bf16[384,3584]{1,0:T(8,128)(2,1)} %get-tuple-element.65.g_a), channel_id=1, source_target_pairs={{0,32},{32,0},{64,96},{96,64},{128,160},{160,128},{192,224},{224,1... | collective-permute-start | bytes 8257544 | tf_op jit(solution)/shard_map/ppermute | solution.py:398
  146.6 11.9 %collective-permute-start.21 = (bf16[96,1792]{1,0:T(8,128)(2,1)}, bf16[96,1792]{1,0:T(8,128)(2,1)S(1)}, u32[]{:S(2)}, u32[]{:S(2)}) collective-permute-start(bf16[96,1792]{1,0:T(8,128)(2,1)} %get-tuple-element.54), channel_id=1, source_target_pairs={{0,64},{32,96},{64,128},{96,160},{128,192},{160,224},{192,0},{224,... | collective-permute-start | bytes 1032200 | tf_op jit(solution)/shard_map/ppermute | solution.py:395
  146.7 12.0 %collective-permute-start.22 = (bf16[96,1792]{1,0:T(8,128)(2,1)}, bf16[96,1792]{1,0:T(8,128)(2,1)S(1)}, u32[]{:S(2)}, u32[]{:S(2)}) collective-permute-start(bf16[96,1792]{1,0:T(8,128)(2,1)} %get-tuple-element.56), channel_id=1, source_target_pairs={{0,192},{32,224},{64,0},{96,32},{128,64},{160,96},{192,128},{224,1... | collective-permute-start | bytes 1032200 | tf_op jit(solution)/shard_map/ppermute | solution.py:395
  149.9 15.3 %collective-permute-start.20 = (bf16[96,1792]{1,0:T(8,128)(2,1)}, bf16[96,1792]{1,0:T(8,128)(2,1)S(1)}, u32[]{:S(2)}, u32[]{:S(2)}) collective-permute-start(bf16[96,1792]{1,0:T(8,128)(2,1)} %get-tuple-element.52), channel_id=1, source_target_pairs={{0,192},{32,224},{64,0},{96,32},{128,64},{160,96},{192,128},{224,1... | collective-permute-start | bytes 1032200 | tf_op jit(solution)/shard_map/ppermute | solution.py:395
  158.5 12.4 %collective-permute-start.24 = (bf16[96,1792]{1,0:T(8,128)(2,1)}, bf16[96,1792]{1,0:T(8,128)(2,1)S(1)}, u32[]{:S(2)}, u32[]{:S(2)}) collective-permute-start(bf16[96,1792]{1,0:T(8,128)(2,1)} %get-tuple-element.59), channel_id=1, source_target_pairs={{0,64},{32,96},{64,128},{96,160},{128,192},{160,224},{192,0},{224,... | collective-permute-start | bytes 1032200 | tf_op jit(solution)/shard_map/ppermute | solution.py:395
  161.7 15.1 %collective-permute-start.23 = (bf16[96,1792]{1,0:T(8,128)(2,1)}, bf16[96,1792]{1,0:T(8,128)(2,1)S(1)}, u32[]{:S(2)}, u32[]{:S(2)}) collective-permute-start(bf16[96,1792]{1,0:T(8,128)(2,1)} %get-tuple-element.57), channel_id=1, source_target_pairs={{0,64},{32,96},{64,128},{96,160},{128,192},{160,224},{192,0},{224,... | collective-permute-start | bytes 1032200 | tf_op jit(solution)/shard_map/ppermute | solution.py:395
  165.2 11.6 %collective-permute-start.25 = (bf16[96,1792]{1,0:T(8,128)(2,1)}, bf16[96,1792]{1,0:T(8,128)(2,1)S(1)}, u32[]{:S(2)}, u32[]{:S(2)}) collective-permute-start(bf16[96,1792]{1,0:T(8,128)(2,1)} %get-tuple-element.60), channel_id=1, source_target_pairs={{0,192},{32,224},{64,0},{96,32},{128,64},{160,96},{192,128},{224,1... | collective-permute-start | bytes 1032200 | tf_op jit(solution)/shard_map/ppermute | solution.py:395
  180.7 30.5 %all-to-all-start.3 = ((bf16[32,8,1408]{2,1,0:T(8,128)(2,1)}), bf16[32,8,1408]{2,1,0:T(8,128)(2,1)S(1)}, u32[]{:S(2)}, u32[]{:S(2)}) async-start(bf16[32,8,1408]{2,1,0:T(8,128)(2,1)} %bitcast.19), calls=%async_computation.3 | async-start | bytes 1441792 | tf_op jit(solution)/shard_map/all_to_all | solution.py:402
  190.5 24.1 %collective-permute-start.27 = (bf16[768,384]{1,0:T(8,128)(2,1)S(1)}, bf16[768,384]{1,0:T(8,128)(2,1)S(1)}, u32[]{:S(2)}, u32[]{:S(2)}) collective-permute-start(bf16[768,384]{1,0:T(8,128)(2,1)S(1)} %copy-done.18), channel_id=1, source_target_pairs={{0,32},{32,0},{64,96},{96,64},{128,160},{160,128},{192,224},{224,1... | collective-permute-start | bytes 1769480 | tf_op jit(solution)/shard_map/ppermute | solution.py:398
  (29 other events, 166.4 us)

commit v4 on v3

--- a/solution.py
+++ b/solution.py
@@ -185,6 +185,7 @@
             pltpu.VMEM((rows, width), BF16),
             pltpu.SemaphoreType.DMA((48,)),
         ],
+        compiler_params=pltpu.CompilerParams(vmem_limit_bytes=28 * 2**20),
         cost_estimate=cost(8 * rows * width * units, 6 * rows * width + 8 * width * units),
     )(*pieces, *weights, *saved)
 
@@ -206,6 +207,7 @@
         in_specs=[full((rows, units))] * 2 + [g_spec, g_spec],
         out_specs=pl.BlockSpec((units, cols), lambda k: (0, k)),
         out_shape=jax.ShapeDtypeStruct((units, width), BF16),
+        compiler_params=pltpu.CompilerParams(vmem_limit_bytes=12 * 2**20),
         cost_estimate=cost(4 * rows * width * units, 2 * (2 * rows * width + width * units)),
         name="wgrad_down",
     )(h_a, h_b, g_a, g_b)
@@ -228,6 +230,7 @@
         in_specs=[t_spec, t_spec, full((rows, units)), pl.BlockSpec((rows, units), lambda k: (1, 0))],
         out_specs=pl.BlockSpec((cols, units), lambda k: (k, 0)),
         out_shape=jax.ShapeDtypeStruct((width, units), BF16),
+        compiler_params=pltpu.CompilerParams(vmem_limit_bytes=12 * 2**20),
         cost_estimate=cost(4 * rows * width * units, 2 * (2 * rows * width + width * units)),
         name="wgrad_up",
     )(t_a, t_b, p_a, p_b)
@@ -291,17 +294,24 @@
     )
 
 
+def to_rows(by_lane):
+    count = by_lane.shape[1]
+    first = lax.broadcasted_iota(I32, (count, count), 0)
+    second = lax.broadcasted_iota(I32, (count, count), 1)
+    wide = jnp.broadcast_to(by_lane, (count, count))
+    return jnp.sum(jnp.where(first == second, wide, 0.0), axis=1, keepdims=True)
+
+
 def pair_slots(ids):
-    by_row = jnp.concatenate([ids[:, 0:1], ids[:, 1:2]], axis=0)
+    by_lane = jnp.concatenate([ids[0:1, :], ids[1:2, :]], axis=1).astype(F32)
+    by_row = to_rows(by_lane)
     count = by_row.shape[0]
     first = lax.broadcasted_iota(I32, (count, count), 0)
     second = lax.broadcasted_iota(I32, (count, count), 1)
-    wide = jnp.broadcast_to(by_row.astype(F32), (count, count))
-    by_lane = jnp.sum(jnp.where(first == second, wide, 0.0), axis=0, keepdims=True)
-    same = wide == by_lane
+    same = by_row == by_lane
     along_lane = jnp.sum((same & (first < second)).astype(F32), axis=0, keepdims=True)
     along_row = jnp.sum((same & (second < first)).astype(F32), axis=1, keepdims=True)
-    return by_lane.astype(I32), along_lane.astype(I32), by_row, along_row.astype(I32)
+    return tuple(v.astype(I32) for v in (by_lane, along_lane, by_row, along_row))
 
 
 def dispatch_body(scaled, ids, *refs):
@@ -313,7 +323,7 @@
     if scaled:
         source = source.astype(F32)
         mix = refs[0][...]
-        pairs = [(mix[:, k : k + 1] * source).astype(BF16) for k in range(2)]
+        pairs = [(to_rows(mix[k : k + 1, :]) * source).astype(BF16) for k in range(2)]
     else:
         pairs = [source, source]
     write_blocks(out, place, jnp.concatenate(pairs, axis=0))
@@ -359,9 +369,10 @@
     count = out.shape[0]
     if weighted:
         mix = refs[0][...]
+        first_mix, second_mix = to_rows(mix[0:1, :]), to_rows(mix[1:2, :])
         split = []
         for p in place:
-            weight = p[:count].astype(F32) * mix[:, 0:1] + p[count:].astype(F32) * mix[:, 1:2]
+            weight = p[:count].astype(F32) * first_mix + p[count:].astype(F32) * second_mix
             pieces = []
             for _ in range(3):
                 pieces.append(weight.astype(BF16))
@@ -376,7 +387,11 @@
     moved = sum(a.size * a.dtype.itemsize for a in args) + 2 * shape[0] * shape[1] * (outs or 1)
     out_shape = jax.ShapeDtypeStruct(shape, BF16)
     return pl.pallas_call(
-        body, out_shape=[out_shape] * outs if outs else out_shape, cost_estimate=cost(flops, moved)
+        body,
+        in_specs=[pl.BlockSpec(memory_space=pltpu.VMEM)] * len(args),
+        out_shape=[out_shape] * outs if outs else out_shape,
+        compiler_params=pltpu.CompilerParams(vmem_limit_bytes=12 * 2**20),
+        cost_estimate=cost(flops, moved),
     )(*args)
 
 
@@ -423,13 +438,14 @@
         return low, low_in, low_other, high, high_in, high_other
 
     up_own, down_own = w_up[0], w_down[0]
+    ids, mix = expert_ids.T, mix_weights.T
 
     token_send = small_call(
-        functools.partial(dispatch_body, False), block_shape, expert_ids, tokens)
+        functools.partial(dispatch_body, False), block_shape, ids, tokens)
     token_moved = exchange(token_send)
     grad_send = small_call(
         functools.partial(dispatch_body, True), block_shape,
-        expert_ids, mix_weights, out_grad)
+        ids, mix, out_grad)
     grad_moved = exchange(grad_send)
 
     up_other, down_other = swap(up_own), swap(down_own)
@@ -456,10 +472,10 @@
 
     layer_out = small_call(
         functools.partial(combine_body, True), (tok_count, width),
-        expert_ids, mix_weights, out_back)
+        ids, mix, out_back)
     token_grad = small_call(
         functools.partial(combine_body, False), (tok_count, width),
-        expert_ids, in_back)
+        ids, in_back)
     return layer_out, token_grad, grad_up[None], grad_down[None]
 
 

time: 230 us -> 225 us (0.978)
  blocking collectives: 0 us -> 33.2 us
  Pallas kernels: 60.2 us -> 40.8 us
  starting transfers between devices: 68.7 us -> 55.8 us
  waiting for transfers between devices: 86.3 us -> 74.8 us
  local copies, waits for them, and re-layouts: 12.5 us -> 18.6 us
    all_to_all x0 -> x1, blocking collectives: none -> 33.2 us  [exchange(): lax.all_to_all(blocks, 'expert', split_axis=0, concat_axis=0, tiled=True)]
    all_to_all x4 -> x3, waiting for transfers between devices: 38.6 us -> 19.2 us  [exchange(): lax.all_to_all(blocks, 'expert', split_axis=0, concat_axis=0, tiled=True)]
    pallas_call x10, Pallas kernels: 25.4 us -> 10.1 us  [single(): pl.pallas_call(body, in_specs=[pl.BlockSpec(memory_space=pltpu.VMEM)] * l...]
    all_to_all x4 -> x3, starting transfers between devices: 34.8 us -> 23.5 us  [exchange(): lax.all_to_all(blocks, 'expert', split_axis=0, concat_axis=0, tiled=True)]
    ppermute x24, waiting for transfers between devices: 47.7 us -> 55.6 us  [shift(): return lax.ppermute(value, 'dp', perm)]
    unnamed x58 -> x42, local copies, waits for them, and re-layouts: 12.5 us -> 18.6 us
    pallas_call x2, Pallas kernels: 21.6 us -> 17.8 us  [layer_call(): pl.pallas_call(functools.partial(layer_body, back), in_specs=[anywhere] *...]
  transfers between devices with their start and end apart: 33 -> 32, of which waited for: 14 -> 13; matrix products, arithmetic and copies ran while one was open for 1% -> 0% of each run, Pallas kernels for 24% -> 15%
where the time goes in v4:
time: 225 us; the launch traced here: 224 us
  waiting for transfers between devices  74.8 us (33%)
  starting transfers between devices  55.8 us (25%)
  Pallas kernels  40.8 us (18%)
  blocking collectives  33.2 us (15%)
  local copies, waits for them, and re-layouts  18.6 us (8%)
    ppermute x24, waiting for transfers between devices, shift(): return lax.ppermute(value, 'dp', perm)  55.6 us
    all_to_all x1, blocking collectives, exchange(): lax.all_to_all(blocks, 'expert', split_axis=0, concat_axis=0, tiled=True)  33.2 us
    ppermute x24, starting transfers between devices, shift(): return lax.ppermute(value, 'dp', perm)  31.5 us
    all_to_all x3, starting transfers between devices, exchange(): lax.all_to_all(blocks, 'expert', split_axis=0, concat_axis=0, tiled=True)  23.5 us
    all_to_all x3, waiting for transfers between devices, exchange(): lax.all_to_all(blocks, 'expert', split_axis=0, concat_axis=0, tiled=True)  19.2 us
    unnamed x42, local copies, waits for them, and re-layouts  18.6 us
    pallas_call x2, Pallas kernels, layer_call(): pl.pallas_call(functools.partial(layer_body, back), in_specs=[anywhere] *...  17.8 us
    pallas_call x10, Pallas kernels, single(): pl.pallas_call(body, in_specs=[pl.BlockSpec(memory_space=pltpu.VMEM)] * l...  10.1 us
  transfers between devices with their start and end apart: 32, of which 13 were waited for; matrix products, arithmetic and copies ran while one was open for 0% of the time, Pallas kernels for 15%

profile of v4, /device:TPU:32, one launch (start us, length us, event | category | flops | bytes accessed | tf_op | source)
XLA Modules:
  0.0 224.0 jit_solution(800931822270503389)
XLA Ops:
  3.5 33.2 %all_to_all.20 = bf16[32,8,1408]{2,1,0:T(8,128)(2,1)S(1)} all-to-all(bf16[32,8,1408]{2,1,0:T(8,128)(2,1)S(1)} %bitcast.17), channel_id=1, replica_groups=mesh['dp'=8,'expert'=32] {'expert'}, dimensions={0} | all-to-all | bytes 1441792 | tf_op jit(solution)/shard_map/all_to_all | solution.py:417
  38.7 1.7 collective-permute-start.3
  42.3 4.9 %all-to-all-start.2 = ((bf16[32,8,1408]{2,1,0:T(8,128)(2,1)}), bf16[32,8,1408]{2,1,0:T(8,128)(2,1)S(1)}, u32[]{:S(2)}, u32[]{:S(2)}) async-start(bf16[32,8,1408]{2,1,0:T(8,128)(2,1)} %bitcast.8), calls=%async_computation.2 | async-start | bytes 1441792 | tf_op jit(solution)/shard_map/all_to_all | solution.py:417
  47.2 6.4 %collective-permute-done.refs_2_ = bf16[96,1792]{1,0:T(8,128)(2,1)S(1)} collective-permute-done((bf16[96,1792]{1,0:T(8,128)(2,1)S(1)}, bf16[96,1792]{1,0:T(8,128)(2,1)S(1)}, u32[]{:S(2)}, u32[]{:S(2)}) %collective-permute-start) | collective-permute-done | bytes 344096 | tf_op jit(solution)/shard_map/ppermute | solution.py:410
  56.4 2.7 %collective-permute-start.5 = (bf16[96,1792]{1,0:T(8,128)(2,1)S(1)}, bf16[96,1792]{1,0:T(8,128)(2,1)S(1)}, u32[]{:S(2)}, u32[]{:S(2)}) collective-permute-start(bf16[96,1792]{1,0:T(8,128)(2,1)S(1)} %collective-permute-done.3.refs_5_), channel_id=1, source_target_pairs={{0,192},{32,224},{64,0},{96,32},{128,64},{160,96},{192,128},{224,1... | collective-permute-start | bytes 1032200 | tf_op jit(solution)/shard_map/ppermute | solution.py:410
  59.9 4.4 %collective-permute-done.2.refs_4_ = bf16[96,1792]{1,0:T(8,128)(2,1)S(1)} collective-permute-done((bf16[96,1792]{1,0:T(8,128)(2,1)S(1)}, bf16[96,1792]{1,0:T(8,128)(2,1)S(1)}, u32[]{:S(2)}, u32[]{:S(2)}) %collective-permute-start.2) | collective-permute-done | bytes 344096 | tf_op jit(solution)/shard_map/ppermute | solution.py:410
  64.3 3.7 %collective-permute-done.5.refs_7_ = bf16[96,1792]{1,0:T(8,128)(2,1)S(1)} collective-permute-done((bf16[96,1792]{1,0:T(8,128)(2,1)S(1)}, bf16[96,1792]{1,0:T(8,128)(2,1)S(1)}, u32[]{:S(2)}, u32[]{:S(2)}) %collective-permute-start.5) | collective-permute-done | bytes 344096 | tf_op jit(solution)/shard_map/ppermute | solution.py:410
  68.0 1.8 copy-done.5
  69.7 1.8 copy-done.7
  73.5 9.2 %shard_map.95 = (bf16[384,3584]{1,0:T(8,128)(2,1)}, f32[384,768]{1,0:T(8,128)S(1)}, bf16[384,384]{1,0:T(8,128)(2,1)S(1)}, bf16[384,384]{1,0:T(8,128)(2,1)S(1)}, ...) custom-call(bf16[96,1792]{1,0:T(8,128)(2,1)S(1)} %get-tuple-element., ...), custom_call_target="tpu_custom_call" | custom-call | flops 4227858432 | bytes 19267584 | tf_op jit(solution)/shard_map/pallas_call | solution.py:172
  86.2 3.0 %collective-permute-start.10 = (bf16[96,1792]{1,0:T(8,128)(2,1)}, bf16[96,1792]{1,0:T(8,128)(2,1)S(1)}, u32[]{:S(2)}, u32[]{:S(2)}) collective-permute-start(bf16[96,1792]{1,0:T(8,128)(2,1)} %get-tuple-element.42), channel_id=1, source_target_pairs={{0,192},{32,224},{64,0},{96,32},{128,64},{160,96},{192,128},{224,1... | collective-permute-start | bytes 1032200 | tf_op jit(solution)/shard_map/ppermute | solution.py:410
  90.5 3.2 %collective-permute-start.17 = (bf16[96,1792]{1,0:T(8,128)(2,1)}, bf16[96,1792]{1,0:T(8,128)(2,1)}, u32[]{:S(2)}, u32[]{:S(2)}) collective-permute-start(bf16[96,1792]{1,0:T(8,128)(2,1)} %get-tuple-element.48.refs_1_), channel_id=1, source_target_pairs={{0,192},{32,224},{64,0},{96,32},{128,64},{160,96},{192,128},{224,1... | collective-permute-start | bytes 1032200 | tf_op jit(solution)/shard_map/ppermute | solution.py:410
  94.0 4.3 %collective-permute-done.9.first_via = bf16[96,1792]{1,0:T(8,128)(2,1)S(1)} collective-permute-done((bf16[96,1792]{1,0:T(8,128)(2,1)}, bf16[96,1792]{1,0:T(8,128)(2,1)S(1)}, u32[]{:S(2)}, u32[]{:S(2)}) %collective-permute-start.9) | collective-permute-done | bytes 344096 | tf_op jit(solution)/shard_map/ppermute | solution.py:410
  99.5 6.3 %collective-permute-done.14.refs_2_ = bf16[96,1792]{1,0:T(8,128)(2,1)} collective-permute-done((bf16[96,1792]{1,0:T(8,128)(2,1)S(1)}, bf16[96,1792]{1,0:T(8,128)(2,1)}, u32[]{:S(2)}, u32[]{:S(2)}) %collective-permute-start.14) | collective-permute-done | bytes 344096 | tf_op jit(solution)/shard_map/ppermute | solution.py:410
  107.8 4.9 %collective-permute-done.8.refs_1_ = bf16[96,1792]{1,0:T(8,128)(2,1)S(1)} collective-permute-done((bf16[96,1792]{1,0:T(8,128)(2,1)}, bf16[96,1792]{1,0:T(8,128)(2,1)S(1)}, u32[]{:S(2)}, u32[]{:S(2)}) %collective-permute-start.8) | collective-permute-done | bytes 344096 | tf_op jit(solution)/shard_map/ppermute | solution.py:410
  112.7 3.6 %collective-permute-start.16 = (bf16[96,1792]{1,0:T(8,128)(2,1)S(1)}, bf16[96,1792]{1,0:T(8,128)(2,1)S(1)}, u32[]{:S(2)}, u32[]{:S(2)}) collective-permute-start(bf16[96,1792]{1,0:T(8,128)(2,1)S(1)} %get-tuple-element.47.refs_0_), channel_id=1, source_target_pairs={{0,192},{32,224},{64,0},{96,32},{128,64},{160,96},{192,128},{224,1... | collective-permute-start | bytes 1032200 | tf_op jit(solution)/shard_map/ppermute | solution.py:410
  116.3 4.1 %collective-permute-done.11.refs_2_ = bf16[96,1792]{1,0:T(8,128)(2,1)S(1)} collective-permute-done((bf16[96,1792]{1,0:T(8,128)(2,1)S(1)}, bf16[96,1792]{1,0:T(8,128)(2,1)S(1)}, u32[]{:S(2)}, u32[]{:S(2)}) %collective-permute-start.11) | collective-permute-done | bytes 344096 | tf_op jit(solution)/shard_map/ppermute | solution.py:410
  121.9 1.6 shard_map.97
  123.5 8.8 %all-to-all-start.1 = ((bf16[32,8,1408]{2,1,0:T(8,128)(2,1)}), bf16[32,8,1408]{2,1,0:T(8,128)(2,1)S(1)}, u32[]{:S(2)}, u32[]{:S(2)}) async-start(bf16[32,8,1408]{2,1,0:T(8,128)(2,1)} %bitcast.6), calls=%async_computation.1 | async-start | bytes 1441792 | tf_op jit(solution)/shard_map/all_to_all | solution.py:417
  132.4 1.8 copy-done.6
  134.2 1.8 copy-done.8
  139.1 8.6 %shard_map.101 = (bf16[384,3584]{1,0:T(8,128)(2,1)}, bf16[384,384]{1,0:T(8,128)(2,1)S(1)}, bf16[768,384]{1,0:T(8,128)(2,1)S(1)}, bf16[96,1792]{1,0:T(8,128)(2,1)...) custom-call(bf16[96,1792]{1,0:T(8,128)(2,1)S(1)} %copy-done.10, ...), custom_call_target="tpu_custom_call" | custom-call | flops 4227858432 | bytes 19267584 | tf_op jit(solution)/shard_map/pallas_call | solution.py:172
  148.5 2.7 %collective-permute-start.22 = (bf16[96,1792]{1,0:T(8,128)(2,1)S(1)}, bf16[96,1792]{1,0:T(8,128)(2,1)S(1)}, u32[]{:S(2)}, u32[]{:S(2)}) collective-permute-start(bf16[96,1792]{1,0:T(8,128)(2,1)S(1)} %get-tuple-element.56), channel_id=1, source_target_pairs={{0,192},{32,224},{64,0},{96,32},{128,64},{160,96},{192,128},{224,1... | collective-permute-start | bytes 1032200 | tf_op jit(solution)/shard_map/ppermute | solution.py:410
  151.7 7.9 %collective-permute-done.21.first_via = bf16[96,1792]{1,0:T(8,128)(2,1)S(1)} collective-permute-done((bf16[96,1792]{1,0:T(8,128)(2,1)S(1)}, bf16[96,1792]{1,0:T(8,128)(2,1)S(1)}, u32[]{:S(2)}, u32[]{:S(2)}) %collective-permute-start.21) | collective-permute-done | bytes 344096 | tf_op jit(solution)/shard_map/ppermute | solution.py:410
  160.6 5.6 %collective-permute-done.20.refs_1_ = bf16[96,1792]{1,0:T(8,128)(2,1)S(1)} collective-permute-done((bf16[96,1792]{1,0:T(8,128)(2,1)S(1)}, bf16[96,1792]{1,0:T(8,128)(2,1)S(1)}, u32[]{:S(2)}, u32[]{:S(2)}) %collective-permute-start.20) | collective-permute-done | bytes 344096 | tf_op jit(solution)/shard_map/ppermute | solution.py:410
  166.2 3.7 %collective-permute-start.25 = (bf16[96,1792]{1,0:T(8,128)(2,1)S(1)}, bf16[96,1792]{1,0:T(8,128)(2,1)S(1)}, u32[]{:S(2)}, u32[]{:S(2)}) collective-permute-start(bf16[96,1792]{1,0:T(8,128)(2,1)S(1)} %get-tuple-element.60), channel_id=1, source_target_pairs={{0,192},{32,224},{64,0},{96,32},{128,64},{160,96},{192,128},{224,1... | collective-permute-start | bytes 1032200 | tf_op jit(solution)/shard_map/ppermute | solution.py:410
  169.9 1.8 collective-permute-done.24.refs_4_
  171.7 6.0 %collective-permute-done.23.refs_2_ = bf16[96,1792]{1,0:T(8,128)(2,1)S(1)} collective-permute-done((bf16[96,1792]{1,0:T(8,128)(2,1)S(1)}, bf16[96,1792]{1,0:T(8,128)(2,1)S(1)}, u32[]{:S(2)}, u32[]{:S(2)}) %collective-permute-start.23) | collective-permute-done | bytes 344096 | tf_op jit(solution)/shard_map/ppermute | solution.py:410
  179.2 9.8 %all-to-all-start.3 = ((bf16[32,8,1408]{2,1,0:T(8,128)(2,1)}), bf16[32,8,1408]{2,1,0:T(8,128)(2,1)S(1)}, u32[]{:S(2)}, u32[]{:S(2)}) async-start(bf16[32,8,1408]{2,1,0:T(8,128)(2,1)} %bitcast.10), calls=%async_computation.3 | async-start | bytes 1441792 | tf_op jit(solution)/shard_map/all_to_all | solution.py:417
  190.5 19.2 %all-to-all-done.3 = bf16[32,8,1408]{2,1,0:T(8,128)(2,1)S(1)} async-done(((bf16[32,8,1408]{2,1,0:T(8,128)(2,1)}), bf16[32,8,1408]{2,1,0:T(8,128)(2,1)S(1)}, u32[]{:S(2)}, u32[]{:S(2)}) %all-to-all-start.3) | async-done | bytes 720928 | tf_op jit(solution)/shard_map/all_to_all | solution.py:417
  211.1 6.6 %wgrad_up.1 = bf16[3584,384]{1,0:T(8,128)(2,1)} custom-call(bf16[384,3584]{1,0:T(8,128)(2,1)} %get-tuple-element.61.t_a, bf16[384,3584]{1,0:T(8,128)(2,1)} %collective-permute-done.26.t_b, bf16[384,384]{1,0:T(8,128)(2,1)S(1)} %get-tuple-element.62.p_a, bf16[768,384]{1,0:T(8,128)(2,1)S(1)} %collective-permute-done.27.p_b.h_b), custom_call_target="tpu_custom_call" | custom-call | flops 2113929216 | bytes 8257536 | tf_op jit(solution)/shard_map/wgrad_up/pallas_call | solution.py:227
  217.7 6.3 %wgrad_down.1 = bf16[384,3584]{1,0:T(8,128)(2,1)} custom-call(bf16[384,384]{1,0:T(8,128)(2,1)S(1)} %get-tuple-element.64.h_a, bf16[768,384]{1,0:T(8,128)(2,1)S(1)} %collective-permute-done.27.p_b.h_b, bf16[384,3584]{1,0:T(8,128)(2,1)} %get-tuple-element.65.g_a, bf16[384,3584]{1,0:T(8,128)(2,1)} %collective-permute-done.28.g_b), custom_call_target="tpu_custom_call" | custom-call | flops 2113929216 | bytes 8257536 | tf_op jit(solution)/shard_map/wgrad_down/pallas_call | solution.py:204
  (89 shorter events, 31.8 us)
Async XLA Ops:
  0.7 67.3 %collective-permute-start.6 = (bf16[3584,384]{1,0:T(8,128)(2,1)}, bf16[3584,384]{1,0:T(8,128)(2,1)}, u32[]{:S(2)}, u32[]{:S(2)}) collective-permute-start(bf16[3584,384]{1,0:T(8,128)(2,1)} %bitcast.25), channel_id=1, source_target_pairs={{0,32},{32,0},{64,96},{96,64},{128,160},{160,128},{192,224},{224,1... | collective-permute-start | bytes 8257544 | tf_op jit(solution)/shard_map/ppermute | solution.py:413
  0.8 67.2 %collective-permute-start.7 = (bf16[384,3584]{1,0:T(8,128)(2,1)}, bf16[384,3584]{1,0:T(8,128)(2,1)}, u32[]{:S(2)}, u32[]{:S(2)}) collective-permute-start(bf16[384,3584]{1,0:T(8,128)(2,1)} %bitcast.28), channel_id=1, source_target_pairs={{0,32},{32,0},{64,96},{96,64},{128,160},{160,128},{192,224},{224,1... | collective-permute-start | bytes 8257544 | tf_op jit(solution)/shard_map/ppermute | solution.py:413
  37.2 18.0 %collective-permute-start.1 = (bf16[96,1792]{1,0:T(8,128)(2,1)S(1)}, bf16[96,1792]{1,0:T(8,128)(2,1)S(1)}, u32[]{:S(2)}, u32[]{:S(2)}) collective-permute-start(bf16[96,1792]{1,0:T(8,128)(2,1)S(1)} %get-tuple-element.36.refs_1_), channel_id=1, source_target_pairs={{0,64},{32,96},{64,128},{96,160},{128,192},{160,224},{192,0},{224,... | collective-permute-start | bytes 1032200 | tf_op jit(solution)/shard_map/ppermute | solution.py:410
  38.7 17.7 %collective-permute-start.3 = (bf16[96,1792]{1,0:T(8,128)(2,1)S(1)}, bf16[96,1792]{1,0:T(8,128)(2,1)S(1)}, u32[]{:S(2)}, u32[]{:S(2)}) collective-permute-start(bf16[96,1792]{1,0:T(8,128)(2,1)S(1)} %get-tuple-element.36.refs_1_), channel_id=1, source_target_pairs={{0,192},{32,224},{64,0},{96,32},{128,64},{160,96},{192,128},{224,1... | collective-permute-start | bytes 1032200 | tf_op jit(solution)/shard_map/ppermute | solution.py:410
  40.5 13.2 %collective-permute-start = (bf16[96,1792]{1,0:T(8,128)(2,1)S(1)}, bf16[96,1792]{1,0:T(8,128)(2,1)S(1)}, u32[]{:S(2)}, u32[]{:S(2)}) collective-permute-start(bf16[96,1792]{1,0:T(8,128)(2,1)S(1)} %get-tuple-element.35.refs_0_), channel_id=1, source_target_pairs={{0,64},{32,96},{64,128},{96,160},{128,192},{160,224},{192,0},{224,... | collective-permute-start | bytes 1032200 | tf_op jit(solution)/shard_map/ppermute | solution.py:410
  42.3 46.9 %all-to-all-start.2 = ((bf16[32,8,1408]{2,1,0:T(8,128)(2,1)}), bf16[32,8,1408]{2,1,0:T(8,128)(2,1)S(1)}, u32[]{:S(2)}, u32[]{:S(2)}) async-start(bf16[32,8,1408]{2,1,0:T(8,128)(2,1)} %bitcast.8), calls=%async_computation.2 | async-start | bytes 1441792 | tf_op jit(solution)/shard_map/all_to_all | solution.py:417
  53.6 10.6 %collective-permute-start.2 = (bf16[96,1792]{1,0:T(8,128)(2,1)S(1)}, bf16[96,1792]{1,0:T(8,128)(2,1)S(1)}, u32[]{:S(2)}, u32[]{:S(2)}) collective-permute-start(bf16[96,1792]{1,0:T(8,128)(2,1)S(1)} %get-tuple-element.35.refs_0_), channel_id=1, source_target_pairs={{0,192},{32,224},{64,0},{96,32},{128,64},{160,96},{192,128},{224,1... | collective-permute-start | bytes 1032200 | tf_op jit(solution)/shard_map/ppermute | solution.py:410
  55.2 9.1 %collective-permute-start.4 = (bf16[96,1792]{1,0:T(8,128)(2,1)S(1)}, bf16[96,1792]{1,0:T(8,128)(2,1)S(1)}, u32[]{:S(2)}, u32[]{:S(2)}) collective-permute-start(bf16[96,1792]{1,0:T(8,128)(2,1)S(1)} %collective-permute-done.refs_2_), channel_id=1, source_target_pairs={{0,64},{32,96},{64,128},{96,160},{128,192},{160,224},{192,0},{224,... | collective-permute-start | bytes 1032200 | tf_op jit(solution)/shard_map/ppermute | solution.py:410
  56.4 11.6 %collective-permute-start.5 = (bf16[96,1792]{1,0:T(8,128)(2,1)S(1)}, bf16[96,1792]{1,0:T(8,128)(2,1)S(1)}, u32[]{:S(2)}, u32[]{:S(2)}) collective-permute-start(bf16[96,1792]{1,0:T(8,128)(2,1)S(1)} %collective-permute-done.3.refs_5_), channel_id=1, source_target_pairs={{0,192},{32,224},{64,0},{96,32},{128,64},{160,96},{192,128},{224,1... | collective-permute-start | bytes 1032200 | tf_op jit(solution)/shard_map/ppermute | solution.py:410
  85.9 12.4 %collective-permute-start.9 = (bf16[96,1792]{1,0:T(8,128)(2,1)}, bf16[96,1792]{1,0:T(8,128)(2,1)S(1)}, u32[]{:S(2)}, u32[]{:S(2)}) collective-permute-start(bf16[96,1792]{1,0:T(8,128)(2,1)} %get-tuple-element.40), channel_id=1, source_target_pairs={{0,64},{32,96},{64,128},{96,160},{128,192},{160,224},{192,0},{224,... | collective-permute-start | bytes 1032200 | tf_op jit(solution)/shard_map/ppermute | solution.py:410
  86.2 12.1 %collective-permute-start.10 = (bf16[96,1792]{1,0:T(8,128)(2,1)}, bf16[96,1792]{1,0:T(8,128)(2,1)S(1)}, u32[]{:S(2)}, u32[]{:S(2)}) collective-permute-start(bf16[96,1792]{1,0:T(8,128)(2,1)} %get-tuple-element.42), channel_id=1, source_target_pairs={{0,192},{32,224},{64,0},{96,32},{128,64},{160,96},{192,128},{224,1... | collective-permute-start | bytes 1032200 | tf_op jit(solution)/shard_map/ppermute | solution.py:410
  90.5 15.3 %collective-permute-start.14 = (bf16[96,1792]{1,0:T(8,128)(2,1)S(1)}, bf16[96,1792]{1,0:T(8,128)(2,1)}, u32[]{:S(2)}, u32[]{:S(2)}) collective-permute-start(bf16[96,1792]{1,0:T(8,128)(2,1)S(1)} %get-tuple-element.47.refs_0_), channel_id=1, source_target_pairs={{0,64},{32,96},{64,128},{96,160},{128,192},{160,224},{192,0},{224,... | collective-permute-start | bytes 1032200 | tf_op jit(solution)/shard_map/ppermute | solution.py:410
  90.5 16.8 %collective-permute-start.17 = (bf16[96,1792]{1,0:T(8,128)(2,1)}, bf16[96,1792]{1,0:T(8,128)(2,1)}, u32[]{:S(2)}, u32[]{:S(2)}) collective-permute-start(bf16[96,1792]{1,0:T(8,128)(2,1)} %get-tuple-element.48.refs_1_), channel_id=1, source_target_pairs={{0,192},{32,224},{64,0},{96,32},{128,64},{160,96},{192,128},{224,1... | collective-permute-start | bytes 1032200 | tf_op jit(solution)/shard_map/ppermute | solution.py:410
  93.7 19.0 %collective-permute-start.8 = (bf16[96,1792]{1,0:T(8,128)(2,1)}, bf16[96,1792]{1,0:T(8,128)(2,1)S(1)}, u32[]{:S(2)}, u32[]{:S(2)}) collective-permute-start(bf16[96,1792]{1,0:T(8,128)(2,1)} %copy-done.12), channel_id=1, source_target_pairs={{0,192},{32,224},{64,0},{96,32},{128,64},{160,96},{192,128},{224,1... | collective-permute-start | bytes 1032200 | tf_op jit(solution)/shard_map/ppermute | solution.py:410
  98.3 18.0 %collective-permute-start.12 = (bf16[96,1792]{1,0:T(8,128)(2,1)}, bf16[96,1792]{1,0:T(8,128)(2,1)S(1)}, u32[]{:S(2)}, u32[]{:S(2)}) collective-permute-start(bf16[96,1792]{1,0:T(8,128)(2,1)} %copy-done.11), channel_id=1, source_target_pairs={{0,64},{32,96},{64,128},{96,160},{128,192},{160,224},{192,0},{224,... | collective-permute-start | bytes 1032200 | tf_op jit(solution)/shard_map/ppermute | solution.py:410
  98.5 22.0 %collective-permute-start.11 = (bf16[96,1792]{1,0:T(8,128)(2,1)S(1)}, bf16[96,1792]{1,0:T(8,128)(2,1)S(1)}, u32[]{:S(2)}, u32[]{:S(2)}) collective-permute-start(bf16[96,1792]{1,0:T(8,128)(2,1)S(1)} %get-tuple-element.43), channel_id=1, source_target_pairs={{0,64},{32,96},{64,128},{96,160},{128,192},{160,224},{192,0},{224,... | collective-permute-start | bytes 1032200 | tf_op jit(solution)/shard_map/ppermute | solution.py:410
  105.8 16.2 %collective-permute-start.13 = (bf16[96,1792]{1,0:T(8,128)(2,1)S(1)}, bf16[96,1792]{1,0:T(8,128)(2,1)S(1)}, u32[]{:S(2)}, u32[]{:S(2)}) collective-permute-start(bf16[96,1792]{1,0:T(8,128)(2,1)S(1)} %get-tuple-element.46), channel_id=1, source_target_pairs={{0,192},{32,224},{64,0},{96,32},{128,64},{160,96},{192,128},{224,1... | collective-permute-start | bytes 1032200 | tf_op jit(solution)/shard_map/ppermute | solution.py:410
  107.3 25.0 %collective-permute-start.15 = (bf16[96,1792]{1,0:T(8,128)(2,1)}, bf16[96,1792]{1,0:T(8,128)(2,1)S(1)}, u32[]{:S(2)}, u32[]{:S(2)}) collective-permute-start(bf16[96,1792]{1,0:T(8,128)(2,1)} %get-tuple-element.48.refs_1_), channel_id=1, source_target_pairs={{0,64},{32,96},{64,128},{96,160},{128,192},{160,224},{192,0},{224,... | collective-permute-start | bytes 1032200 | tf_op jit(solution)/shard_map/ppermute | solution.py:410
  112.7 19.6 %collective-permute-start.16 = (bf16[96,1792]{1,0:T(8,128)(2,1)S(1)}, bf16[96,1792]{1,0:T(8,128)(2,1)S(1)}, u32[]{:S(2)}, u32[]{:S(2)}) collective-permute-start(bf16[96,1792]{1,0:T(8,128)(2,1)S(1)} %get-tuple-element.47.refs_0_), channel_id=1, source_target_pairs={{0,192},{32,224},{64,0},{96,32},{128,64},{160,96},{192,128},{224,1... | collective-permute-start | bytes 1032200 | tf_op jit(solution)/shard_map/ppermute | solution.py:410
  116.3 16.1 %collective-permute-start.18 = (bf16[96,1792]{1,0:T(8,128)(2,1)}, bf16[96,1792]{1,0:T(8,128)(2,1)S(1)}, u32[]{:S(2)}, u32[]{:S(2)}) collective-permute-start(bf16[96,1792]{1,0:T(8,128)(2,1)} %collective-permute-done.14.refs_2_), channel_id=1, source_target_pairs={{0,64},{32,96},{64,128},{96,160},{128,192},{160,224},{192,0},{224,... | collective-permute-start | bytes 1032200 | tf_op jit(solution)/shard_map/ppermute | solution.py:410
  120.4 11.9 %collective-permute-start.19 = (bf16[96,1792]{1,0:T(8,128)(2,1)}, bf16[96,1792]{1,0:T(8,128)(2,1)S(1)}, u32[]{:S(2)}, u32[]{:S(2)}) collective-permute-start(bf16[96,1792]{1,0:T(8,128)(2,1)} %collective-permute-done.17.refs_5_), channel_id=1, source_target_pairs={{0,192},{32,224},{64,0},{96,32},{128,64},{160,96},{192,128},{224,1... | collective-permute-start | bytes 1032200 | tf_op jit(solution)/shard_map/ppermute | solution.py:410
  121.9 89.1 %collective-permute-start.26 = (bf16[384,3584]{1,0:T(8,128)(2,1)}, bf16[384,3584]{1,0:T(8,128)(2,1)}, u32[]{:S(2)}, u32[]{:S(2)}) collective-permute-start(bf16[384,3584]{1,0:T(8,128)(2,1)} %get-tuple-element.61.t_a), channel_id=1, source_target_pairs={{0,32},{32,0},{64,96},{96,64},{128,160},{160,128},{192,224},{224,1... | collective-permute-start | bytes 8257544 | tf_op jit(solution)/shard_map/ppermute | solution.py:413
  123.5 55.7 %all-to-all-start.1 = ((bf16[32,8,1408]{2,1,0:T(8,128)(2,1)}), bf16[32,8,1408]{2,1,0:T(8,128)(2,1)S(1)}, u32[]{:S(2)}, u32[]{:S(2)}) async-start(bf16[32,8,1408]{2,1,0:T(8,128)(2,1)} %bitcast.6), calls=%async_computation.1 | async-start | bytes 1441792 | tf_op jit(solution)/shard_map/all_to_all | solution.py:417
  147.8 69.9 %collective-permute-start.28 = (bf16[384,3584]{1,0:T(8,128)(2,1)}, bf16[384,3584]{1,0:T(8,128)(2,1)}, u32[]{:S(2)}, u32[]{:S(2)}) collective-permute-start(bf16[384,3584]{1,0:T(8,128)(2,1)} %get-tuple-element.65.g_a), channel_id=1, source_target_pairs={{0,32},{32,0},{64,96},{96,64},{128,160},{160,128},{192,224},{224,1... | collective-permute-start | bytes 8257544 | tf_op jit(solution)/shard_map/ppermute | solution.py:413
  147.9 11.7 %collective-permute-start.21 = (bf16[96,1792]{1,0:T(8,128)(2,1)S(1)}, bf16[96,1792]{1,0:T(8,128)(2,1)S(1)}, u32[]{:S(2)}, u32[]{:S(2)}) collective-permute-start(bf16[96,1792]{1,0:T(8,128)(2,1)S(1)} %get-tuple-element.54), channel_id=1, source_target_pairs={{0,64},{32,96},{64,128},{96,160},{128,192},{160,224},{192,0},{224,... | collective-permute-start | bytes 1032200 | tf_op jit(solution)/shard_map/ppermute | solution.py:410
  148.5 11.2 %collective-permute-start.22 = (bf16[96,1792]{1,0:T(8,128)(2,1)S(1)}, bf16[96,1792]{1,0:T(8,128)(2,1)S(1)}, u32[]{:S(2)}, u32[]{:S(2)}) collective-permute-start(bf16[96,1792]{1,0:T(8,128)(2,1)S(1)} %get-tuple-element.56), channel_id=1, source_target_pairs={{0,192},{32,224},{64,0},{96,32},{128,64},{160,96},{192,128},{224,1... | collective-permute-start | bytes 1032200 | tf_op jit(solution)/shard_map/ppermute | solution.py:410
  151.2 15.0 %collective-permute-start.20 = (bf16[96,1792]{1,0:T(8,128)(2,1)S(1)}, bf16[96,1792]{1,0:T(8,128)(2,1)S(1)}, u32[]{:S(2)}, u32[]{:S(2)}) collective-permute-start(bf16[96,1792]{1,0:T(8,128)(2,1)S(1)} %get-tuple-element.52), channel_id=1, source_target_pairs={{0,192},{32,224},{64,0},{96,32},{128,64},{160,96},{192,128},{224,1... | collective-permute-start | bytes 1032200 | tf_op jit(solution)/shard_map/ppermute | solution.py:410
  159.6 12.1 %collective-permute-start.24 = (bf16[96,1792]{1,0:T(8,128)(2,1)S(1)}, bf16[96,1792]{1,0:T(8,128)(2,1)S(1)}, u32[]{:S(2)}, u32[]{:S(2)}) collective-permute-start(bf16[96,1792]{1,0:T(8,128)(2,1)S(1)} %get-tuple-element.59), channel_id=1, source_target_pairs={{0,64},{32,96},{64,128},{96,160},{128,192},{160,224},{192,0},{224,... | collective-permute-start | bytes 1032200 | tf_op jit(solution)/shard_map/ppermute | solution.py:410
  159.8 17.9 %collective-permute-start.23 = (bf16[96,1792]{1,0:T(8,128)(2,1)S(1)}, bf16[96,1792]{1,0:T(8,128)(2,1)S(1)}, u32[]{:S(2)}, u32[]{:S(2)}) collective-permute-start(bf16[96,1792]{1,0:T(8,128)(2,1)S(1)} %get-tuple-element.57), channel_id=1, source_target_pairs={{0,64},{32,96},{64,128},{96,160},{128,192},{160,224},{192,0},{224,... | collective-permute-start | bytes 1032200 | tf_op jit(solution)/shard_map/ppermute | solution.py:410
  166.2 11.5 %collective-permute-start.25 = (bf16[96,1792]{1,0:T(8,128)(2,1)S(1)}, bf16[96,1792]{1,0:T(8,128)(2,1)S(1)}, u32[]{:S(2)}, u32[]{:S(2)}) collective-permute-start(bf16[96,1792]{1,0:T(8,128)(2,1)S(1)} %get-tuple-element.60), channel_id=1, source_target_pairs={{0,192},{32,224},{64,0},{96,32},{128,64},{160,96},{192,128},{224,1... | collective-permute-start | bytes 1032200 | tf_op jit(solution)/shard_map/ppermute | solution.py:410
  179.2 30.5 %all-to-all-start.3 = ((bf16[32,8,1408]{2,1,0:T(8,128)(2,1)}), bf16[32,8,1408]{2,1,0:T(8,128)(2,1)S(1)}, u32[]{:S(2)}, u32[]{:S(2)}) async-start(bf16[32,8,1408]{2,1,0:T(8,128)(2,1)} %bitcast.10), calls=%async_computation.3 | async-start | bytes 1441792 | tf_op jit(solution)/shard_map/all_to_all | solution.py:417
  189.0 22.1 %collective-permute-start.27 = (bf16[768,384]{1,0:T(8,128)(2,1)S(1)}, bf16[768,384]{1,0:T(8,128)(2,1)S(1)}, u32[]{:S(2)}, u32[]{:S(2)}) collective-permute-start(bf16[768,384]{1,0:T(8,128)(2,1)S(1)} %get-tuple-element.63), channel_id=1, source_target_pairs={{0,32},{32,0},{64,96},{96,64},{128,160},{160,128},{192,224},{224,1... | collective-permute-start | bytes 1769480 | tf_op jit(solution)/shard_map/ppermute | solution.py:413
  (21 other events, 169.9 us)

commit v5 on v4

--- a/solution.py
+++ b/solution.py
@@ -169,10 +169,11 @@
     outs += [shape((rows, units), BF16), shape((2 * rows if back else rows, units), BF16)]
     outs += [shape((size, half), BF16)] * 8
     anywhere = pl.BlockSpec(memory_space=pl.ANY)
+    main = pl.BlockSpec(memory_space=pltpu.HBM)
     return pl.pallas_call(
         functools.partial(layer_body, back),
-        in_specs=[anywhere] * (12 + len(saved)),
-        out_specs=[anywhere] * len(outs),
+        in_specs=[anywhere] * 8 + [main] * 4 + [anywhere] * len(saved),
+        out_specs=[main] + [anywhere] * (not back) + [main] + [anywhere] * 9,
         out_shape=outs,
         scratch_shapes=[
             pltpu.VMEM((rows, width), BF16),
@@ -187,7 +188,7 @@
         ],
         compiler_params=pltpu.CompilerParams(vmem_limit_bytes=28 * 2**20),
         cost_estimate=cost(8 * rows * width * units, 6 * rows * width + 8 * width * units),
-    )(*pieces, *weights, *saved)
+    )(*pieces, *map(in_hbm, weights), *saved)
 
 
 def down_grad_body(h_a, h_b, g_a, g_b, out):
@@ -383,6 +384,37 @@
         out[...] = read_blocks(out.shape[1], [p[:count] + p[count:] for p in place], block[...])
 
 
+def fetch_body(body, count, *refs):
+    inputs, out = refs[:count], refs[count]
+    buffers, sems = refs[count + 1 : -1], refs[-1]
+    tasks = [
+        pltpu.make_async_copy(source, target, sems.at[i])
+        for i, (source, target) in enumerate(zip(inputs, buffers))
+    ]
+    for task in tasks:
+        task.start()
+    for task in tasks:
+        task.wait()
+    body(*buffers, out)
+
+
+def in_hbm(value):
+    return pltpu.with_memory_space_constraint(value, pltpu.HBM)
+
+
+def fetching(body, shape, flops, *args):
+    moved = sum(a.size * a.dtype.itemsize for a in args) + 2 * shape[0] * shape[1]
+    return pl.pallas_call(
+        functools.partial(fetch_body, body, len(args)),
+        in_specs=[pl.BlockSpec(memory_space=pltpu.HBM)] * len(args),
+        out_shape=jax.ShapeDtypeStruct(shape, BF16),
+        scratch_shapes=[pltpu.VMEM(a.shape, a.dtype) for a in args]
+        + [pltpu.SemaphoreType.DMA((len(args),))],
+        compiler_params=pltpu.CompilerParams(vmem_limit_bytes=12 * 2**20),
+        cost_estimate=cost(flops, moved),
+    )(*map(in_hbm, args))
+
+
 def single(body, shape, flops, *args, outs=None):
     moved = sum(a.size * a.dtype.itemsize for a in args) + 2 * shape[0] * shape[1] * (outs or 1)
     out_shape = jax.ShapeDtypeStruct(shape, BF16)
@@ -440,11 +472,11 @@
     up_own, down_own = w_up[0], w_down[0]
     ids, mix = expert_ids.T, mix_weights.T
 
-    token_send = small_call(
-        functools.partial(dispatch_body, False), block_shape, ids, tokens)
+    token_send = fetching(
+        functools.partial(dispatch_body, False), block_shape, small, ids, tokens)
     token_moved = exchange(token_send)
-    grad_send = small_call(
-        functools.partial(dispatch_body, True), block_shape,
+    grad_send = fetching(
+        functools.partial(dispatch_body, True), block_shape, small,
         ids, mix, out_grad)
     grad_moved = exchange(grad_send)
 
@@ -467,8 +499,8 @@
 
     both_in = swap(both_other)
     g_in, t_in = swap(grad_rows), swap(token_rows)
-    grad_down = down_grad(h_own, both_in, grad_rows, g_in, 2 * STEPS)
-    grad_up = up_grad(token_rows, t_in, p_own, both_in, 2 * STEPS)
+    grad_down = down_grad(in_hbm(h_own), both_in, grad_rows, g_in, 2 * STEPS)
+    grad_up = up_grad(token_rows, t_in, in_hbm(p_own), both_in, 2 * STEPS)
 
     layer_out = small_call(
         functools.partial(combine_body, True), (tok_count, width),

time: 225 us -> 218 us (0.969)
  local copies, waits for them, and re-layouts: 18.6 us -> 9.31 us
  Pallas kernels: 40.8 us -> 43.6 us
    unnamed x42 -> x28, local copies, waits for them, and re-layouts: 18.6 us -> 9.31 us
    pallas_call x0 -> x2, Pallas kernels: none -> 4.02 us  [fetching(): pl.pallas_call(functools.partial(fetch_body, body, len(args)), in_specs=[...]
    pallas_call x10 -> x8, Pallas kernels: 10.1 us -> 7.16 us  [single(): pl.pallas_call(body, in_specs=[pl.BlockSpec(memory_space=pltpu.VMEM)] * l...]
  transfers between devices with their start and end apart: 32 -> 32, of which waited for: 13 -> 13; matrix products, arithmetic and copies ran while one was open for 0% -> 0% of each run, Pallas kernels for 15% -> 17%
where the time goes in v5:
time: 218 us; the launch traced here: 217 us
  waiting for transfers between devices  74.3 us (34%)
  starting transfers between devices  55.8 us (26%)
  Pallas kernels  43.6 us (20%)
  blocking collectives  33.2 us (15%)
  local copies, waits for them, and re-layouts  9.31 us (4%)
    ppermute x24, waiting for transfers between devices, shift(): return lax.ppermute(value, 'dp', perm)  54.9 us
    all_to_all x1, blocking collectives, exchange(): lax.all_to_all(blocks, 'expert', split_axis=0, concat_axis=0, tiled=True)  33.2 us
    ppermute x24, starting transfers between devices, shift(): return lax.ppermute(value, 'dp', perm)  31.5 us
    all_to_all x3, starting transfers between devices, exchange(): lax.all_to_all(blocks, 'expert', split_axis=0, concat_axis=0, tiled=True)  23.5 us
    all_to_all x3, waiting for transfers between devices, exchange(): lax.all_to_all(blocks, 'expert', split_axis=0, concat_axis=0, tiled=True)  19.4 us
    pallas_call x2, Pallas kernels, layer_call(): pl.pallas_call(functools.partial(layer_body, back), in_specs=[anywhere] *...  19.4 us
    unnamed x28, local copies, waits for them, and re-layouts  9.31 us
    pallas_call x8, Pallas kernels, single(): pl.pallas_call(body, in_specs=[pl.BlockSpec(memory_space=pltpu.VMEM)] * l...  7.16 us
  transfers between devices with their start and end apart: 32, of which 13 were waited for; matrix products, arithmetic and copies ran while one was open for 0% of the time, Pallas kernels for 17%

profile of v5, /device:TPU:32, one launch (start us, length us, event | category | flops | bytes accessed | tf_op | source)
XLA Modules:
  0.0 217.0 jit_solution(18077386889381843426)
XLA Ops:
  1.2 1.6 shard_map.93
  2.8 33.2 %all_to_all.20 = bf16[32,8,1408]{2,1,0:T(8,128)(2,1)S(1)} all-to-all(bf16[32,8,1408]{2,1,0:T(8,128)(2,1)S(1)} %bitcast.17), channel_id=1, replica_groups=mesh['dp'=8,'expert'=32] {'expert'}, dimensions={0} | all-to-all | bytes 1441792 | tf_op jit(solution)/shard_map/all_to_all | solution.py:449
  36.5 1.6 collective-permute-start.1
  38.1 1.7 collective-permute-start.3
  40.1 2.5 %shard_map.99 = bf16[256,1408]{1,0:T(8,128)(2,1)} custom-call(s32[2,32]{1,0:T(2,128)} %bitcast.20, f32[2,32]{1,0:T(2,128)} %bitcast.23, bf16[32,3584]{1,0:T(8,128)(2,1)} %refs_2_.1), custom_call_target="tpu_custom_call" | custom-call | flops 184549376 | bytes 950784 | tf_op jit(solution)/shard_map/pallas_call | solution.py:407
  42.5 5.0 %all-to-all-start.2 = ((bf16[32,8,1408]{2,1,0:T(8,128)(2,1)}), bf16[32,8,1408]{2,1,0:T(8,128)(2,1)S(1)}, u32[]{:S(2)}, u32[]{:S(2)}) async-start(bf16[32,8,1408]{2,1,0:T(8,128)(2,1)} %bitcast.8), calls=%async_computation.2 | async-start | bytes 1441792 | tf_op jit(solution)/shard_map/all_to_all | solution.py:449
  47.5 5.4 %collective-permute-done.refs_2_ = bf16[96,1792]{1,0:T(8,128)(2,1)S(1)} collective-permute-done((bf16[96,1792]{1,0:T(8,128)(2,1)S(1)}, bf16[96,1792]{1,0:T(8,128)(2,1)S(1)}, u32[]{:S(2)}, u32[]{:S(2)}) %collective-permute-start) | collective-permute-done | bytes 344096 | tf_op jit(solution)/shard_map/ppermute | solution.py:442
  55.7 2.8 %collective-permute-start.5 = (bf16[96,1792]{1,0:T(8,128)(2,1)S(1)}, bf16[96,1792]{1,0:T(8,128)(2,1)S(1)}, u32[]{:S(2)}, u32[]{:S(2)}) collective-permute-start(bf16[96,1792]{1,0:T(8,128)(2,1)S(1)} %collective-permute-done.3.refs_5_), channel_id=1, source_target_pairs={{0,192},{32,224},{64,0},{96,32},{128,64},{160,96},{192,128},{224,1... | collective-permute-start | bytes 1032200 | tf_op jit(solution)/shard_map/ppermute | solution.py:442
  59.2 4.4 %collective-permute-done.2.refs_4_ = bf16[96,1792]{1,0:T(8,128)(2,1)S(1)} collective-permute-done((bf16[96,1792]{1,0:T(8,128)(2,1)S(1)}, bf16[96,1792]{1,0:T(8,128)(2,1)S(1)}, u32[]{:S(2)}, u32[]{:S(2)}) %collective-permute-start.2) | collective-permute-done | bytes 344096 | tf_op jit(solution)/shard_map/ppermute | solution.py:442
  63.6 3.7 %collective-permute-done.5.refs_7_ = bf16[96,1792]{1,0:T(8,128)(2,1)S(1)} collective-permute-done((bf16[96,1792]{1,0:T(8,128)(2,1)S(1)}, bf16[96,1792]{1,0:T(8,128)(2,1)S(1)}, u32[]{:S(2)}, u32[]{:S(2)}) %collective-permute-start.5) | collective-permute-done | bytes 344096 | tf_op jit(solution)/shard_map/ppermute | solution.py:442
  69.2 9.9 %shard_map.95 = (bf16[384,3584]{1,0:T(8,128)(2,1)}, f32[384,768]{1,0:T(8,128)S(1)}, bf16[384,384]{1,0:T(8,128)(2,1)S(1)}, bf16[384,384]{1,0:T(8,128)(2,1)S(1)}, ...) custom-call(bf16[96,1792]{1,0:T(8,128)(2,1)S(1)} %get-tuple-element., ...), custom_call_target="tpu_custom_call" | custom-call | flops 4227858432 | bytes 19267584 | tf_op jit(solution)/shard_map/pallas_call | solution.py:173
  83.1 2.8 %collective-permute-start.10 = (bf16[96,1792]{1,0:T(8,128)(2,1)}, bf16[96,1792]{1,0:T(8,128)(2,1)S(1)}, u32[]{:S(2)}, u32[]{:S(2)}) collective-permute-start(bf16[96,1792]{1,0:T(8,128)(2,1)} %get-tuple-element.42), channel_id=1, source_target_pairs={{0,192},{32,224},{64,0},{96,32},{128,64},{160,96},{192,128},{224,1... | collective-permute-start | bytes 1032200 | tf_op jit(solution)/shard_map/ppermute | solution.py:442
  86.5 3.2 %collective-permute-start.17 = (bf16[96,1792]{1,0:T(8,128)(2,1)S(1)}, bf16[96,1792]{1,0:T(8,128)(2,1)S(1)}, u32[]{:S(2)}, u32[]{:S(2)}) collective-permute-start(bf16[96,1792]{1,0:T(8,128)(2,1)S(1)} %get-tuple-element.48.refs_1_), channel_id=1, source_target_pairs={{0,192},{32,224},{64,0},{96,32},{128,64},{160,96},{192,128},{224,1... | collective-permute-start | bytes 1032200 | tf_op jit(solution)/shard_map/ppermute | solution.py:442
  89.7 4.9 %collective-permute-done.9.first_via = bf16[96,1792]{1,0:T(8,128)(2,1)S(1)} collective-permute-done((bf16[96,1792]{1,0:T(8,128)(2,1)}, bf16[96,1792]{1,0:T(8,128)(2,1)S(1)}, u32[]{:S(2)}, u32[]{:S(2)}) %collective-permute-start.9) | collective-permute-done | bytes 344096 | tf_op jit(solution)/shard_map/ppermute | solution.py:442
  95.9 6.2 %collective-permute-done.14.refs_2_ = bf16[96,1792]{1,0:T(8,128)(2,1)S(1)} collective-permute-done((bf16[96,1792]{1,0:T(8,128)(2,1)S(1)}, bf16[96,1792]{1,0:T(8,128)(2,1)S(1)}, u32[]{:S(2)}, u32[]{:S(2)}) %collective-permute-start.14) | collective-permute-done | bytes 344096 | tf_op jit(solution)/shard_map/ppermute | solution.py:442
  102.1 1.5 collective-permute-start.13
  104.1 5.3 %collective-permute-done.8.refs_1_ = bf16[96,1792]{1,0:T(8,128)(2,1)S(1)} collective-permute-done((bf16[96,1792]{1,0:T(8,128)(2,1)}, bf16[96,1792]{1,0:T(8,128)(2,1)S(1)}, u32[]{:S(2)}, u32[]{:S(2)}) %collective-permute-start.8) | collective-permute-done | bytes 344096 | tf_op jit(solution)/shard_map/ppermute | solution.py:442
  109.4 3.6 %collective-permute-start.16 = (bf16[96,1792]{1,0:T(8,128)(2,1)S(1)}, bf16[96,1792]{1,0:T(8,128)(2,1)}, u32[]{:S(2)}, u32[]{:S(2)}) collective-permute-start(bf16[96,1792]{1,0:T(8,128)(2,1)S(1)} %get-tuple-element.47.refs_0_), channel_id=1, source_target_pairs={{0,192},{32,224},{64,0},{96,32},{128,64},{160,96},{192,128},{224,1... | collective-permute-start | bytes 1032200 | tf_op jit(solution)/shard_map/ppermute | solution.py:442
  113.0 3.8 %collective-permute-done.11.refs_2_ = bf16[96,1792]{1,0:T(8,128)(2,1)S(1)} collective-permute-done((bf16[96,1792]{1,0:T(8,128)(2,1)S(1)}, bf16[96,1792]{1,0:T(8,128)(2,1)S(1)}, u32[]{:S(2)}, u32[]{:S(2)}) %collective-permute-start.11) | collective-permute-done | bytes 344096 | tf_op jit(solution)/shard_map/ppermute | solution.py:442
  118.3 1.6 shard_map.97
  119.9 8.8 %all-to-all-start.1 = ((bf16[32,8,1408]{2,1,0:T(8,128)(2,1)}), bf16[32,8,1408]{2,1,0:T(8,128)(2,1)S(1)}, u32[]{:S(2)}, u32[]{:S(2)}) async-start(bf16[32,8,1408]{2,1,0:T(8,128)(2,1)} %bitcast.6), calls=%async_computation.1 | async-start | bytes 1441792 | tf_op jit(solution)/shard_map/all_to_all | solution.py:449
  131.0 9.5 %shard_map.101 = (bf16[384,3584]{1,0:T(8,128)(2,1)}, bf16[384,384]{1,0:T(8,128)(2,1)S(1)}, bf16[768,384]{1,0:T(8,128)(2,1)S(1)}, bf16[96,1792]{1,0:T(8,128)(2,1)...) custom-call(bf16[96,1792]{1,0:T(8,128)(2,1)S(1)} %get-tuple-element., ...), custom_call_target="tpu_custom_call" | custom-call | flops 4227858432 | bytes 19267584 | tf_op jit(solution)/shard_map/pallas_call | solution.py:173
  141.2 2.7 %collective-permute-start.22 = (bf16[96,1792]{1,0:T(8,128)(2,1)S(1)}, bf16[96,1792]{1,0:T(8,128)(2,1)S(1)}, u32[]{:S(2)}, u32[]{:S(2)}) collective-permute-start(bf16[96,1792]{1,0:T(8,128)(2,1)S(1)} %get-tuple-element.56), channel_id=1, source_target_pairs={{0,192},{32,224},{64,0},{96,32},{128,64},{160,96},{192,128},{224,1... | collective-permute-start | bytes 1032200 | tf_op jit(solution)/shard_map/ppermute | solution.py:442
  144.7 7.6 %collective-permute-done.21.first_via = bf16[96,1792]{1,0:T(8,128)(2,1)S(1)} collective-permute-done((bf16[96,1792]{1,0:T(8,128)(2,1)S(1)}, bf16[96,1792]{1,0:T(8,128)(2,1)S(1)}, u32[]{:S(2)}, u32[]{:S(2)}) %collective-permute-start.21) | collective-permute-done | bytes 344096 | tf_op jit(solution)/shard_map/ppermute | solution.py:442
  153.3 5.6 %collective-permute-done.20.refs_1_ = bf16[96,1792]{1,0:T(8,128)(2,1)S(1)} collective-permute-done((bf16[96,1792]{1,0:T(8,128)(2,1)S(1)}, bf16[96,1792]{1,0:T(8,128)(2,1)S(1)}, u32[]{:S(2)}, u32[]{:S(2)}) %collective-permute-start.20) | collective-permute-done | bytes 344096 | tf_op jit(solution)/shard_map/ppermute | solution.py:442
  158.9 3.7 %collective-permute-start.25 = (bf16[96,1792]{1,0:T(8,128)(2,1)S(1)}, bf16[96,1792]{1,0:T(8,128)(2,1)S(1)}, u32[]{:S(2)}, u32[]{:S(2)}) collective-permute-start(bf16[96,1792]{1,0:T(8,128)(2,1)S(1)} %get-tuple-element.60), channel_id=1, source_target_pairs={{0,192},{32,224},{64,0},{96,32},{128,64},{160,96},{192,128},{224,1... | collective-permute-start | bytes 1032200 | tf_op jit(solution)/shard_map/ppermute | solution.py:442
  162.6 1.8 collective-permute-done.24.refs_4_
  164.4 6.0 %collective-permute-done.23.refs_2_ = bf16[96,1792]{1,0:T(8,128)(2,1)S(1)} collective-permute-done((bf16[96,1792]{1,0:T(8,128)(2,1)S(1)}, bf16[96,1792]{1,0:T(8,128)(2,1)S(1)}, u32[]{:S(2)}, u32[]{:S(2)}) %collective-permute-start.23) | collective-permute-done | bytes 344096 | tf_op jit(solution)/shard_map/ppermute | solution.py:442
  171.9 9.8 %all-to-all-start.3 = ((bf16[32,8,1408]{2,1,0:T(8,128)(2,1)}), bf16[32,8,1408]{2,1,0:T(8,128)(2,1)S(1)}, u32[]{:S(2)}, u32[]{:S(2)}) async-start(bf16[32,8,1408]{2,1,0:T(8,128)(2,1)} %bitcast.10), calls=%async_computation.3 | async-start | bytes 1441792 | tf_op jit(solution)/shard_map/all_to_all | solution.py:449
  183.2 19.4 %all-to-all-done.3 = bf16[32,8,1408]{2,1,0:T(8,128)(2,1)S(1)} async-done(((bf16[32,8,1408]{2,1,0:T(8,128)(2,1)}), bf16[32,8,1408]{2,1,0:T(8,128)(2,1)S(1)}, u32[]{:S(2)}, u32[]{:S(2)}) %all-to-all-start.3) | async-done | bytes 720928 | tf_op jit(solution)/shard_map/all_to_all | solution.py:449
  204.0 6.7 %wgrad_up.1 = bf16[3584,384]{1,0:T(8,128)(2,1)} custom-call(bf16[384,3584]{1,0:T(8,128)(2,1)} %get-tuple-element.61.t_a, bf16[384,3584]{1,0:T(8,128)(2,1)} %collective-permute-done.26.t_b, bf16[384,384]{1,0:T(8,128)(2,1)} %copy-done.1, bf16[768,384]{1,0:T(8,128)(2,1)S(1)} %collective-permute-done.27.p_b.h_b), custom_call_target="tpu_custom_call" | custom-call | flops 2113929216 | bytes 8257536 | tf_op jit(solution)/shard_map/wgrad_up/pallas_call | solution.py:228
  210.6 6.4 %wgrad_down.1 = bf16[384,3584]{1,0:T(8,128)(2,1)} custom-call(bf16[384,384]{1,0:T(8,128)(2,1)} %copy-done, bf16[768,384]{1,0:T(8,128)(2,1)S(1)} %collective-permute-done.27.p_b.h_b, bf16[384,3584]{1,0:T(8,128)(2,1)} %get-tuple-element.65.g_a, bf16[384,3584]{1,0:T(8,128)(2,1)} %collective-permute-done.28.g_b), custom_call_target="tpu_custom_call" | custom-call | flops 2113929216 | bytes 8257536 | tf_op jit(solution)/shard_map/wgrad_down/pallas_call | solution.py:205
  (75 shorter events, 23.7 us)
Async XLA Ops:
  0.6 66.7 %collective-permute-start.6 = (bf16[3584,384]{1,0:T(8,128)(2,1)}, bf16[3584,384]{1,0:T(8,128)(2,1)}, u32[]{:S(2)}, u32[]{:S(2)}) collective-permute-start(bf16[3584,384]{1,0:T(8,128)(2,1)} %bitcast.27), channel_id=1, source_target_pairs={{0,32},{32,0},{64,96},{96,64},{128,160},{160,128},{192,224},{224,1... | collective-permute-start | bytes 8257544 | tf_op jit(solution)/shard_map/ppermute | solution.py:445
  0.7 66.5 %collective-permute-start.7 = (bf16[384,3584]{1,0:T(8,128)(2,1)}, bf16[384,3584]{1,0:T(8,128)(2,1)}, u32[]{:S(2)}, u32[]{:S(2)}) collective-permute-start(bf16[384,3584]{1,0:T(8,128)(2,1)} %bitcast.30), channel_id=1, source_target_pairs={{0,32},{32,0},{64,96},{96,64},{128,160},{160,128},{192,224},{224,1... | collective-permute-start | bytes 8257544 | tf_op jit(solution)/shard_map/ppermute | solution.py:445
  36.5 18.0 %collective-permute-start.1 = (bf16[96,1792]{1,0:T(8,128)(2,1)S(1)}, bf16[96,1792]{1,0:T(8,128)(2,1)S(1)}, u32[]{:S(2)}, u32[]{:S(2)}) collective-permute-start(bf16[96,1792]{1,0:T(8,128)(2,1)S(1)} %get-tuple-element.36.refs_1_), channel_id=1, source_target_pairs={{0,64},{32,96},{64,128},{96,160},{128,192},{160,224},{192,0},{224,... | collective-permute-start | bytes 1032200 | tf_op jit(solution)/shard_map/ppermute | solution.py:442
  38.1 17.7 %collective-permute-start.3 = (bf16[96,1792]{1,0:T(8,128)(2,1)S(1)}, bf16[96,1792]{1,0:T(8,128)(2,1)S(1)}, u32[]{:S(2)}, u32[]{:S(2)}) collective-permute-start(bf16[96,1792]{1,0:T(8,128)(2,1)S(1)} %get-tuple-element.36.refs_1_), channel_id=1, source_target_pairs={{0,192},{32,224},{64,0},{96,32},{128,64},{160,96},{192,128},{224,1... | collective-permute-start | bytes 1032200 | tf_op jit(solution)/shard_map/ppermute | solution.py:442
  39.8 13.2 %collective-permute-start = (bf16[96,1792]{1,0:T(8,128)(2,1)S(1)}, bf16[96,1792]{1,0:T(8,128)(2,1)S(1)}, u32[]{:S(2)}, u32[]{:S(2)}) collective-permute-start(bf16[96,1792]{1,0:T(8,128)(2,1)S(1)} %get-tuple-element.35.refs_0_), channel_id=1, source_target_pairs={{0,64},{32,96},{64,128},{96,160},{128,192},{160,224},{192,0},{224,... | collective-permute-start | bytes 1032200 | tf_op jit(solution)/shard_map/ppermute | solution.py:442
  42.5 43.3 %all-to-all-start.2 = ((bf16[32,8,1408]{2,1,0:T(8,128)(2,1)}), bf16[32,8,1408]{2,1,0:T(8,128)(2,1)S(1)}, u32[]{:S(2)}, u32[]{:S(2)}) async-start(bf16[32,8,1408]{2,1,0:T(8,128)(2,1)} %bitcast.8), calls=%async_computation.2 | async-start | bytes 1441792 | tf_op jit(solution)/shard_map/all_to_all | solution.py:449
  53.0 10.6 %collective-permute-start.2 = (bf16[96,1792]{1,0:T(8,128)(2,1)S(1)}, bf16[96,1792]{1,0:T(8,128)(2,1)S(1)}, u32[]{:S(2)}, u32[]{:S(2)}) collective-permute-start(bf16[96,1792]{1,0:T(8,128)(2,1)S(1)} %get-tuple-element.35.refs_0_), channel_id=1, source_target_pairs={{0,192},{32,224},{64,0},{96,32},{128,64},{160,96},{192,128},{224,1... | collective-permute-start | bytes 1032200 | tf_op jit(solution)/shard_map/ppermute | solution.py:442
  54.5 9.1 %collective-permute-start.4 = (bf16[96,1792]{1,0:T(8,128)(2,1)S(1)}, bf16[96,1792]{1,0:T(8,128)(2,1)S(1)}, u32[]{:S(2)}, u32[]{:S(2)}) collective-permute-start(bf16[96,1792]{1,0:T(8,128)(2,1)S(1)} %collective-permute-done.refs_2_), channel_id=1, source_target_pairs={{0,64},{32,96},{64,128},{96,160},{128,192},{160,224},{192,0},{224,... | collective-permute-start | bytes 1032200 | tf_op jit(solution)/shard_map/ppermute | solution.py:442
  55.7 11.6 %collective-permute-start.5 = (bf16[96,1792]{1,0:T(8,128)(2,1)S(1)}, bf16[96,1792]{1,0:T(8,128)(2,1)S(1)}, u32[]{:S(2)}, u32[]{:S(2)}) collective-permute-start(bf16[96,1792]{1,0:T(8,128)(2,1)S(1)} %collective-permute-done.3.refs_5_), channel_id=1, source_target_pairs={{0,192},{32,224},{64,0},{96,32},{128,64},{160,96},{192,128},{224,1... | collective-permute-start | bytes 1032200 | tf_op jit(solution)/shard_map/ppermute | solution.py:442
  82.3 12.4 %collective-permute-start.9 = (bf16[96,1792]{1,0:T(8,128)(2,1)}, bf16[96,1792]{1,0:T(8,128)(2,1)S(1)}, u32[]{:S(2)}, u32[]{:S(2)}) collective-permute-start(bf16[96,1792]{1,0:T(8,128)(2,1)} %get-tuple-element.40), channel_id=1, source_target_pairs={{0,64},{32,96},{64,128},{96,160},{128,192},{160,224},{192,0},{224,... | collective-permute-start | bytes 1032200 | tf_op jit(solution)/shard_map/ppermute | solution.py:442
  83.1 11.6 %collective-permute-start.10 = (bf16[96,1792]{1,0:T(8,128)(2,1)}, bf16[96,1792]{1,0:T(8,128)(2,1)S(1)}, u32[]{:S(2)}, u32[]{:S(2)}) collective-permute-start(bf16[96,1792]{1,0:T(8,128)(2,1)} %get-tuple-element.42), channel_id=1, source_target_pairs={{0,192},{32,224},{64,0},{96,32},{128,64},{160,96},{192,128},{224,1... | collective-permute-start | bytes 1032200 | tf_op jit(solution)/shard_map/ppermute | solution.py:442
  86.4 15.7 %collective-permute-start.14 = (bf16[96,1792]{1,0:T(8,128)(2,1)S(1)}, bf16[96,1792]{1,0:T(8,128)(2,1)S(1)}, u32[]{:S(2)}, u32[]{:S(2)}) collective-permute-start(bf16[96,1792]{1,0:T(8,128)(2,1)S(1)} %get-tuple-element.47.refs_0_), channel_id=1, source_target_pairs={{0,64},{32,96},{64,128},{96,160},{128,192},{160,224},{192,0},{224,... | collective-permute-start | bytes 1032200 | tf_op jit(solution)/shard_map/ppermute | solution.py:442
  86.5 17.1 %collective-permute-start.17 = (bf16[96,1792]{1,0:T(8,128)(2,1)S(1)}, bf16[96,1792]{1,0:T(8,128)(2,1)S(1)}, u32[]{:S(2)}, u32[]{:S(2)}) collective-permute-start(bf16[96,1792]{1,0:T(8,128)(2,1)S(1)} %get-tuple-element.48.refs_1_), channel_id=1, source_target_pairs={{0,192},{32,224},{64,0},{96,32},{128,64},{160,96},{192,128},{224,1... | collective-permute-start | bytes 1032200 | tf_op jit(solution)/shard_map/ppermute | solution.py:442
  89.7 19.7 %collective-permute-start.8 = (bf16[96,1792]{1,0:T(8,128)(2,1)}, bf16[96,1792]{1,0:T(8,128)(2,1)S(1)}, u32[]{:S(2)}, u32[]{:S(2)}) collective-permute-start(bf16[96,1792]{1,0:T(8,128)(2,1)} %copy-done.5), channel_id=1, source_target_pairs={{0,192},{32,224},{64,0},{96,32},{128,64},{160,96},{192,128},{224,1... | collective-permute-start | bytes 1032200 | tf_op jit(solution)/shard_map/ppermute | solution.py:442
  94.7 18.3 %collective-permute-start.12 = (bf16[96,1792]{1,0:T(8,128)(2,1)}, bf16[96,1792]{1,0:T(8,128)(2,1)S(1)}, u32[]{:S(2)}, u32[]{:S(2)}) collective-permute-start(bf16[96,1792]{1,0:T(8,128)(2,1)} %copy-done.4), channel_id=1, source_target_pairs={{0,64},{32,96},{64,128},{96,160},{128,192},{160,224},{192,0},{224,... | collective-permute-start | bytes 1032200 | tf_op jit(solution)/shard_map/ppermute | solution.py:442
  94.8 22.0 %collective-permute-start.11 = (bf16[96,1792]{1,0:T(8,128)(2,1)S(1)}, bf16[96,1792]{1,0:T(8,128)(2,1)S(1)}, u32[]{:S(2)}, u32[]{:S(2)}) collective-permute-start(bf16[96,1792]{1,0:T(8,128)(2,1)S(1)} %get-tuple-element.43), channel_id=1, source_target_pairs={{0,64},{32,96},{64,128},{96,160},{128,192},{160,224},{192,0},{224,... | collective-permute-start | bytes 1032200 | tf_op jit(solution)/shard_map/ppermute | solution.py:442
  102.1 16.3 %collective-permute-start.13 = (bf16[96,1792]{1,0:T(8,128)(2,1)S(1)}, bf16[96,1792]{1,0:T(8,128)(2,1)S(1)}, u32[]{:S(2)}, u32[]{:S(2)}) collective-permute-start(bf16[96,1792]{1,0:T(8,128)(2,1)S(1)} %get-tuple-element.46), channel_id=1, source_target_pairs={{0,192},{32,224},{64,0},{96,32},{128,64},{160,96},{192,128},{224,1... | collective-permute-start | bytes 1032200 | tf_op jit(solution)/shard_map/ppermute | solution.py:442
  103.6 25.1 %collective-permute-start.15 = (bf16[96,1792]{1,0:T(8,128)(2,1)S(1)}, bf16[96,1792]{1,0:T(8,128)(2,1)S(1)}, u32[]{:S(2)}, u32[]{:S(2)}) collective-permute-start(bf16[96,1792]{1,0:T(8,128)(2,1)S(1)} %get-tuple-element.48.refs_1_), channel_id=1, source_target_pairs={{0,64},{32,96},{64,128},{96,160},{128,192},{160,224},{192,0},{224,... | collective-permute-start | bytes 1032200 | tf_op jit(solution)/shard_map/ppermute | solution.py:442
  109.4 19.3 %collective-permute-start.16 = (bf16[96,1792]{1,0:T(8,128)(2,1)S(1)}, bf16[96,1792]{1,0:T(8,128)(2,1)}, u32[]{:S(2)}, u32[]{:S(2)}) collective-permute-start(bf16[96,1792]{1,0:T(8,128)(2,1)S(1)} %get-tuple-element.47.refs_0_), channel_id=1, source_target_pairs={{0,192},{32,224},{64,0},{96,32},{128,64},{160,96},{192,128},{224,1... | collective-permute-start | bytes 1032200 | tf_op jit(solution)/shard_map/ppermute | solution.py:442
  113.0 15.8 %collective-permute-start.18 = (bf16[96,1792]{1,0:T(8,128)(2,1)S(1)}, bf16[96,1792]{1,0:T(8,128)(2,1)}, u32[]{:S(2)}, u32[]{:S(2)}) collective-permute-start(bf16[96,1792]{1,0:T(8,128)(2,1)S(1)} %collective-permute-done.14.refs_2_), channel_id=1, source_target_pairs={{0,64},{32,96},{64,128},{96,160},{128,192},{160,224},{192,0},{224,... | collective-permute-start | bytes 1032200 | tf_op jit(solution)/shard_map/ppermute | solution.py:442
  116.8 11.9 %collective-permute-start.19 = (bf16[96,1792]{1,0:T(8,128)(2,1)S(1)}, bf16[96,1792]{1,0:T(8,128)(2,1)}, u32[]{:S(2)}, u32[]{:S(2)}) collective-permute-start(bf16[96,1792]{1,0:T(8,128)(2,1)S(1)} %collective-permute-done.17.refs_5_), channel_id=1, source_target_pairs={{0,192},{32,224},{64,0},{96,32},{128,64},{160,96},{192,128},{224,1... | collective-permute-start | bytes 1032200 | tf_op jit(solution)/shard_map/ppermute | solution.py:442
  118.3 85.6 %collective-permute-start.26 = (bf16[384,3584]{1,0:T(8,128)(2,1)}, bf16[384,3584]{1,0:T(8,128)(2,1)}, u32[]{:S(2)}, u32[]{:S(2)}) collective-permute-start(bf16[384,3584]{1,0:T(8,128)(2,1)} %get-tuple-element.61.t_a), channel_id=1, source_target_pairs={{0,32},{32,0},{64,96},{96,64},{128,160},{160,128},{192,224},{224,1... | collective-permute-start | bytes 8257544 | tf_op jit(solution)/shard_map/ppermute | solution.py:445
  119.9 52.0 %all-to-all-start.1 = ((bf16[32,8,1408]{2,1,0:T(8,128)(2,1)}), bf16[32,8,1408]{2,1,0:T(8,128)(2,1)S(1)}, u32[]{:S(2)}, u32[]{:S(2)}) async-start(bf16[32,8,1408]{2,1,0:T(8,128)(2,1)} %bitcast.6), calls=%async_computation.1 | async-start | bytes 1441792 | tf_op jit(solution)/shard_map/all_to_all | solution.py:449
  140.5 70.2 %collective-permute-start.28 = (bf16[384,3584]{1,0:T(8,128)(2,1)}, bf16[384,3584]{1,0:T(8,128)(2,1)}, u32[]{:S(2)}, u32[]{:S(2)}) collective-permute-start(bf16[384,3584]{1,0:T(8,128)(2,1)} %get-tuple-element.65.g_a), channel_id=1, source_target_pairs={{0,32},{32,0},{64,96},{96,64},{128,160},{160,128},{192,224},{224,1... | collective-permute-start | bytes 8257544 | tf_op jit(solution)/shard_map/ppermute | solution.py:445
  140.6 11.7 %collective-permute-start.21 = (bf16[96,1792]{1,0:T(8,128)(2,1)S(1)}, bf16[96,1792]{1,0:T(8,128)(2,1)S(1)}, u32[]{:S(2)}, u32[]{:S(2)}) collective-permute-start(bf16[96,1792]{1,0:T(8,128)(2,1)S(1)} %get-tuple-element.54), channel_id=1, source_target_pairs={{0,64},{32,96},{64,128},{96,160},{128,192},{160,224},{192,0},{224,... | collective-permute-start | bytes 1032200 | tf_op jit(solution)/shard_map/ppermute | solution.py:442
  141.2 11.2 %collective-permute-start.22 = (bf16[96,1792]{1,0:T(8,128)(2,1)S(1)}, bf16[96,1792]{1,0:T(8,128)(2,1)S(1)}, u32[]{:S(2)}, u32[]{:S(2)}) collective-permute-start(bf16[96,1792]{1,0:T(8,128)(2,1)S(1)} %get-tuple-element.56), channel_id=1, source_target_pairs={{0,192},{32,224},{64,0},{96,32},{128,64},{160,96},{192,128},{224,1... | collective-permute-start | bytes 1032200 | tf_op jit(solution)/shard_map/ppermute | solution.py:442
  143.9 15.0 %collective-permute-start.20 = (bf16[96,1792]{1,0:T(8,128)(2,1)S(1)}, bf16[96,1792]{1,0:T(8,128)(2,1)S(1)}, u32[]{:S(2)}, u32[]{:S(2)}) collective-permute-start(bf16[96,1792]{1,0:T(8,128)(2,1)S(1)} %get-tuple-element.52), channel_id=1, source_target_pairs={{0,192},{32,224},{64,0},{96,32},{128,64},{160,96},{192,128},{224,1... | collective-permute-start | bytes 1032200 | tf_op jit(solution)/shard_map/ppermute | solution.py:442
  152.3 12.1 %collective-permute-start.24 = (bf16[96,1792]{1,0:T(8,128)(2,1)S(1)}, bf16[96,1792]{1,0:T(8,128)(2,1)S(1)}, u32[]{:S(2)}, u32[]{:S(2)}) collective-permute-start(bf16[96,1792]{1,0:T(8,128)(2,1)S(1)} %get-tuple-element.59), channel_id=1, source_target_pairs={{0,64},{32,96},{64,128},{96,160},{128,192},{160,224},{192,0},{224,... | collective-permute-start | bytes 1032200 | tf_op jit(solution)/shard_map/ppermute | solution.py:442
  152.5 17.9 %collective-permute-start.23 = (bf16[96,1792]{1,0:T(8,128)(2,1)S(1)}, bf16[96,1792]{1,0:T(8,128)(2,1)S(1)}, u32[]{:S(2)}, u32[]{:S(2)}) collective-permute-start(bf16[96,1792]{1,0:T(8,128)(2,1)S(1)} %get-tuple-element.57), channel_id=1, source_target_pairs={{0,64},{32,96},{64,128},{96,160},{128,192},{160,224},{192,0},{224,... | collective-permute-start | bytes 1032200 | tf_op jit(solution)/shard_map/ppermute | solution.py:442
  158.9 11.5 %collective-permute-start.25 = (bf16[96,1792]{1,0:T(8,128)(2,1)S(1)}, bf16[96,1792]{1,0:T(8,128)(2,1)S(1)}, u32[]{:S(2)}, u32[]{:S(2)}) collective-permute-start(bf16[96,1792]{1,0:T(8,128)(2,1)S(1)} %get-tuple-element.60), channel_id=1, source_target_pairs={{0,192},{32,224},{64,0},{96,32},{128,64},{160,96},{192,128},{224,1... | collective-permute-start | bytes 1032200 | tf_op jit(solution)/shard_map/ppermute | solution.py:442
  171.9 30.7 %all-to-all-start.3 = ((bf16[32,8,1408]{2,1,0:T(8,128)(2,1)}), bf16[32,8,1408]{2,1,0:T(8,128)(2,1)S(1)}, u32[]{:S(2)}, u32[]{:S(2)}) async-start(bf16[32,8,1408]{2,1,0:T(8,128)(2,1)} %bitcast.10), calls=%async_computation.3 | async-start | bytes 1441792 | tf_op jit(solution)/shard_map/all_to_all | solution.py:449
  181.7 22.3 %collective-permute-start.27 = (bf16[768,384]{1,0:T(8,128)(2,1)S(1)}, bf16[768,384]{1,0:T(8,128)(2,1)S(1)}, u32[]{:S(2)}, u32[]{:S(2)}) collective-permute-start(bf16[768,384]{1,0:T(8,128)(2,1)S(1)} %get-tuple-element.63), channel_id=1, source_target_pairs={{0,32},{32,0},{64,96},{96,64},{128,160},{160,128},{192,224},{224,1... | collective-permute-start | bytes 1769480 | tf_op jit(solution)/shard_map/ppermute | solution.py:445
  (14 other events, 98.4 us)
